TPU v7x, 32 devices: a whole 2x2x4 slice. The times are simulated.
32 devices in a mesh: ctx: 8 (over z, core), wsh: 4 (over y, x).
Axes of the slice: x: 2, y: 2, z: 4, core: 2. Of those that a mesh axis runs over, the one named last changes fastest.
Arguments:
- hidden: bfloat16 [4, 1024, 2048], P('wsh', 'ctx'), may hold values from -6 to 6
- cotangent: bfloat16 [4, 1024, 2048], P('wsh', 'ctx'), may hold values from -6 to 6
- doc_ids: int32 [4, 1024], replicated, may hold values from 0 to 3, never falling along the last dimension, each value on 1 to 512 neighbouring positions
- w_qkv: float32 [2048, 3, 2048], P('ctx', None, 'wsh'), may hold values from -4 to 4
- w_out: float32 [2048, 2048], P('wsh', 'ctx'), may hold values from -2 to 2
- w_gu: float32 [2048, 2, 5632], P('ctx', None, 'wsh'), may hold values from -0.125 to 0.125
- w_down: float32 [5632, 2048], P('wsh', 'ctx'), may hold values from -0.078125 to 0.078125
- norm_vecs: float32 [2048, 6], P('ctx'), may hold values from -2 to 2
- first_qkv: float32 [2048, 3, 2048], P('ctx', None, 'wsh'), may hold values from -192 to 192
- first_out: float32 [2048, 2048], P('wsh', 'ctx'), may hold values from -6 to 6
- first_gu: float32 [2048, 2, 5632], P('ctx', None, 'wsh'), may hold values from -40 to 40
- first_down: float32 [5632, 2048], P('wsh', 'ctx'), may hold values from -64 to 64
- first_vecs: float32 [2048, 6], P('ctx'), may hold values from -128 to 128
- second_qkv: float32 [2048, 3, 2048], P('ctx', None, 'wsh'), may hold values from 10 to 100000
- second_out: float32 [2048, 2048], P('wsh', 'ctx'), may hold values from 1 to 100
- second_gu: float32 [2048, 2, 5632], P('ctx', None, 'wsh'), may hold values from 20 to 2000
- second_down: float32 [5632, 2048], P('wsh', 'ctx'), may hold values from 60 to 6000
- second_vecs: float32 [2048, 6], P('ctx'), may hold values from 10 to 10000
Outputs:
- block_out: bfloat16 [4, 1024, 2048], P('wsh', 'ctx')
- grad_hidden: float32 [4, 1024, 2048], P('wsh', 'ctx')
- grad_qkv: float32 [2048, 3, 2048], P('ctx', None, 'wsh')
- grad_out: float32 [2048, 2048], P('wsh', 'ctx')
- grad_gu: float32 [2048, 2, 5632], P('ctx', None, 'wsh')
- grad_down: float32 [5632, 2048], P('wsh', 'ctx')
- grad_vecs: float32 [2048, 6], P('ctx')
- new_qkv: float32 [2048, 3, 2048], P('ctx', None, 'wsh')
- new_out: float32 [2048, 2048], P('wsh', 'ctx')
- new_gu: float32 [2048, 2, 5632], P('ctx', None, 'wsh')
- new_down: float32 [5632, 2048], P('wsh', 'ctx')
- new_vecs: float32 [2048, 6], P('ctx')
- new_first_qkv: float32 [2048, 3, 2048], P('ctx', None, 'wsh')
- new_first_out: float32 [2048, 2048], P('wsh', 'ctx')
- new_first_gu: float32 [2048, 2, 5632], P('ctx', None, 'wsh')
- new_first_down: float32 [5632, 2048], P('wsh', 'ctx')
- new_first_vecs: float32 [2048, 6], P('ctx')
- new_second_qkv: float32 [2048, 3, 2048], P('ctx', None, 'wsh')
- new_second_out: float32 [2048, 2048], P('wsh', 'ctx')
- new_second_gu: float32 [2048, 2, 5632], P('ctx', None, 'wsh')
- new_second_down: float32 [5632, 2048], P('wsh', 'ctx')
- new_second_vecs: float32 [2048, 6], P('ctx')
Inputs may be any that keep to these rules, and one draw needn't show every extreme that they name: `doc_ids`: within each sequence the ids never fall, each of the 4 documents holds 1 to 512 positions, and one holds exactly 512.
All inputs are finite; a program needn't handle non-finite values.
Results may differ from a plain program's by a relative error of at most 0.024.
Values may be sent and summed in bfloat16 or wider, within the bound.
No kernel may reach another device: no remote copies, remote signals or barrier semaphores. Data moves between devices by JAX's collectives and lax.ppermute only.
A program may use at most 256 MiB of HBM per device.

v0:
```python
import jax
import jax.numpy as jnp
from jax import lax
from jax.sharding import PartitionSpec as P

D = 2048
HD = 64
ROT = 16
STEP = 4


learn_rate = 0.005
beta_first = 0.9
beta_second = 0.95
adam_epsilon = 1e-08
weight_decay = 0.1
norm_epsilon = 1e-05
masked_score = -1e30


def shifted(value, axis, steps):
    count = lax.axis_size(axis)
    pairs = [(source, (source + steps) % count) for source in range(count)]
    return lax.ppermute(value, axis, pairs)


def layer_norm(matrix, gain_vec, shift_vec):
    centre = matrix - jnp.mean(matrix, axis=-1, keepdims=True)
    inverse = lax.rsqrt(jnp.mean(centre * centre, axis=-1, keepdims=True) + norm_epsilon)
    normed = centre * inverse
    return (normed * gain_vec + shift_vec, normed, inverse)


def norm_back(incoming, normed, inverse, gain_vec):
    scaled = incoming * gain_vec
    inner = (
        scaled
        - jnp.mean(scaled, axis=-1, keepdims=True)
        - normed * jnp.mean(scaled * normed, axis=-1, keepdims=True)
    )
    return (inner * inverse, jnp.sum(incoming * normed, axis=0), jnp.sum(incoming, axis=0))


def rotary_tables(positions):
    half_rot = ROT // 2
    frequency = 10000.0 ** (-2.0 * jnp.arange(half_rot, dtype=jnp.float32) / ROT)
    angles = positions.astype(jnp.float32)[:, None] * frequency[None, :]
    return (jnp.cos(angles), jnp.sin(angles))


def rotate(matrix, cos_table, sin_table, direction):
    per_head = matrix.reshape(matrix.shape[0], matrix.shape[1] // HD, HD)
    half_rot = ROT // 2
    low_part = per_head[:, :, :half_rot]
    high_part = per_head[:, :, half_rot:ROT]
    cos_part = cos_table[:, None, :]
    sin_part = sin_table[:, None, :] * direction
    turned = jnp.concatenate(
        [
            low_part * cos_part - high_part * sin_part,
            high_part * cos_part + low_part * sin_part,
            per_head[:, :, ROT:],
        ],
        axis=-1,
    )
    return turned.reshape(matrix.shape)


def dot_rows(left_side, right_side):
    return lax.dot_general(
        left_side, right_side, (((0,), (0,)), ((), ())), preferred_element_type=jnp.float32
    )


def dot_back(left_side, right_side):
    return lax.dot_general(
        left_side, right_side, (((1,), (1,)), ((), ())), preferred_element_type=jnp.float32
    )


def adam_step(master, gradient, first_moment, second_moment, decay_rate):
    moment_one = beta_first * first_moment + (1.0 - beta_first) * gradient
    moment_two = beta_second * second_moment + (1.0 - beta_second) * gradient * gradient
    corrected = moment_one / (1.0 - beta_first**STEP)
    spread = jnp.sqrt(moment_two / (1.0 - beta_second**STEP))
    updated = master - learn_rate * (corrected / (spread + adam_epsilon) + decay_rate * master)
    return (updated, moment_one, moment_two)


def local(
    hidden,
    cotangent,
    doc_ids,
    w_qkv,
    w_out,
    w_gu,
    w_down,
    norm_vecs,
    first_qkv,
    first_out,
    first_gu,
    first_down,
    first_vecs,
    second_qkv,
    second_out,
    second_gu,
    second_down,
    second_vecs,
):
    ctx_size = lax.axis_size("ctx")
    ctx_place = lax.axis_index("ctx")
    shard_count = lax.axis_size("wsh")
    shard_place = lax.axis_index("wsh")
    tok_rows = hidden.shape[1]
    all_rows = shard_count * tok_rows
    head_cols = w_qkv.shape[2]
    heads_here = head_cols // HD
    unit_cols = w_gu.shape[2]
    score_scale = HD ** (-0.5)
    qkv_weight, out_weight, gu_weight, down_weight, vec_weight = (
        lax.all_gather(w_qkv.astype(jnp.bfloat16), "ctx", axis=0, tiled=True),
        lax.all_gather(w_out.astype(jnp.bfloat16), "ctx", axis=1, tiled=True),
        lax.all_gather(w_gu.astype(jnp.bfloat16), "ctx", axis=0, tiled=True),
        lax.all_gather(w_down.astype(jnp.bfloat16), "ctx", axis=1, tiled=True),
        lax.all_gather(norm_vecs.astype(jnp.bfloat16), "ctx", axis=0, tiled=True),
    )
    qkv_flat = qkv_weight.reshape(D, 3 * head_cols)
    gu_flat = gu_weight.reshape(D, 2 * unit_cols)
    vectors = vec_weight.astype(jnp.float32)
    gain_one, shift_one, gain_two, shift_two = [vectors[:, column] for column in range(4)]
    col_start = shard_place * head_cols
    bias_query = lax.dynamic_slice_in_dim(vectors[:, 4], col_start, head_cols, 0)
    bias_value = lax.dynamic_slice_in_dim(vectors[:, 5], col_start, head_cols, 0)
    positions = ctx_place * tok_rows + jnp.arange(tok_rows, dtype=jnp.int32)
    last_position = ctx_place * tok_rows + tok_rows - 1
    cos_table, sin_table = rotary_tables(positions)
    cos_all = jnp.tile(cos_table, (shard_count, 1))
    sin_all = jnp.tile(sin_table, (shard_count, 1))
    own_ids = lax.dynamic_slice_in_dim(doc_ids, ctx_place * tok_rows, tok_rows, 1)

    def visible(key_start, key_count):
        key_pos = key_start + jnp.arange(key_count, dtype=jnp.int32)
        key_ids = lax.dynamic_slice_in_dim(doc_ids, key_start, key_count, 1)
        return (
            (key_pos[None, None, :] <= positions[None, :, None])
            & (key_ids[:, None, :] == own_ids[:, :, None])
        )[:, None]

    hidden_f32 = hidden[0].astype(jnp.float32)
    normed_one, hat_one, inverse_one = layer_norm(hidden_f32, gain_one, shift_one)
    normed_one = normed_one.astype(jnp.bfloat16)
    gathered_one, cot_all = (
        lax.all_gather(normed_one, "wsh", axis=0, tiled=True),
        lax.all_gather(cotangent[0], "wsh", axis=0, tiled=True),
    )
    projected = jnp.dot(gathered_one, qkv_flat, preferred_element_type=jnp.float32)
    queries = rotate(projected[:, :head_cols] + bias_query, cos_all, sin_all, 1.0).astype(
        jnp.bfloat16
    )
    key_rows = rotate(projected[:, head_cols : 2 * head_cols], cos_all, sin_all, 1.0).astype(
        jnp.bfloat16
    )
    values = (projected[:, 2 * head_cols :] + bias_value).astype(jnp.bfloat16)
    query_heads = queries.reshape(shard_count, tok_rows, heads_here, HD)
    key_three = key_rows.reshape(shard_count, tok_rows, head_cols)
    value_three = values.reshape(shard_count, tok_rows, head_cols)
    start_state = (
        jnp.zeros((shard_count, heads_here, tok_rows, HD), jnp.float32),
        jnp.full((shard_count, heads_here, tok_rows), masked_score, jnp.float32),
        jnp.zeros((shard_count, heads_here, tok_rows), jnp.float32),
    )
    running = start_state
    key_shard = lax.all_gather(key_three, "ctx", axis=1, tiled=True)
    value_shard = lax.all_gather(value_three, "ctx", axis=1, tiled=True)
    key_count = key_shard.shape[1]
    block_rows = 512
    block_count = key_count // block_rows
    key_blocks = key_shard.reshape(shard_count, block_count, block_rows, heads_here, HD).transpose(
        1, 0, 2, 3, 4
    )
    value_blocks = value_shard.reshape(
        shard_count, block_count, block_rows, heads_here, HD
    ).transpose(1, 0, 2, 3, 4)
    block_starts = block_rows * jnp.arange(block_count, dtype=jnp.int32)

    def visit(partial_state, block_items):
        key_block, value_block, block_start = block_items

        def attend(inner_state):
            output_sum, row_top, weight_sum = inner_state
            allowed = visible(block_start, block_rows)
            scores = (
                jnp.einsum(
                    "sqhd,skhd->shqk", query_heads, key_block, preferred_element_type=jnp.float32
                )
                * score_scale
            )
            new_top = jnp.maximum(
                row_top, jnp.max(jnp.where(allowed, scores, masked_score), axis=-1)
            )
            rescale = jnp.exp(row_top - new_top)
            weights = jnp.where(allowed, jnp.exp(scores - new_top[..., None]), 0.0)
            weight_sum = weight_sum * rescale + jnp.sum(weights, axis=-1)
            output_sum = output_sum * rescale[..., None] + jnp.einsum(
                "shqk,skhd->shqd",
                weights.astype(jnp.bfloat16),
                value_block,
                preferred_element_type=jnp.float32,
            )
            return (output_sum, new_top, weight_sum)

        return (
            lax.cond(
                block_start <= last_position, attend, lambda inner_state: inner_state, partial_state
            ),
            None,
        )

    running, _ = lax.scan(visit, running, (key_blocks, value_blocks, block_starts))
    output_sum, row_top, weight_sum = running
    attended = (
        (output_sum / weight_sum[..., None])
        .transpose(0, 2, 1, 3)
        .reshape(all_rows, head_cols)
        .astype(jnp.bfloat16)
    )
    log_sums = row_top + jnp.log(weight_sum)
    attn_terms = jnp.dot(attended, out_weight, preferred_element_type=jnp.float32)
    middle = hidden_f32 + lax.psum_scatter(
        attn_terms.astype(jnp.bfloat16), "wsh", scatter_dimension=0, tiled=True
    ).astype(jnp.float32)
    normed_two, hat_two, inverse_two = layer_norm(middle, gain_two, shift_two)
    normed_two = normed_two.astype(jnp.bfloat16)
    gathered_two = lax.all_gather(normed_two, "wsh", axis=0, tiled=True)
    gate_up = jnp.dot(gathered_two, gu_flat, preferred_element_type=jnp.float32)
    gate_part = gate_up[:, :unit_cols]
    up_part = gate_up[:, unit_cols:]
    sigmoid_gate = jax.nn.sigmoid(gate_part)
    activated = (gate_part * sigmoid_gate * up_part).astype(jnp.bfloat16)
    ffn_terms = jnp.dot(activated, down_weight, preferred_element_type=jnp.float32)
    block_out = (
        middle
        + lax.psum_scatter(
            ffn_terms.astype(jnp.bfloat16), "wsh", scatter_dimension=0, tiled=True
        ).astype(jnp.float32)
    ).astype(jnp.bfloat16)
    cot_rows = cotangent[0]
    grad_act = dot_back(cot_all, down_weight)
    grad_down = dot_rows(activated, cot_all)
    grad_gate = grad_act * up_part * sigmoid_gate * (1.0 + gate_part * (1.0 - sigmoid_gate))
    grad_up = grad_act * gate_part * sigmoid_gate
    grad_gate_up = jnp.concatenate([grad_gate, grad_up], axis=1).astype(jnp.bfloat16)
    grad_gu = dot_rows(gathered_two, grad_gate_up).reshape(D, 2, unit_cols)
    grad_normed_two = lax.psum_scatter(
        dot_back(grad_gate_up, gu_flat).astype(jnp.bfloat16), "wsh", scatter_dimension=0, tiled=True
    ).astype(jnp.float32)
    grad_middle, grad_gain_two, grad_shift_two = norm_back(
        grad_normed_two, hat_two, inverse_two, gain_two
    )
    grad_middle = grad_middle + cot_rows.astype(jnp.float32)
    middle_bf16 = grad_middle.astype(jnp.bfloat16)
    middle_all = lax.all_gather(middle_bf16, "wsh", axis=0, tiled=True)
    grad_out = dot_rows(attended, middle_all)
    grad_att = dot_back(middle_all, out_weight).astype(jnp.bfloat16)
    grad_heads = grad_att.reshape(shard_count, tok_rows, heads_here, HD)
    deltas = jnp.sum(
        grad_heads.astype(jnp.float32)
        * attended.astype(jnp.float32).reshape(shard_count, tok_rows, heads_here, HD),
        axis=-1,
    ).transpose(0, 2, 1)

    def pass_step(turn, pass_state):
        key_now, value_now, grad_keys, grad_values, grad_query = pass_state
        source = (ctx_place - turn) % ctx_size

        def contribute(grad_parts):
            part_keys, part_values, part_query = grad_parts
            key_heads = key_now.reshape(shard_count, tok_rows, heads_here, HD)
            value_heads = value_now.reshape(shard_count, tok_rows, heads_here, HD)
            allowed = visible(source * tok_rows, tok_rows)
            scores = (
                jnp.einsum(
                    "sqhd,skhd->shqk", query_heads, key_heads, preferred_element_type=jnp.float32
                )
                * score_scale
            )
            probability = jnp.where(allowed, jnp.exp(scores - log_sums[..., None]), 0.0)
            part_values = part_values + jnp.einsum(
                "shqk,sqhd->skhd",
                probability.astype(jnp.bfloat16),
                grad_heads,
                preferred_element_type=jnp.float32,
            ).reshape(shard_count, tok_rows, head_cols)
            grad_prob = jnp.einsum(
                "sqhd,skhd->shqk", grad_heads, value_heads, preferred_element_type=jnp.float32
            )
            grad_score = (probability * (grad_prob - deltas[..., None]) * score_scale).astype(
                jnp.bfloat16
            )
            part_query = part_query + jnp.einsum(
                "shqk,skhd->sqhd", grad_score, key_heads, preferred_element_type=jnp.float32
            )
            part_keys = part_keys + jnp.einsum(
                "shqk,sqhd->skhd", grad_score, query_heads, preferred_element_type=jnp.float32
            ).reshape(shard_count, tok_rows, head_cols)
            return (part_keys, part_values, part_query)

        grad_keys, grad_values, grad_query = lax.cond(
            source <= ctx_place,
            contribute,
            lambda grad_parts: grad_parts,
            (grad_keys, grad_values, grad_query),
        )
        key_wide, value_wide, grad_keys, grad_values = (
            shifted(key_now.astype(jnp.float32).astype(jnp.bfloat16), "ctx", 1).astype(jnp.float32),
            shifted(value_now.astype(jnp.float32).astype(jnp.bfloat16), "ctx", 1).astype(
                jnp.float32
            ),
            shifted(grad_keys.astype(jnp.bfloat16), "ctx", 1).astype(grad_keys.dtype),
            shifted(grad_values.astype(jnp.bfloat16), "ctx", 1).astype(grad_values.dtype),
        )
        key_now = key_wide.astype(jnp.bfloat16)
        value_now = value_wide.astype(jnp.bfloat16)
        return (key_now, value_now, grad_keys, grad_values, grad_query)

    zero_rows = jnp.zeros((shard_count, tok_rows, head_cols), jnp.float32)
    pass_start = (
        key_three,
        value_three,
        zero_rows,
        zero_rows,
        jnp.zeros((shard_count, tok_rows, heads_here, HD), jnp.float32),
    )
    _, _, grad_keys, grad_values, grad_query = lax.fori_loop(0, ctx_size, pass_step, pass_start)
    grad_query = rotate(grad_query.reshape(all_rows, head_cols), cos_all, sin_all, -1.0)
    grad_keys = rotate(grad_keys.reshape(all_rows, head_cols), cos_all, sin_all, -1.0)
    grad_values = grad_values.reshape(all_rows, head_cols)
    grad_rows = jnp.concatenate([grad_query, grad_keys, grad_values], axis=1).astype(jnp.bfloat16)
    grad_qkv = dot_rows(gathered_one, grad_rows).reshape(D, 3, head_cols)
    grad_normed_one = lax.psum_scatter(
        dot_back(grad_rows, qkv_flat).astype(jnp.bfloat16), "wsh", scatter_dimension=0, tiled=True
    ).astype(jnp.float32)
    grad_input, grad_gain_one, grad_shift_one = norm_back(
        grad_normed_one, hat_one, inverse_one, gain_one
    )
    grad_input = grad_input + grad_middle
    zero_width = jnp.zeros((D,), jnp.float32)
    bias_query_grad = lax.dynamic_update_slice_in_dim(
        zero_width, jnp.sum(grad_query, axis=0), col_start, 0
    )
    bias_value_grad = lax.dynamic_update_slice_in_dim(
        zero_width, jnp.sum(grad_values, axis=0), col_start, 0
    )
    vec_terms = jnp.stack(
        [
            grad_gain_one,
            grad_shift_one,
            grad_gain_two,
            grad_shift_two,
            bias_query_grad,
            bias_value_grad,
        ],
        axis=1,
    )
    share_qkv, share_out, share_gu, share_down, vec_block = (
        lax.psum_scatter(
            grad_qkv.astype(jnp.bfloat16), "ctx", scatter_dimension=0, tiled=True
        ).astype(jnp.float32),
        lax.psum_scatter(
            grad_out.astype(jnp.bfloat16), "ctx", scatter_dimension=1, tiled=True
        ).astype(jnp.float32),
        lax.psum_scatter(
            grad_gu.astype(jnp.bfloat16), "ctx", scatter_dimension=0, tiled=True
        ).astype(jnp.float32),
        lax.psum_scatter(
            grad_down.astype(jnp.bfloat16), "ctx", scatter_dimension=1, tiled=True
        ).astype(jnp.float32),
        lax.psum_scatter(
            vec_terms.astype(jnp.bfloat16), "ctx", scatter_dimension=0, tiled=True
        ).astype(jnp.float32),
    )
    share_vecs = lax.psum(vec_block, "wsh")
    new_qkv, new_first_qkv, new_second_qkv = adam_step(
        w_qkv, share_qkv, first_qkv, second_qkv, weight_decay
    )
    new_out, new_first_out, new_second_out = adam_step(
        w_out, share_out, first_out, second_out, weight_decay
    )
    new_gu, new_first_gu, new_second_gu = adam_step(
        w_gu, share_gu, first_gu, second_gu, weight_decay
    )
    new_down, new_first_down, new_second_down = adam_step(
        w_down, share_down, first_down, second_down, weight_decay
    )
    new_vecs, new_first_vecs, new_second_vecs = adam_step(
        norm_vecs, share_vecs, first_vecs, second_vecs, 0.0
    )
    return (
        block_out[None],
        grad_input[None],
        share_qkv,
        share_out,
        share_gu,
        share_down,
        share_vecs,
        new_qkv,
        new_out,
        new_gu,
        new_down,
        new_vecs,
        new_first_qkv,
        new_first_out,
        new_first_gu,
        new_first_down,
        new_first_vecs,
        new_second_qkv,
        new_second_out,
        new_second_gu,
        new_second_down,
        new_second_vecs,
    )


def solution(mesh):
    return jax.shard_map(
        local,
        mesh=mesh,
        in_specs=(
            P("wsh", "ctx", None),
            P("wsh", "ctx", None),
            P(),
            P("ctx", None, "wsh"),
            P("wsh", "ctx"),
            P("ctx", None, "wsh"),
            P("wsh", "ctx"),
            P("ctx", None),
            P("ctx", None, "wsh"),
            P("wsh", "ctx"),
            P("ctx", None, "wsh"),
            P("wsh", "ctx"),
            P("ctx", None),
            P("ctx", None, "wsh"),
            P("wsh", "ctx"),
            P("ctx", None, "wsh"),
            P("wsh", "ctx"),
            P("ctx", None),
        ),
        out_specs=(
            P("wsh", "ctx", None),
            P("wsh", "ctx", None),
            P("ctx", None, "wsh"),
            P("wsh", "ctx"),
            P("ctx", None, "wsh"),
            P("wsh", "ctx"),
            P("ctx", None),
            P("ctx", None, "wsh"),
            P("wsh", "ctx"),
            P("ctx", None, "wsh"),
            P("wsh", "ctx"),
            P("ctx", None),
            P("ctx", None, "wsh"),
            P("wsh", "ctx"),
            P("ctx", None, "wsh"),
            P("wsh", "ctx"),
            P("ctx", None),
            P("ctx", None, "wsh"),
            P("wsh", "ctx"),
            P("ctx", None, "wsh"),
            P("wsh", "ctx"),
            P("ctx", None),
        ),
        check_vma=False,
    )
```

profile of v0, /device:TPU:0, one launch (start us, length us, event | category | flops | bytes accessed | tf_op | source)
XLA Modules:
  0.0 1494.8 jit_solution(11580008069787179538)
XLA Ops:
  8.1 15.8 %all_gather.33 = bf16[2048,6]{0,1:T(8,128)(2,1)S(1)} all-gather(bf16[256,6]{0,1:T(8,128)(2,1)S(1)} %convert_element_type.234), channel_id=1, replica_groups=mesh['ctx'=8,'wsh'=4] {'ctx'}, dimensions={0}, use_global_device_ids=true | all-gather | bytes 27648 | tf_op jit(solution)/shard_map/all_gather | solution.py:125
  30.2 34.9 %all-gather.12.cloned.1.call-done = bf16[512,2048]{1,0:T(8,128)(2,1)} async-done(((bf16[128,2048]{1,0:T(8,128)(2,1)}), bf16[512,2048]{1,0:T(8,128)(2,1)}) %all-gather.12.cloned.1.call-update) | async-done | bytes 2097168 | tf_op jit(solution)/shard_map/all_gather | solution.py:153
  65.0 67.3 %all-gather.14.cloned.1.call-done = bf16[2048,3,512]{0,2,1:T(8,128)(2,1)} async-done(((bf16[256,3,512]{0,2,1:T(8,128)(2,1)}), bf16[2048,3,512]{0,2,1:T(8,128)(2,1)}) %all-gather.14.cloned.1.call-update) | async-done | bytes 6291472 | tf_op jit(solution)/shard_map/all_gather | solution.py:121
  144.0 43.8 %all-gather.16.cloned.1.call-done = bf16[4,1024,512]{1,0,2:T(4,128)(2,1)} async-done(((bf16[4,128,512]{1,0,2:T(4,128)(2,1)}), bf16[4,1024,512]{1,0,2:T(4,128)(2,1)}) %all-gather.16.cloned.1.call-update) | async-done | bytes 4194320 | tf_op jit(solution)/shard_map/all_gather | solution.py:173
  200.9 34.9 %all-gather.18.cloned.1.call-done = bf16[4,1024,512]{1,2,0:T(8,128)(2,1)} async-done(((bf16[4,128,512]{1,2,0:T(8,128)(2,1)}), bf16[4,1024,512]{1,2,0:T(8,128)(2,1)}) %all-gather.18.cloned.1.call-update) | async-done | bytes 4194320 | tf_op jit(solution)/shard_map/all_gather | solution.py:174
  249.0 13.8 while.39
  250.3 11.3 conditional.6
  273.8 39.7 %reduce-scatter.9.cloned.1.call-done = bf16[128,2048]{1,0:T(8,128)(2,1)} async-done(((bf16[512,2048]{1,0:T(8,128)(2,1)}), bf16[128,2048]{1,0:T(8,128)(2,1)}) %reduce-scatter.9.cloned.1.call-update) | async-done | bytes 524304 | tf_op jit(solution)/shard_map/reduce_scatter | solution.py:229
  319.3 104.5 %all-gather.24.cloned.1.call-done = bf16[2048,2,1408]{2,1,0:T(2,128)(2,1)} async-done(((bf16[256,2,1408]{2,1,0:T(2,128)(2,1)}), bf16[2048,2,1408]{2,1,0:T(2,128)(2,1)}) %all-gather.24.cloned.1.call-update) | async-done | bytes 11534352 | tf_op jit(solution)/shard_map/all_gather | solution.py:123
  423.8 11.3 copy.91
  435.2 24.5 %all-gather.22.cloned.1.call-done = bf16[512,2048]{1,0:T(8,128)(2,1)} async-done(((bf16[128,2048]{1,0:T(8,128)(2,1)}), bf16[512,2048]{1,0:T(8,128)(2,1)}) %all-gather.22.cloned.1.call-update) | async-done | bytes 2097168 | tf_op jit(solution)/shard_map/all_gather | solution.py:234
  459.7 12.5 fusion.89
  472.2 24.5 %all-gather.30.cloned.1.call-done = bf16[1,512,2048]{2,1,0:T(8,128)(2,1)} async-done(((bf16[1,128,2048]{2,1,0:T(8,128)(2,1)}), bf16[1,512,2048]{2,1,0:T(8,128)(2,1)}) %all-gather.30.cloned.1.call-update) | async-done | bytes 2097168 | tf_op jit(solution)/shard_map/all_gather | solution.py:154
  496.8 62.9 %all-gather.26.cloned.1.call-done = bf16[1408,2048]{1,0:T(8,128)(2,1)} async-done(((bf16[1408,256]{1,0:T(8,128)(2,1)}), bf16[1408,2048]{1,0:T(8,128)(2,1)}) %all-gather.26.cloned.1.call-update) | async-done | bytes 5767184 | tf_op jit(solution)/shard_map/all_gather | solution.py:124
  559.6 10.4 multiply_convert_fusion.2
  571.6 10.0 convolution_convert_fusion.5
  581.8 33.3 %reduce-scatter.13.cloned.1.call-done = bf16[128,2048]{1,0:T(8,128)(2,1)} async-done(((bf16[512,2048]{1,0:T(8,128)(2,1)}), bf16[128,2048]{1,0:T(8,128)(2,1)}) %reduce-scatter.13.cloned.1.call-update) | async-done | bytes 524304 | tf_op jit(solution)/shard_map/reduce_scatter | solution.py:254
  620.6 34.6 %all-gather.28.cloned.1.call-done = bf16[512,2048]{1,0:T(8,128)(2,1)} async-done(((bf16[128,2048]{1,0:T(8,128)(2,1)}), bf16[512,2048]{1,0:T(8,128)(2,1)}) %all-gather.28.cloned.1.call-update) | async-done | bytes 2097168 | tf_op jit(solution)/shard_map/all_gather | solution.py:262
  661.9 282.6 %while.40 = (s32[]{:T(128)}, bf16[4,128,512]{1,2,0:T(8,128)(2,1)S(1)}, bf16[4,128,512]{1,2,0:T(8,128)(2,1)S(1)}, f32[4,128,512]{1,2,0:T(8,128)}, f32[4,128,512]{...) while((s32[]{:T(128)}, ...), condition=%wide.region_19.20_spmd.clone, body=%wide.region_16.19_spmd.clone.sunk | while | flops 342245632 | bytes 55258892 | solution.py:334
  738.0 10.5 collective-permute-start.3
  814.2 10.6 collective-permute-start.1
  960.0 11.1 convolution_convert_fusion
  971.1 22.6 %convert_element_type.270 = bf16[2048,2,1408]{2,1,0:T(2,128)(2,1)} reshape(bf16[2048,2816]{1,0:T(8,128)(2,1)} %convolution_convert_fusion) | data formatting | bytes 23068672 | tf_op jit(solution)/shard_map/convert_element_type | solution.py:373
  1028.1 8.7 copy.86
  1038.7 200.1 %all-reduce.3.cloned.1.call-done = bf16[2048,2,1408]{2,1,0:T(2,128)(2,1)} async-done(((bf16[2048,2,1408]{2,1,0:T(2,128)(2,1)}), bf16[2048,2,1408]{2,1,0:T(2,128)(2,1)}) %all-reduce.3.cloned.1.call-update) | async-done | bytes 11534352
  1238.7 13.6 multiply_subtract_fusion
  1253.3 23.7 %reduce-scatter.19.cloned.1.call-done = bf16[512,256]{1,0:T(8,128)(2,1)} async-done(((bf16[512,2048]{1,0:T(8,128)(2,1)}), bf16[512,256]{1,0:T(8,128)(2,1)}) %reduce-scatter.19.cloned.1.call-update) | async-done | bytes 262160 | tf_op jit(solution)/shard_map/reduce_scatter | solution.py:369
  1279.5 34.2 %reduce-scatter.11.cloned.1.call-done = bf16[128,2048]{1,0:T(8,128)(2,1)} async-done(((bf16[512,2048]{1,0:T(8,128)(2,1)}), bf16[128,2048]{1,0:T(8,128)(2,1)}) %reduce-scatter.11.cloned.1.call-update) | async-done | bytes 524304 | tf_op jit(solution)/shard_map/reduce_scatter | solution.py:243
  1317.3 63.4 %reduce-scatter.21.cloned.1.call-done = bf16[1408,256]{1,0:T(8,128)(2,1)} async-done(((bf16[1408,2048]{1,0:T(8,128)(2,1)}), bf16[1408,256]{1,0:T(8,128)(2,1)}) %reduce-scatter.21.cloned.1.call-update) | async-done | bytes 720912 | tf_op jit(solution)/shard_map/reduce_scatter | solution.py:375
  1385.5 26.8 %reduce-scatter.23.cloned.1.call-done = bf16[256,6]{0,1:T(8,128)(2,1)} async-done(((bf16[2048,6]{0,1:T(8,128)(2,1)}), bf16[256,6]{0,1:T(8,128)(2,1)}) %reduce-scatter.23.cloned.1.call-update) | async-done | bytes 3088 | tf_op jit(solution)/shard_map/reduce_scatter | solution.py:378
  1412.3 10.1 psum.7
  1423.1 59.4 %reduce-scatter.17.cloned.1.call-done = bf16[256,3,512]{2,0,1:T(8,128)(2,1)} async-done(((bf16[2048,3,512]{2,0,1:T(8,128)(2,1)}), bf16[256,3,512]{2,0,1:T(8,128)(2,1)}) %reduce-scatter.17.cloned.1.call-update) | async-done | bytes 786448 | tf_op jit(solution)/shard_map/reduce_scatter | solution.py:366
  (411 shorter events, 423.8 us)
Async XLA Ops:
  7.2 57.8 %all-gather.12.cloned.1.call-start = ((), (), s32[]{:S(2)}) async-start(), calls=%async_computation.8 | async-start | bytes 2621440 | tf_op jit(solution)/shard_map/all_gather | solution.py:153
  28.7 103.7 %all-gather.14.cloned.1.call-start = ((), (), s32[]{:S(2)}) async-start(), calls=%async_computation.9 | async-start | bytes 7077888 | tf_op jit(solution)/shard_map/all_gather | solution.py:121
  30.0 157.8 %all-gather.16.cloned.1.call-start = ((), (), s32[]{:S(2)}) async-start(), calls=%async_computation.10 | async-start | bytes 4718592 | tf_op jit(solution)/shard_map/all_gather | solution.py:173
  141.6 94.2 %all-gather.18.cloned.1.call-start = ((), (), s32[]{:S(2)}) async-start(), calls=%async_computation.11 | async-start | bytes 4718592 | tf_op jit(solution)/shard_map/all_gather | solution.py:174
  142.7 124.0 %all-gather.20.cloned.1.call-start = ((), (), s32[]{:S(2)}) async-start(), calls=%async_computation.12 | async-start | bytes 2359296 | tf_op jit(solution)/shard_map/all_gather | solution.py:122
  143.5 170.0 %reduce-scatter.9.cloned.1.call-start = ((), (), s32[]{:S(2)}) async-start(), calls=%async_computation.13 | async-start | bytes 2621440 | tf_op jit(solution)/shard_map/reduce_scatter | solution.py:229
  271.2 152.6 %all-gather.24.cloned.1.call-start = ((), (), s32[]{:S(2)}) async-start(), calls=%async_computation.15 | async-start | bytes 12976128 | tf_op jit(solution)/shard_map/all_gather | solution.py:123
  273.8 185.9 %all-gather.22.cloned.1.call-start = ((), (), s32[]{:S(2)}) async-start(), calls=%async_computation.14 | async-start | bytes 2621440 | tf_op jit(solution)/shard_map/all_gather | solution.py:234
  317.5 179.3 %all-gather.30.cloned.1.call-start = ((), (), s32[]{:S(2)}) async-start(), calls=%async_computation.25 | async-start | bytes 2621440 | tf_op jit(solution)/shard_map/all_gather | solution.py:154
  318.2 241.4 %all-gather.26.cloned.1.call-start = ((), (), s32[]{:S(2)}) async-start(), calls=%async_computation.16 | async-start | bytes 6488064 | tf_op jit(solution)/shard_map/all_gather | solution.py:124
  319.2 295.9 %reduce-scatter.13.cloned.1.call-start = ((), (), s32[]{:S(2)}) async-start(), calls=%async_computation.18 | async-start | bytes 2621440 | tf_op jit(solution)/shard_map/reduce_scatter | solution.py:254
  581.6 73.6 %all-gather.28.cloned.1.call-start = ((), (), s32[]{:S(2)}) async-start(), calls=%async_computation.19 | async-start | bytes 2621440 | tf_op jit(solution)/shard_map/all_gather | solution.py:262
  619.8 396.5 %reduce-scatter.15.cloned.1.call-start = ((), (), s32[]{:S(2)}) async-start(), calls=%async_computation.20 | async-start | bytes 2621440 | tf_op jit(solution)/shard_map/reduce_scatter | solution.py:340
  673.9 25.7 %collective-permute-start.1 = (bf16[4,128,512]{1,2,0:T(8,128)(2,1)}, bf16[4,128,512]{1,2,0:T(8,128)(2,1)S(1)}, u32[]{:S(2)}, u32[]{:S(2)}) collective-permute-start(bf16[4,128,512]{1,2,0:T(8,128)(2,1)} %copy.141), channel_id=1, source_target_pairs={{0,4},{4,8},{8,12},{12,16},{16,20},{20,24},{24,28},{28,0},{1,5},{5... | collective-permute-start | bytes 1572872 | tf_op jit(solution)/shard_map/while/body/eval_jaxpr/ppermute | solution.py:24
  711.2 23.3 %collective-permute-start.1 = (bf16[4,128,512]{1,2,0:T(8,128)(2,1)}, bf16[4,128,512]{1,2,0:T(8,128)(2,1)S(1)}, u32[]{:S(2)}, u32[]{:S(2)}) collective-permute-start(bf16[4,128,512]{1,2,0:T(8,128)(2,1)} %copy.141), channel_id=1, source_target_pairs={{0,4},{4,8},{8,12},{12,16},{16,20},{20,24},{24,28},{28,0},{1,5},{5... | collective-permute-start | bytes 1572872 | tf_op jit(solution)/shard_map/while/body/eval_jaxpr/ppermute | solution.py:24
  748.6 20.9 %collective-permute-start.1 = (bf16[4,128,512]{1,2,0:T(8,128)(2,1)}, bf16[4,128,512]{1,2,0:T(8,128)(2,1)S(1)}, u32[]{:S(2)}, u32[]{:S(2)}) collective-permute-start(bf16[4,128,512]{1,2,0:T(8,128)(2,1)} %copy.141), channel_id=1, source_target_pairs={{0,4},{4,8},{8,12},{12,16},{16,20},{20,24},{24,28},{28,0},{1,5},{5... | collective-permute-start | bytes 1572872 | tf_op jit(solution)/shard_map/while/body/eval_jaxpr/ppermute | solution.py:24
  777.6 21.3 %collective-permute-start = (bf16[4,128,512]{1,2,0:T(8,128)(2,1)S(1)}, bf16[4,128,512]{1,2,0:T(8,128)(2,1)S(1)}, u32[]{:S(2)}, u32[]{:S(2)}) collective-permute-start(bf16[4,128,512]{1,2,0:T(8,128)(2,1)S(1)} %copy.140), channel_id=1, source_target_pairs={{0,4},{4,8},{8,12},{12,16},{16,20},{20,24},{24,28},{28,0},{1,5},{5... | collective-permute-start | bytes 1572872 | tf_op jit(solution)/shard_map/while/body/eval_jaxpr/ppermute | solution.py:24
  808.0 20.4 %collective-permute-start.3 = (bf16[4,128,512]{1,2,0:T(8,128)(2,1)S(1)}, bf16[4,128,512]{1,2,0:T(8,128)(2,1)}, u32[]{:S(2)}, u32[]{:S(2)}) collective-permute-start(bf16[4,128,512]{1,2,0:T(8,128)(2,1)S(1)} %convert_element_type.443), channel_id=1, source_target_pairs={{0,4},{4,8},{8,12},{12,16},{16,20},{20,24},{24,28},{28,0},{1,5},{5... | collective-permute-start | bytes 1572872 | tf_op jit(solution)/shard_map/while/body/eval_jaxpr/ppermute | solution.py:24
  808.5 25.4 %collective-permute-start = (bf16[4,128,512]{1,2,0:T(8,128)(2,1)S(1)}, bf16[4,128,512]{1,2,0:T(8,128)(2,1)S(1)}, u32[]{:S(2)}, u32[]{:S(2)}) collective-permute-start(bf16[4,128,512]{1,2,0:T(8,128)(2,1)S(1)} %copy.140), channel_id=1, source_target_pairs={{0,4},{4,8},{8,12},{12,16},{16,20},{20,24},{24,28},{28,0},{1,5},{5... | collective-permute-start | bytes 1572872 | tf_op jit(solution)/shard_map/while/body/eval_jaxpr/ppermute | solution.py:24
  814.2 25.3 %collective-permute-start.1 = (bf16[4,128,512]{1,2,0:T(8,128)(2,1)}, bf16[4,128,512]{1,2,0:T(8,128)(2,1)S(1)}, u32[]{:S(2)}, u32[]{:S(2)}) collective-permute-start(bf16[4,128,512]{1,2,0:T(8,128)(2,1)} %copy.141), channel_id=1, source_target_pairs={{0,4},{4,8},{8,12},{12,16},{16,20},{20,24},{24,28},{28,0},{1,5},{5... | collective-permute-start | bytes 1572872 | tf_op jit(solution)/shard_map/while/body/eval_jaxpr/ppermute | solution.py:24
  843.1 25.8 %collective-permute-start = (bf16[4,128,512]{1,2,0:T(8,128)(2,1)S(1)}, bf16[4,128,512]{1,2,0:T(8,128)(2,1)S(1)}, u32[]{:S(2)}, u32[]{:S(2)}) collective-permute-start(bf16[4,128,512]{1,2,0:T(8,128)(2,1)S(1)} %copy.140), channel_id=1, source_target_pairs={{0,4},{4,8},{8,12},{12,16},{16,20},{20,24},{24,28},{28,0},{1,5},{5... | collective-permute-start | bytes 1572872 | tf_op jit(solution)/shard_map/while/body/eval_jaxpr/ppermute | solution.py:24
  851.6 22.9 %collective-permute-start.1 = (bf16[4,128,512]{1,2,0:T(8,128)(2,1)}, bf16[4,128,512]{1,2,0:T(8,128)(2,1)S(1)}, u32[]{:S(2)}, u32[]{:S(2)}) collective-permute-start(bf16[4,128,512]{1,2,0:T(8,128)(2,1)} %copy.141), channel_id=1, source_target_pairs={{0,4},{4,8},{8,12},{12,16},{16,20},{20,24},{24,28},{28,0},{1,5},{5... | collective-permute-start | bytes 1572872 | tf_op jit(solution)/shard_map/while/body/eval_jaxpr/ppermute | solution.py:24
  878.1 25.8 %collective-permute-start = (bf16[4,128,512]{1,2,0:T(8,128)(2,1)S(1)}, bf16[4,128,512]{1,2,0:T(8,128)(2,1)S(1)}, u32[]{:S(2)}, u32[]{:S(2)}) collective-permute-start(bf16[4,128,512]{1,2,0:T(8,128)(2,1)S(1)} %copy.140), channel_id=1, source_target_pairs={{0,4},{4,8},{8,12},{12,16},{16,20},{20,24},{24,28},{28,0},{1,5},{5... | collective-permute-start | bytes 1572872 | tf_op jit(solution)/shard_map/while/body/eval_jaxpr/ppermute | solution.py:24
  882.5 27.0 %collective-permute-start.1 = (bf16[4,128,512]{1,2,0:T(8,128)(2,1)}, bf16[4,128,512]{1,2,0:T(8,128)(2,1)S(1)}, u32[]{:S(2)}, u32[]{:S(2)}) collective-permute-start(bf16[4,128,512]{1,2,0:T(8,128)(2,1)} %copy.141), channel_id=1, source_target_pairs={{0,4},{4,8},{8,12},{12,16},{16,20},{20,24},{24,28},{28,0},{1,5},{5... | collective-permute-start | bytes 1572872 | tf_op jit(solution)/shard_map/while/body/eval_jaxpr/ppermute | solution.py:24
  913.1 25.8 %collective-permute-start = (bf16[4,128,512]{1,2,0:T(8,128)(2,1)S(1)}, bf16[4,128,512]{1,2,0:T(8,128)(2,1)S(1)}, u32[]{:S(2)}, u32[]{:S(2)}) collective-permute-start(bf16[4,128,512]{1,2,0:T(8,128)(2,1)S(1)} %copy.140), channel_id=1, source_target_pairs={{0,4},{4,8},{8,12},{12,16},{16,20},{20,24},{24,28},{28,0},{1,5},{5... | collective-permute-start | bytes 1572872 | tf_op jit(solution)/shard_map/while/body/eval_jaxpr/ppermute | solution.py:24
  916.6 27.9 %collective-permute-start.1 = (bf16[4,128,512]{1,2,0:T(8,128)(2,1)}, bf16[4,128,512]{1,2,0:T(8,128)(2,1)S(1)}, u32[]{:S(2)}, u32[]{:S(2)}) collective-permute-start(bf16[4,128,512]{1,2,0:T(8,128)(2,1)} %copy.141), channel_id=1, source_target_pairs={{0,4},{4,8},{8,12},{12,16},{16,20},{20,24},{24,28},{28,0},{1,5},{5... | collective-permute-start | bytes 1572872 | tf_op jit(solution)/shard_map/while/body/eval_jaxpr/ppermute | solution.py:24
  959.8 279.0 %all-reduce.3.cloned.1.call-start = ((), (), s32[]{:S(2)}) async-start(), calls=%async_computation.26 | async-start | bytes 23068672
  993.7 283.3 %reduce-scatter.19.cloned.1.call-start = ((), (), s32[]{:S(2)}) async-start(), calls=%async_computation.22 | async-start | bytes 2359296 | tf_op jit(solution)/shard_map/reduce_scatter | solution.py:369
  999.0 314.8 %reduce-scatter.11.cloned.1.call-start = ((), (), s32[]{:S(2)}) async-start(), calls=%async_computation.17 | async-start | bytes 2621440 | tf_op jit(solution)/shard_map/reduce_scatter | solution.py:243
  1007.0 373.8 %reduce-scatter.21.cloned.1.call-start = ((), (), s32[]{:S(2)}) async-start(), calls=%async_computation.23 | async-start | bytes 6488064 | tf_op jit(solution)/shard_map/reduce_scatter | solution.py:375
  1014.8 397.6 %reduce-scatter.23.cloned.1.call-start = ((), (), s32[]{:S(2)}) async-start(), calls=%async_computation.24 | async-start | bytes 36864 | tf_op jit(solution)/shard_map/reduce_scatter | solution.py:378
  1019.8 462.7 %reduce-scatter.17.cloned.1.call-start = ((), (), s32[]{:S(2)}) async-start(), calls=%async_computation.21 | async-start | bytes 7077888 | tf_op jit(solution)/shard_map/reduce_scatter | solution.py:366
  (75 other events, 2528.3 us)
Sparse Core Ops, SparseCore 0:
  28.8 36.1 all-gather.11
  67.2 65.1 all-gather.13
  141.7 45.9 all-gather.15
  189.8 45.9 all-gather.17
  237.8 28.7 all-gather.19
  271.3 42.1 reduce-scatter.8
  315.8 108.0 all-gather.23
  426.2 33.4 all-gather.21
  461.6 35.1 all-gather.29
  498.8 60.7 all-gather.25
  581.7 33.3 reduce-scatter.12
  619.9 35.1 all-gather.27
  959.9 41.7 reduce-scatter.14
  1003.9 234.7 all-reduce.2
  1240.9 36.0 reduce-scatter.18
  1279.8 33.8 reduce-scatter.10
  1315.9 64.7 reduce-scatter.20
  1383.4 28.9 reduce-scatter.22
  1414.6 67.8 reduce-scatter.16
where the time goes:
time: 1500 us; the launch traced here: 1490 us
  waiting for transfers between devices  1060 us (71%)
  other arithmetic  107 us (7%)
  matrix products  105 us (7%)
  local copies, waits for them, and re-layouts  96.9 us (6%)
  starting transfers between devices  82.2 us (5%)
  blocking collectives  25.9 us (2%)
  between operations  15.9 us (1%)
    unnamed x20, waiting for transfers between devices  201 us
    ppermute x32, waiting for transfers between devices, shifted(): return lax.ppermute(value, axis, pairs)  143 us
    all_gather x1, waiting for transfers between devices, local(): lax.all_gather(w_gu.astype(jnp.bfloat16), 'ctx', axis=0, tiled=True)  105 us
    ppermute x32, starting transfers between devices, shifted(): return lax.ppermute(value, axis, pairs)  80.1 us
    all_gather x1, waiting for transfers between devices, local(): lax.all_gather(w_qkv.astype(jnp.bfloat16), 'ctx', axis=0, tiled=True)  67.3 us
    reduce_scatter x1, waiting for transfers between devices, local(): lax.psum_scatter(grad_down.astype(jnp.bfloat16), 'ctx', scatter_dimension...  63.4 us
    all_gather x1, waiting for transfers between devices, local(): lax.all_gather(w_down.astype(jnp.bfloat16), 'ctx', axis=1, tiled=True)  62.9 us
    reduce_scatter x1, waiting for transfers between devices, local(): lax.psum_scatter(grad_qkv.astype(jnp.bfloat16), 'ctx', scatter_dimension=...  59.4 us
  transfers between devices with their start and end apart: 51, of which 49 were waited for; matrix products, arithmetic and copies ran while one was open for 13% of the time, Pallas kernels for 0%

commit v1 on v0

v1 whole, which is shorter than its diff:
```python
import functools

import jax
import jax.numpy as jnp
from jax import lax
from jax.experimental import pallas as pl
from jax.experimental.pallas import tpu as pltpu
from jax.sharding import PartitionSpec as P

HD = 64
ROT = 16
STEP = 4


learn_rate = 0.005
beta_first = 0.9
beta_second = 0.95
adam_epsilon = 1e-08
weight_decay = 0.1
norm_epsilon = 1e-05
masked_score = -1e30
score_scale = HD ** (-0.5)
F32 = jnp.float32
BF16 = jnp.bfloat16


def swapped(value, axis, bits):
    count = lax.axis_size(axis)
    return lax.ppermute(value, axis, [(source, source ^ bits) for source in range(count)])


def gather_rows(block, axis):
    count = lax.axis_size(axis)
    return [block] + [swapped(block, axis, bits) for bits in range(1, count)]


def scatter_sum(blocks, axis):
    total = blocks[0].astype(F32)
    for bits in range(1, len(blocks)):
        total = total + swapped(blocks[bits], axis, bits).astype(F32)
    return total


def butterfly(value, axis):
    count = lax.axis_size(axis)
    bits = 1
    while bits < count:
        value = value + swapped(value, axis, bits)
        bits *= 2
    return value


def layer_norm(matrix, gain_vec, shift_vec):
    centre = matrix - jnp.mean(matrix, axis=-1, keepdims=True)
    inverse = lax.rsqrt(jnp.mean(centre * centre, axis=-1, keepdims=True) + norm_epsilon)
    normed = centre * inverse
    return (normed * gain_vec + shift_vec, normed, inverse)


def norm_back(incoming, normed, inverse, gain_vec):
    scaled = incoming * gain_vec
    inner = (
        scaled
        - jnp.mean(scaled, axis=-1, keepdims=True)
        - normed * jnp.mean(scaled * normed, axis=-1, keepdims=True)
    )
    return (inner * inverse, jnp.sum(incoming * normed, axis=0), jnp.sum(incoming, axis=0))


def rotary_tables(positions, width):
    half_rot = ROT // 2
    lane = jnp.arange(width, dtype=jnp.int32) % HD
    frequency = 10000.0 ** (-2.0 * (lane % half_rot).astype(F32) / ROT)
    angles = positions.astype(F32)[:, None] * frequency[None, :]
    turning = (lane < ROT)[None, :]
    low_lane = (lane < half_rot)[None, :]
    cosine = jnp.where(turning, jnp.cos(angles), 1.0)
    sine = jnp.where(turning, jnp.sin(angles), 0.0)
    return cosine, jnp.where(low_lane, -sine, 0.0), jnp.where(low_lane, 0.0, sine)


def turned(value, cosine, from_right, from_left):
    width = value.shape[-1]
    half_rot = ROT // 2
    return (
        value * cosine
        + pltpu.roll(value, width - half_rot, 1) * from_right
        + pltpu.roll(value, half_rot, 1) * from_left
    )


def dot_rows(left_side, right_side):
    return lax.dot_general(
        left_side, right_side, (((0,), (0,)), ((), ())), preferred_element_type=F32
    )


def dot_back(left_side, right_side):
    return lax.dot_general(
        left_side, right_side, (((1,), (1,)), ((), ())), preferred_element_type=F32
    )


def dot(left_side, right_side):
    return jnp.dot(left_side, right_side, preferred_element_type=F32)


def adam_step(master, gradient, first_moment, second_moment, decay_rate):
    moment_one = beta_first * first_moment + (1.0 - beta_first) * gradient
    moment_two = beta_second * second_moment + (1.0 - beta_second) * gradient * gradient
    corrected = moment_one / (1.0 - beta_first**STEP)
    spread = jnp.sqrt(moment_two / (1.0 - beta_second**STEP))
    updated = master - learn_rate * (corrected / (spread + adam_epsilon) + decay_rate * master)
    return (updated, moment_one, moment_two)


def kernel_params(megabytes=48):
    return pltpu.CompilerParams(vmem_limit_bytes=megabytes * 1024 * 1024)


def project_kernel(count, groups, *refs):
    blocks = refs[:count]
    gain, shift, bias_q, bias_v, cosine, from_right, from_left, wq, wk, wv = refs[count : count + 10]
    normed_ref, out_ref = refs[count + 10 :]
    rows, _ = blocks[0].shape
    width = wq.shape[1]

    @pl.when(pl.program_id(0) == 0)
    def _():
        for place in range(count):
            value, _, _ = layer_norm(blocks[place][...].astype(F32), gain[...], shift[...])
            normed_ref[place * rows : (place + 1) * rows, :] = value.astype(BF16)

    for which, weight in enumerate((wq, wk, wv)):
        result = dot(normed_ref[...], weight[...])
        if which == 0:
            result = result + bias_q[...]
        if which == 2:
            result = result + bias_v[...]
        for place in range(count):
            part = result[place * rows : (place + 1) * rows]
            if which < 2:
                part = turned(part, cosine[...], from_right[...], from_left[...])
            out_ref[place, 0, :, which * width : (which + 1) * width] = part.astype(BF16)


def project(blocks, gain, shift, bias_q, bias_v, tables, weights, groups):
    count = len(blocks)
    rows, depth = blocks[0].shape
    head_cols = bias_q.shape[1]
    width = head_cols // groups

    def whole(array):
        return pl.BlockSpec(array.shape, lambda g: (0, 0))

    def column(first):
        return pl.BlockSpec((depth, width), lambda g: (0, first * groups + g))

    operands = [*blocks, gain, shift, bias_q, bias_v, *tables]
    specs = [whole(block) for block in blocks] + [whole(gain), whole(shift)]
    specs += [pl.BlockSpec((1, width), lambda g: (0, g))] * 2
    specs += [whole(table) for table in tables]
    specs += [column(0), column(1), column(2)]
    return pl.pallas_call(
        functools.partial(project_kernel, count, groups),
        grid=(groups,),
        in_specs=specs,
        out_specs=[
            pl.BlockSpec((count * rows, depth), lambda g: (0, 0)),
            pl.BlockSpec((count, 1, rows, 3 * width), lambda g: (0, g, 0, 0)),
        ],
        out_shape=[
            jax.ShapeDtypeStruct((count * rows, depth), BF16),
            jax.ShapeDtypeStruct((count, groups, rows, 3 * width), BF16),
        ],
        compiler_params=kernel_params(),
        cost_estimate=pl.CostEstimate(
            flops=2 * count * rows * depth * 3 * head_cols,
            bytes_accessed=2 * depth * 3 * head_cols + 4 * count * rows * depth,
            transcendentals=0,
        ),
        name="project",
    )(*operands, weights, weights, weights)


def windows(length, most, rows):
    for start in range(0, length, rows):
        first = max(0, (start - (most - 1)) // rows * rows)
        yield start, first, start + rows


def seen(start, first, stop, rows, ids_row, ids_col):
    query_pos = start + lax.broadcasted_iota(jnp.int32, (rows, stop - first), 0)
    key_pos = first + lax.broadcasted_iota(jnp.int32, (rows, stop - first), 1)
    same = ids_row[:, first:stop] == ids_col[start : start + rows, :]
    return (key_pos <= query_pos) & same


def head_mask(width, head):
    lane = lax.broadcasted_iota(jnp.int32, (1, width), 1) // HD
    return jnp.where(lane == head, 1.0, 0.0).astype(F32)


def attend_kernel(count, most, step_rows, me_ref, ids_row_ref, ids_col_ref, *refs):
    pieces = refs[:count]
    att_ref, all_ref, lse_ref = refs[count:]
    rows = pieces[0].shape[0]
    width = pieces[0].shape[1] // 3
    length = count * rows
    me = me_ref[0]
    for bits in range(count):
        place = pl.multiple_of((me ^ bits) * rows, rows)
        all_ref[pl.ds(place, rows), :] = pieces[bits][...]
    ids_row = ids_row_ref[...]
    stat_lane = lax.broadcasted_iota(jnp.int32, (step_rows, 128), 1)
    for start, first, stop in windows(length, most, step_rows):
        allowed = seen(start, first, stop, step_rows, ids_row, ids_col_ref)
        query = all_ref[start : start + step_rows, 0:width]
        key = all_ref[first:stop, width : 2 * width]
        value = all_ref[first:stop, 2 * width : 3 * width]
        stats = jnp.zeros((step_rows, 128), F32)
        total = jnp.zeros((step_rows, width), F32)
        for head in range(width // HD):
            mask = head_mask(width, head).astype(BF16)
            scores = dot_back(query * mask, key) * score_scale
            scores = jnp.where(allowed, scores, masked_score)
            top = jnp.max(scores, axis=-1, keepdims=True)
            weights = jnp.exp(scores - top)
            weight_sum = jnp.sum(weights, axis=-1, keepdims=True)
            total = total + dot(weights.astype(BF16), value * mask) / weight_sum
            stats = jnp.where(stat_lane == head, top + jnp.log(weight_sum), stats)
        att_ref[start : start + step_rows, :] = total.astype(BF16)
        lse_ref[start : start + step_rows, :] = stats


def attend(me, ids_row, ids_col, pieces, most):
    count = len(pieces)
    rows, wide = pieces[0].shape
    width = wide // 3
    length = count * rows
    step_rows = min(256, length)
    vmem = pl.BlockSpec(memory_space=pltpu.VMEM)
    return pl.pallas_call(
        functools.partial(attend_kernel, count, most, step_rows),
        in_specs=[pl.BlockSpec(memory_space=pltpu.SMEM)] + [vmem] * (2 + count),
        out_specs=[vmem] * 3,
        out_shape=[
            jax.ShapeDtypeStruct((length, width), BF16),
            jax.ShapeDtypeStruct((length, wide), BF16),
            jax.ShapeDtypeStruct((length, 128), F32),
        ],
        compiler_params=kernel_params(),
        cost_estimate=pl.CostEstimate(
            flops=4 * length * most * width * 4, bytes_accessed=4 * length * wide, transcendentals=0
        ),
        name="attend",
    )(me, ids_row, ids_col, *pieces)


def attend_back_kernel(
    count, most, step_rows, me_ref, ids_row_ref, ids_col_ref, cos_ref, right_ref, left_ref, *refs
):
    pieces = refs[:count]
    att_ref, all_ref, lse_ref, out_ref, sums_ref, grad_ref, dk_ref, dv_ref = refs[count:]
    rows, width = pieces[0].shape
    length = count * rows
    me = me_ref[0]
    for bits in range(count):
        place = pl.multiple_of((me ^ bits) * rows, rows)
        grad_ref[pl.ds(place, rows), :] = pieces[bits][...]
    dk_ref[...] = jnp.zeros_like(dk_ref)
    dv_ref[...] = jnp.zeros_like(dv_ref)
    ids_row = ids_row_ref[...]
    query_sum = jnp.zeros((1, width), F32)
    for start, first, stop in windows(length, most, step_rows):
        own = slice(start, start + step_rows)
        allowed = seen(start, first, stop, step_rows, ids_row, ids_col_ref)
        query = all_ref[own, 0:width]
        key = all_ref[first:stop, width : 2 * width]
        value = all_ref[first:stop, 2 * width : 3 * width]
        incoming = grad_ref[own, :]
        product = incoming.astype(F32) * att_ref[own, :].astype(F32)
        query_grad = jnp.zeros((step_rows, width), F32)
        key_grad = jnp.zeros((stop - first, width), F32)
        value_grad = jnp.zeros((stop - first, width), F32)
        for head in range(width // HD):
            mask32 = head_mask(width, head)
            mask = mask32.astype(BF16)
            delta = jnp.sum(product * mask32, axis=-1, keepdims=True)
            scores = dot_back(query * mask, key) * score_scale
            probability = jnp.where(
                allowed, jnp.exp(scores - lse_ref[own, head : head + 1]), 0.0
            )
            incoming_head = incoming * mask
            value_grad = value_grad + dot_rows(probability.astype(BF16), incoming_head)
            grad_prob = dot_back(incoming_head, value)
            grad_score = (probability * (grad_prob - delta) * score_scale).astype(BF16)
            query_grad = query_grad + dot(grad_score, key * mask)
            key_grad = key_grad + dot_rows(grad_score, query * mask)
        dk_ref[first:stop, :] += key_grad
        dv_ref[first:stop, :] += value_grad
        query_grad = turned(query_grad, cos_ref[own, :], -right_ref[own, :], -left_ref[own, :])
        query_sum = query_sum + jnp.sum(query_grad, axis=0, keepdims=True)
        out_ref[own, 0:width] = query_grad.astype(BF16)
    out_ref[:, width : 2 * width] = turned(
        dk_ref[...], cos_ref[...], -right_ref[...], -left_ref[...]
    ).astype(BF16)
    value_grad = dv_ref[...]
    out_ref[:, 2 * width : 3 * width] = value_grad.astype(BF16)
    value_sum = jnp.sum(value_grad, axis=0, keepdims=True)
    sums_ref[...] = jnp.concatenate(
        [query_sum, value_sum, jnp.zeros((6, width), F32)], axis=0
    )


def attend_back(me, ids_row, ids_col, tables, pieces, att, everything, lse, most):
    count = len(pieces)
    rows, width = pieces[0].shape
    length = count * rows
    step_rows = min(256, length)
    vmem = pl.BlockSpec(memory_space=pltpu.VMEM)
    return pl.pallas_call(
        functools.partial(attend_back_kernel, count, most, step_rows),
        in_specs=[pl.BlockSpec(memory_space=pltpu.SMEM)] + [vmem] * (8 + count),
        out_specs=[vmem] * 2,
        out_shape=[
            jax.ShapeDtypeStruct((length, 3 * width), BF16),
            jax.ShapeDtypeStruct((8, width), F32),
        ],
        scratch_shapes=[
            pltpu.VMEM((length, width), BF16),
            pltpu.VMEM((length, width), F32),
            pltpu.VMEM((length, width), F32),
        ],
        compiler_params=kernel_params(),
        cost_estimate=pl.CostEstimate(
            flops=10 * length * most * width * 4,
            bytes_accessed=16 * length * width,
            transcendentals=0,
        ),
        name="attend_back",
    )(me, ids_row, ids_col, *tables, *pieces, att, everything, lse)


def place_kernel(count, groups, parts, me_ref, *refs):
    pieces = refs[:count]
    out_ref = refs[count]
    rows = pieces[0].shape[0]
    width = pieces[0].shape[1] // parts
    for bits in range(count):
        source = me_ref[0] ^ bits
        row = pl.multiple_of(((source // groups) ^ me_ref[1]) * rows, rows)
        for part in range(parts):
            col = pl.multiple_of((part * groups + source % groups) * width, width)
            out_ref[pl.ds(row, rows), pl.ds(col, width)] = pieces[bits][
                :, part * width : (part + 1) * width
            ]


def place(places, pieces, groups, parts):
    count = len(pieces)
    rows, wide = pieces[0].shape
    vmem = pl.BlockSpec(memory_space=pltpu.VMEM)
    return pl.pallas_call(
        functools.partial(place_kernel, count, groups, parts),
        in_specs=[pl.BlockSpec(memory_space=pltpu.SMEM)] + [vmem] * count,
        out_specs=vmem,
        out_shape=jax.ShapeDtypeStruct((count // groups * rows, groups * wide), BF16),
        compiler_params=kernel_params(),
        cost_estimate=pl.CostEstimate(
            flops=0, bytes_accessed=4 * count * rows * wide, transcendentals=0
        ),
        name="place",
    )(places, *pieces)


def local(
    hidden,
    cotangent,
    doc_ids,
    w_qkv,
    w_out,
    w_gu,
    w_down,
    norm_vecs,
    first_qkv,
    first_out,
    first_gu,
    first_down,
    first_vecs,
    second_qkv,
    second_out,
    second_gu,
    second_down,
    second_vecs,
):
    ctx_size = lax.axis_size("ctx")
    ctx_place = lax.axis_index("ctx")
    shard_count = lax.axis_size("wsh")
    shard_place = lax.axis_index("wsh")
    tok_rows = hidden.shape[1]
    depth = hidden.shape[2]
    length = doc_ids.shape[1]
    most = length // 2
    head_cols = w_qkv.shape[2]
    unit_cols = w_gu.shape[2]
    own_rows = w_qkv.shape[0]
    groups = ctx_size // shard_count
    width = head_cols // groups
    ctx_scalar = ctx_place.astype(jnp.int32).reshape(1)
    places = jnp.stack([ctx_place, shard_place]).astype(jnp.int32)

    vec_cols = jnp.pad(norm_vecs.astype(BF16), ((0, 0), (0, 128 - norm_vecs.shape[1])))
    first_weights = jnp.concatenate(
        [w_qkv.astype(BF16).reshape(own_rows, 3 * head_cols), w_out.astype(BF16).T, vec_cols], axis=1
    )
    first_all = lax.all_gather(first_weights, "ctx", axis=0, tiled=True)
    gu_flat = lax.all_gather(
        w_gu.astype(BF16).reshape(own_rows, 2 * unit_cols), "ctx", axis=0, tiled=True
    )
    down_weight = lax.all_gather(w_down.astype(BF16), "ctx", axis=1, tiled=True)

    hidden_blocks = gather_rows(hidden[0], "wsh")
    cot_all = jnp.concatenate(gather_rows(cotangent[0], "wsh"), axis=0)

    own_seq = ctx_place // groups
    ids_own = lax.dynamic_slice_in_dim(doc_ids, own_seq, 1, 0)
    ids_col = ids_own.reshape(length, 1)
    positions = ctx_place * tok_rows + jnp.arange(tok_rows, dtype=jnp.int32)
    tables = rotary_tables(positions, width)
    tables_all = rotary_tables(jnp.arange(length, dtype=jnp.int32), width)

    vectors = first_all[:, 4 * head_cols : 4 * head_cols + 8].astype(F32).T
    gain_one, shift_one, gain_two, shift_two = [vectors[row : row + 1] for row in range(4)]
    col_start = shard_place * head_cols
    bias_query = lax.dynamic_slice_in_dim(vectors[4:5], col_start, head_cols, 1)
    bias_value = lax.dynamic_slice_in_dim(vectors[5:6], col_start, head_cols, 1)
    qkv_flat = first_all[:, : 3 * head_cols]
    out_turned = first_all[:, 3 * head_cols : 4 * head_cols]

    gathered_one, projected = project(
        hidden_blocks, gain_one, shift_one, bias_query, bias_value, tables, first_all, groups
    )

    def exchange_out(array, bits):
        target = ctx_place ^ bits
        picked = lax.dynamic_slice(
            array,
            ((target // groups) ^ shard_place, target % groups, 0, 0),
            (1, 1) + array.shape[2:],
        )[0, 0]
        return picked if bits == 0 else swapped(picked, "ctx", bits)

    def exchange_back(array, bits):
        picked = lax.dynamic_slice_in_dim(array, (ctx_place ^ bits) * tok_rows, tok_rows, 0)
        return picked if bits == 0 else swapped(picked, "ctx", bits)

    pieces = [exchange_out(projected, bits) for bits in range(ctx_size)]
    att_own, qkv_own, log_sums = attend(ctx_scalar, ids_own, ids_col, pieces, most)
    attended = place(
        places, [exchange_back(att_own, bits) for bits in range(ctx_size)], groups, 1
    )

    def row_blocks(matrix):
        return [
            matrix[place_row * tok_rows : (place_row + 1) * tok_rows]
            for place_row in range(shard_count)
        ]

    attn_terms = dot_back(attended, out_turned).astype(BF16)
    middle = hidden[0].astype(F32) + scatter_sum(row_blocks(attn_terms), "wsh")
    normed_two, hat_two, inverse_two = layer_norm(middle, gain_two, shift_two)
    gathered_two = jnp.concatenate(gather_rows(normed_two.astype(BF16), "wsh"), axis=0)
    gate_up = dot(gathered_two, gu_flat)
    gate_part = gate_up[:, :unit_cols]
    up_part = gate_up[:, unit_cols:]
    sigmoid_gate = jax.nn.sigmoid(gate_part)
    activated = (gate_part * sigmoid_gate * up_part).astype(BF16)
    grad_down = dot_rows(activated, cot_all).astype(BF16)
    share_down = lax.psum_scatter(grad_down, "ctx", scatter_dimension=1, tiled=True).astype(F32)

    grad_act = dot_back(cot_all, down_weight)
    grad_gate = grad_act * up_part * sigmoid_gate * (1.0 + gate_part * (1.0 - sigmoid_gate))
    grad_up = grad_act * gate_part * sigmoid_gate
    grad_gate_up = jnp.concatenate([grad_gate, grad_up], axis=1).astype(BF16)
    grad_gu = dot_rows(gathered_two, grad_gate_up).astype(BF16)
    share_gu = lax.psum_scatter(grad_gu, "ctx", scatter_dimension=0, tiled=True).astype(F32)
    normed_two_terms = dot_back(grad_gate_up, gu_flat).astype(BF16)
    grad_normed_two = scatter_sum(row_blocks(normed_two_terms), "wsh")
    grad_middle, grad_gain_two, grad_shift_two = norm_back(
        grad_normed_two, hat_two, inverse_two, gain_two
    )
    grad_middle = grad_middle + cotangent[0].astype(F32)
    middle_all = jnp.concatenate(gather_rows(grad_middle.astype(BF16), "wsh"), axis=0)
    grad_out = dot_rows(attended, middle_all).astype(BF16)
    share_out = lax.psum_scatter(grad_out, "ctx", scatter_dimension=1, tiled=True).astype(F32)
    grad_att = dot(middle_all, out_turned).astype(BF16)
    grad_att = grad_att.reshape(shard_count, tok_rows, groups, width).transpose(0, 2, 1, 3)
    grad_pieces = [exchange_out(grad_att, bits) for bits in range(ctx_size)]
    grad_own, bias_sums = attend_back(
        ctx_scalar, ids_own, ids_col, tables_all, grad_pieces, att_own, qkv_own, log_sums, most
    )
    grad_rows = place(
        places, [exchange_back(grad_own, bits) for bits in range(ctx_size)], groups, 3
    )
    grad_qkv = dot_rows(gathered_one, grad_rows).astype(BF16)
    share_qkv = lax.psum_scatter(grad_qkv, "ctx", scatter_dimension=0, tiled=True).astype(F32)

    ffn_terms = dot(activated, down_weight).astype(BF16)
    block_out = (middle + scatter_sum(row_blocks(ffn_terms), "wsh")).astype(BF16)

    normed_one_terms = dot_back(grad_rows, qkv_flat).astype(BF16)
    grad_normed_one = scatter_sum(row_blocks(normed_one_terms), "wsh")
    _, hat_one, inverse_one = layer_norm(hidden[0].astype(F32), gain_one, shift_one)
    grad_input, grad_gain_one, grad_shift_one = norm_back(
        grad_normed_one, hat_one, inverse_one, gain_one
    )
    grad_input = grad_input + grad_middle

    bias_start = shard_place * head_cols + (ctx_place % groups) * width
    bias_rows = lax.dynamic_update_slice(
        jnp.zeros((2, depth), F32), bias_sums[:2], (0, bias_start)
    )
    vec_terms = jnp.concatenate(
        [
            grad_gain_one[None],
            grad_shift_one[None],
            grad_gain_two[None],
            grad_shift_two[None],
            bias_rows,
            jnp.zeros((2, depth), F32),
        ],
        axis=0,
    )
    vec_sums = butterfly(butterfly(vec_terms, "ctx"), "wsh")
    share_vecs = lax.dynamic_slice_in_dim(vec_sums, ctx_place * own_rows, own_rows, 1).T[:, :6]

    share_qkv = share_qkv.reshape(w_qkv.shape)
    share_gu = share_gu.reshape(w_gu.shape)
    new_qkv, new_first_qkv, new_second_qkv = adam_step(
        w_qkv, share_qkv, first_qkv, second_qkv, weight_decay
    )
    new_out, new_first_out, new_second_out = adam_step(
        w_out, share_out, first_out, second_out, weight_decay
    )
    new_gu, new_first_gu, new_second_gu = adam_step(
        w_gu, share_gu, first_gu, second_gu, weight_decay
    )
    new_down, new_first_down, new_second_down = adam_step(
        w_down, share_down, first_down, second_down, weight_decay
    )
    new_vecs, new_first_vecs, new_second_vecs = adam_step(
        norm_vecs, share_vecs, first_vecs, second_vecs, 0.0
    )
    return (
        block_out[None],
        grad_input[None],
        share_qkv,
        share_out,
        share_gu,
        share_down,
        share_vecs,
        new_qkv,
        new_out,
        new_gu,
        new_down,
        new_vecs,
        new_first_qkv,
        new_first_out,
        new_first_gu,
        new_first_down,
        new_first_vecs,
        new_second_qkv,
        new_second_out,
        new_second_gu,
        new_second_down,
        new_second_vecs,
    )


def solution(mesh):
    rows = P("wsh", "ctx", None)
    weights = (
        P("ctx", None, "wsh"),
        P("wsh", "ctx"),
        P("ctx", None, "wsh"),
        P("wsh", "ctx"),
        P("ctx", None),
    )
    return jax.shard_map(
        local,
        mesh=mesh,
        in_specs=(rows, rows, P()) + weights * 3,
        out_specs=(rows, rows) + weights * 4,
        check_vma=False,
    )
```

time: 1500 us -> 781 us (0.52)
  waiting for transfers between devices: 1060 us -> 457 us
  other arithmetic: 107 us -> 45.8 us
  local copies, waits for them, and re-layouts: 96.9 us -> 48.3 us
  matrix products: 105 us -> 73.8 us
  Pallas kernels: 0 us -> 26.4 us
  blocking collectives: 25.9 us -> 0 us
  starting transfers between devices: 82.2 us -> 107 us
    all_gather x10 -> x3, waiting for transfers between devices: 434 us -> 93.3 us  [the longest x1 80.1 us: local(): first_all = lax.all_gather(first_weights, 'ctx', axis=0, tiled=True)]
    unnamed x20 -> x7, waiting for transfers between devices: 201 us -> 0.11 us
    reduce_scatter x8 -> x4, waiting for transfers between devices: 281 us -> 106 us  [the longest x1 100 us: local(): lax.psum_scatter(grad_gu, 'ctx', scatter_dimension=0, tiled=True)]
    ppermute x32 -> x57, waiting for transfers between devices: 143 us -> 257 us  [swapped(): lax.ppermute(value, axis, [(source, source ^ bits) for source in range(co...]
    convert_element_type x42 -> x8, other arithmetic: 45.3 us -> 5.34 us  [the longest x1 3.08 us: local(): grad_middle.astype(BF16)]
    convert_element_type x4 -> x1, local copies, waits for them, and re-layouts: 32.4 us -> 0.14 us  [local(): norm_vecs.astype(BF16)]
    pallas_call x0 -> x5, Pallas kernels: none -> 26.4 us  [the longest x1 11.9 us: attend_back(): pl.pallas_call(functools.partial(attend_back_kernel, count, most, step_ro...]
    ppermute x32 -> x57, starting transfers between devices: 80.1 us -> 106 us  [swapped(): lax.ppermute(value, axis, [(source, source ^ bits) for source in range(co...]
  transfers between devices with their start and end apart: 51 -> 64, of which waited for: 49 -> 42; matrix products, arithmetic and copies ran while one was open for 13% -> 15% of each run, Pallas kernels for 0% -> 3%
where the time goes in v1:
time: 781 us; the launch traced here: 773 us
  waiting for transfers between devices  457 us (59%)
  starting transfers between devices  107 us (14%)
  matrix products  73.8 us (9%)
  local copies, waits for them, and re-layouts  48.3 us (6%)
  other arithmetic  45.8 us (6%)
  Pallas kernels  26.4 us (3%)
  between operations  15.4 us (2%)
    ppermute x57, waiting for transfers between devices, swapped(): lax.ppermute(value, axis, [(source, source ^ bits) for source in range(co...  257 us
    ppermute x57, starting transfers between devices, swapped(): lax.ppermute(value, axis, [(source, source ^ bits) for source in range(co...  106 us
    reduce_scatter x1, waiting for transfers between devices, local(): lax.psum_scatter(grad_gu, 'ctx', scatter_dimension=0, tiled=True)  100 us
    all_gather x1, waiting for transfers between devices, local(): first_all = lax.all_gather(first_weights, 'ctx', axis=0, tiled=True)  80.1 us
    unnamed x87, local copies, waits for them, and re-layouts  28.4 us
    sub x5, other arithmetic, adam_step(): master - learn_rate * (corrected / (spread + adam_epsilon) + decay_rate *...  27.4 us
    dot_general x4, matrix products, dot_rows(): lax.dot_general(left_side, right_side, (((0,), (0,)), ((), ())), preferre...  26.5 us
    dot_general x4, matrix products, dot_back(): lax.dot_general(left_side, right_side, (((1,), (1,)), ((), ())), preferre...  25.5 us
  transfers between devices with their start and end apart: 64, of which 42 were waited for; matrix products, arithmetic and copies ran while one was open for 15% of the time, Pallas kernels for 3%

profile of v1, /device:TPU:0, one launch (start us, length us, event | category | flops | bytes accessed | tf_op | source)
XLA Modules:
  0.0 773.1 jit_solution(11997896256791488020)
XLA Ops:
  23.1 80.1 %all-gather.4.cloned.1.call-done.refs_11_.refs_12_.refs_13_ = bf16[2048,2176]{1,0:T(8,128)(2,1)} async-done(((bf16[256,2176]{1,0:T(8,128)(2,1)}), bf16[2048,2176]{1,0:T(8,128)(2,1)}) %all-gather.4.cloned.1.call-update) | async-done | bytes 8912912 | tf_op jit(solution)/shard_map/all_gather | solution.py:417
  110.6 8.2 %project.1 = (bf16[512,2048]{1,0:T(8,128)(2,1)S(1)}, bf16[4,2,128,768]{3,2,1,0:T(8,128)(2,1)S(1)}) custom-call(bf16[128,2048]{1,0:T(8,128)(2,1)S(1)} %bitcast.88, bf16[128,2048]{1,0:T(8,128)(2,1)S(1)} %collective-permute-done.refs_1_, bf16[128,2048]{1,0:T(8,128)(2,1)S(1)} %collective-permute-done.1.refs_2_, ...), custom_call_target="tpu_custom_call" | custom-call | flops 3221225472 | bytes 10485760 | tf_op jit(solution)/shard_map/project/pallas_call | solution.py:164
  125.0 20.9 %collective-permute-done.4.refs_2_ = bf16[128,768]{1,0:T(8,128)(2,1)S(1)} collective-permute-done((bf16[128,768]{1,0:T(8,128)(2,1)S(1)}, bf16[128,768]{1,0:T(8,128)(2,1)S(1)}, u32[]{:S(2)}, u32[]{:S(2)}) %collective-permute-start.4) | collective-permute-done | bytes 196640 | tf_op jit(solution)/shard_map/ppermute | solution.py:29
  146.3 12.7 %collective-permute-done.5.refs_3_ = bf16[128,768]{1,0:T(8,128)(2,1)S(1)} collective-permute-done((bf16[128,768]{1,0:T(8,128)(2,1)}, bf16[128,768]{1,0:T(8,128)(2,1)S(1)}, u32[]{:S(2)}, u32[]{:S(2)}) %collective-permute-start.5) | collective-permute-done | bytes 196640 | tf_op jit(solution)/shard_map/ppermute | solution.py:29
  159.0 9.8 %collective-permute-done.7.refs_5_ = bf16[128,768]{1,0:T(8,128)(2,1)S(1)} collective-permute-done((bf16[128,768]{1,0:T(8,128)(2,1)S(1)}, bf16[128,768]{1,0:T(8,128)(2,1)S(1)}, u32[]{:S(2)}, u32[]{:S(2)}) %collective-permute-start.7) | collective-permute-done | bytes 196640 | tf_op jit(solution)/shard_map/ppermute | solution.py:29
  180.5 30.1 %collective-permute-start.11 = (bf16[128,256]{1,0:T(8,128)(2,1)S(1)}, bf16[128,256]{1,0:T(8,128)(2,1)S(1)}, u32[]{:S(2)}, u32[]{:S(2)}) collective-permute-start(bf16[128,256]{1,0:T(8,128)(2,1)S(1)} %get-tuple-element.187), channel_id=1, source_target_pairs={{0,8},{4,12},{8,0},{12,4},{16,24},{20,28},{24,16},{28,20},{1,9},{5... | collective-permute-start | bytes 196616 | tf_op jit(solution)/shard_map/ppermute | solution.py:29
  236.6 8.5 %collective-permute-done.17 = bf16[128,2048]{1,0:T(8,128)(2,1)S(1)} collective-permute-done((bf16[128,2048]{1,0:T(8,128)(2,1)S(1)}, bf16[128,2048]{1,0:T(8,128)(2,1)S(1)}, u32[]{:S(2)}, u32[]{:S(2)}) %collective-permute-start.17) | collective-permute-done | bytes 524320 | tf_op jit(solution)/shard_map/ppermute | solution.py:29
  247.6 9.7 %collective-permute-done.19 = bf16[128,2048]{1,0:T(8,128)(2,1)S(1)} collective-permute-done((bf16[128,2048]{1,0:T(8,128)(2,1)S(1)}, bf16[128,2048]{1,0:T(8,128)(2,1)S(1)}, u32[]{:S(2)}, u32[]{:S(2)}) %collective-permute-start.19) | collective-permute-done | bytes 524320 | tf_op jit(solution)/shard_map/ppermute | solution.py:29
  264.0 7.4 collective-permute-done.20
  272.8 9.1 %collective-permute-done.21 = bf16[128,2048]{1,0:T(8,128)(2,1)S(1)} collective-permute-done((bf16[128,2048]{1,0:T(8,128)(2,1)S(1)}, bf16[128,2048]{1,0:T(8,128)(2,1)S(1)}, u32[]{:S(2)}, u32[]{:S(2)}) %collective-permute-start.21) | collective-permute-done | bytes 524320 | tf_op jit(solution)/shard_map/ppermute | solution.py:29
  282.7 12.2 %fusion.36 = f32[512,2816]{1,0:T(8,128)} fusion(bf16[2048,2816]{1,0:T(8,128)(2,1)} %all-gather.6.cloned.1.call-done, bf16[128,2048]{1,0:T(8,128)(2,1)} %collective-permute-done.22, bf16[128,2048]{1,0:T(8,128)(2,1)} %copy-done.29, bf16[128,2048]{1,0:T(8,128)(2,1)} %copy-done.27, bf16[128,2048]{1,0:T(8,128)(2,1)} %copy-done.21), kind=kOutput, calls=%fused_computation.79 | convolution fusion | flops 5913968640 | bytes 19398656 | tf_op jit(solution)/shard_map/dot_general | solution.py:105
  304.6 13.2 %all-gather.8.cloned.1.call-done = bf16[1408,2048]{1,0:T(8,128)(2,1)} async-done(((bf16[1408,256]{1,0:T(8,128)(2,1)}), bf16[1408,2048]{1,0:T(8,128)(2,1)}) %all-gather.8.cloned.1.call-update) | async-done | bytes 5767184 | tf_op jit(solution)/shard_map/all_gather | solution.py:421
  317.7 9.5 %multiply_convert_fusion.1 = (bf16[512,1408]{1,0:T(8,128)(2,1)S(1)}, bf16[512,1408]{1,0:T(8,128)(2,1)S(1)}, bf16[512,1408]{1,0:T(8,128)(2,1)S(1)}) fusion(f32[512,2816]{1,0:T(8,128)} %fusion.36, bf16[1408,2048]{1,0:T(8,128)(2,1)} %all-gather.8.cloned.1.call-done, bf16[128,2048]{1,0:T(8,128)(2,1)} %collective-permute-done.28, ...), kind=kOutput, calls=%fused_computation.16 | convolution fusion | flops 2972712960 | bytes 17956864 | tf_op jit(solution)/shard_map/dot_general | solution.py:99
  351.0 10.3 %collective-permute-done.30 = bf16[128,2048]{1,0:T(8,128)(2,1)S(1)} collective-permute-done((bf16[128,2048]{1,0:T(8,128)(2,1)S(1)}, bf16[128,2048]{1,0:T(8,128)(2,1)S(1)}, u32[]{:S(2)}, u32[]{:S(2)}) %collective-permute-start.30) | collective-permute-done | bytes 524320 | tf_op jit(solution)/shard_map/ppermute | solution.py:29
  362.1 9.1 %collective-permute-done.23 = bf16[128,2048]{1,0:T(8,128)(2,1)S(1)} collective-permute-done((bf16[128,2048]{1,0:T(8,128)(2,1)S(1)}, bf16[128,2048]{1,0:T(8,128)(2,1)S(1)}, u32[]{:S(2)}, u32[]{:S(2)}) %collective-permute-start.23) | collective-permute-done | bytes 524320 | tf_op jit(solution)/shard_map/ppermute | solution.py:29
  371.2 11.7 %collective-permute-done.24 = bf16[128,2048]{1,0:T(8,128)(2,1)S(1)} collective-permute-done((bf16[128,2048]{1,0:T(8,128)(2,1)S(1)}, bf16[128,2048]{1,0:T(8,128)(2,1)S(1)}, u32[]{:S(2)}, u32[]{:S(2)}) %collective-permute-start.24) | collective-permute-done | bytes 524320 | tf_op jit(solution)/shard_map/ppermute | solution.py:29
  389.4 11.3 %collective-permute-done.32 = bf16[128,2048]{1,0:T(8,128)(2,1)S(1)} collective-permute-done((bf16[128,2048]{1,0:T(8,128)(2,1)S(1)}, bf16[128,2048]{1,0:T(8,128)(2,1)S(1)}, u32[]{:S(2)}, u32[]{:S(2)}) %collective-permute-start.32) | collective-permute-done | bytes 524320 | tf_op jit(solution)/shard_map/ppermute | solution.py:29
  400.7 10.6 %collective-permute-done.33 = bf16[128,2048]{1,0:T(8,128)(2,1)S(1)} collective-permute-done((bf16[128,2048]{1,0:T(8,128)(2,1)S(1)}, bf16[128,2048]{1,0:T(8,128)(2,1)S(1)}, u32[]{:S(2)}, u32[]{:S(2)}) %collective-permute-start.33) | collective-permute-done | bytes 524320 | tf_op jit(solution)/shard_map/ppermute | solution.py:29
  414.8 7.6 convolution_convert_fusion.1
  447.4 11.9 %attend_back.1 = (bf16[1024,768]{1,0:T(8,128)(2,1)}, f32[8,256]{1,0:T(8,128)S(1)}) custom-call(s32[1]{0:T(128)} %bitcast.1.me_ref, s32[1,1024]{1,0:T(1,128)S(1)} %constant_dynamic-slice_fusion.28.ids_row_ref, s32[1024,1]{1,0:T(8,128)S(1)} %copy.94.ids_col_ref, f32[1024,256]{1,0:T(8,128)S(1)} %get-tuple-element.192.cos_ref, ...), custom_call_target="tpu_custom_call" | custom-call | flops 5368709120 | bytes 4194304 | tf_op jit(solution)/shard_map/attend_back/pallas_call | solution.py:322
  471.8 16.6 %collective-permute-done.43.refs_2_ = bf16[128,768]{1,0:T(8,128)(2,1)S(1)} collective-permute-done((bf16[128,768]{1,0:T(8,128)(2,1)S(1)}, bf16[128,768]{1,0:T(8,128)(2,1)S(1)}, u32[]{:S(2)}, u32[]{:S(2)}) %collective-permute-start.43) | collective-permute-done | bytes 196640 | tf_op jit(solution)/shard_map/ppermute | solution.py:29
  490.0 7.4 collective-permute-done.44.refs_3_
  501.2 10.2 %collective-permute-done.47.refs_6_ = bf16[128,768]{1,0:T(8,128)(2,1)S(1)} collective-permute-done((bf16[128,768]{1,0:T(8,128)(2,1)S(1)}, bf16[128,768]{1,0:T(8,128)(2,1)S(1)}, u32[]{:S(2)}, u32[]{:S(2)}) %collective-permute-start.47) | collective-permute-done | bytes 196640 | tf_op jit(solution)/shard_map/ppermute | solution.py:29
  511.4 7.9 %collective-permute-done.48.refs_7_ = bf16[128,768]{1,0:T(8,128)(2,1)S(1)} collective-permute-done((bf16[128,768]{1,0:T(8,128)(2,1)S(1)}, bf16[128,768]{1,0:T(8,128)(2,1)S(1)}, u32[]{:S(2)}, u32[]{:S(2)}) %collective-permute-start.48) | collective-permute-done | bytes 196640 | tf_op jit(solution)/shard_map/ppermute | solution.py:29
  526.6 10.9 %convolution_convert_fusion = bf16[2048,2816]{1,0:T(8,128)(2,1)} fusion(bf16[512,1408]{1,0:T(8,128)(2,1)} %copy-done.34, bf16[512,1408]{1,0:T(8,128)(2,1)} %copy-done.33, bf16[128,2048]{1,0:T(8,128)(2,1)} %collective-permute-done.22, bf16[128,2048]{1,0:T(8,128)(2,1)} %copy-done.29, bf16[128,2048]{1,0:T(8,128)(2,1)S(1)} %copy-done.28, ...), kind=kOutput, calls=%fused_computation | convolution fusion | flops 5925502976 | bytes 16515072 | tf_op jit(solution)/shard_map/dot_general | solution.py:93
  537.5 6.7 fusion.2
  550.1 11.5 %collective-permute-done.49 = bf16[128,2048]{1,0:T(8,128)(2,1)S(1)} collective-permute-done((bf16[128,2048]{1,0:T(8,128)(2,1)}, bf16[128,2048]{1,0:T(8,128)(2,1)S(1)}, u32[]{:S(2)}, u32[]{:S(2)}) %collective-permute-start.49) | collective-permute-done | bytes 524320 | tf_op jit(solution)/shard_map/ppermute | solution.py:29
  561.9 10.9 %collective-permute-done.51 = bf16[128,2048]{1,0:T(8,128)(2,1)S(1)} collective-permute-done((bf16[128,2048]{1,0:T(8,128)(2,1)S(1)}, bf16[128,2048]{1,0:T(8,128)(2,1)S(1)}, u32[]{:S(2)}, u32[]{:S(2)}) %collective-permute-start.51) | collective-permute-done | bytes 524320 | tf_op jit(solution)/shard_map/ppermute | solution.py:29
  575.9 13.7 %collective-permute-start.53 = (f32[8,2048]{1,0:T(8,128)S(1)}, f32[8,2048]{1,0:T(8,128)S(1)}, u32[]{:S(2)}, u32[]{:S(2)}) collective-permute-start(f32[8,2048]{1,0:T(8,128)S(1)} %add.455), channel_id=1, source_target_pairs={{0,8},{4,12},{8,0},{12,4},{16,24},{20,28},{24,16},{28,20},{1,9},{5... | collective-permute-start | bytes 196616 | tf_op jit(solution)/shard_map/ppermute | solution.py:29
  596.0 9.4 %collective-permute-done.54 = f32[8,2048]{1,0:T(8,128)S(1)} collective-permute-done((f32[8,2048]{1,0:T(8,128)S(1)}, f32[8,2048]{1,0:T(8,128)S(1)}, u32[]{:S(2)}, u32[]{:S(2)}) %collective-permute-start.54) | collective-permute-done | bytes 65568 | tf_op jit(solution)/shard_map/ppermute | solution.py:29
  648.4 100.1 %reduce-scatter.9.cloned.1.call-done = bf16[256,2816]{1,0:T(8,128)(2,1)} async-done(((bf16[2048,2816]{1,0:T(8,128)(2,1)}), bf16[256,2816]{1,0:T(8,128)(2,1)}) %reduce-scatter.9.cloned.1.call-update) | async-done | bytes 1441808 | tf_op jit(solution)/shard_map/reduce_scatter | solution.py:487
  752.9 12.9 %multiply_subtract_fusion = (f32[256,2,1408]{2,1,0:T(2,128)}, f32[256,2,1408]{2,1,0:T(2,128)}, f32[256,2,1408]{2,1,0:T(2,128)}) fusion(f32[256,2,1408]{2,1,0:T(2,128)S(1)} %copy-done.11, f32[256,2,1408]{2,1,0:T(2,128)} %reshape.174, f32[256,2,1408]{2,1,0:T(2,128)} %param.28, f32[256,2,1408]{2,1,0:T(2,128)} %param.33), kind=kLoop, calls=%fused_computation.13 | loop fusion | flops 10813440 | bytes 20185088 | tf_op jit(solution)/shard_map/sub | solution.py:113
  (271 shorter events, 235.7 us)
Async XLA Ops:
  7.2 96.1 %all-gather.4.cloned.1.call-start = ((), (), s32[]{:S(2)}) async-start(), calls=%async_computation.4 | async-start | bytes 10027008 | tf_op jit(solution)/shard_map/all_gather | solution.py:417
  14.0 268.7 %all-gather.6.cloned.1.call-start = ((), (), s32[]{:S(2)}) async-start(), calls=%async_computation.5 | async-start | bytes 12976128 | tf_op jit(solution)/shard_map/all_gather | solution.py:418
  16.4 301.4 %all-gather.8.cloned.1.call-start = ((), (), s32[]{:S(2)}) async-start(), calls=%async_computation.6 | async-start | bytes 6488064 | tf_op jit(solution)/shard_map/all_gather | solution.py:421
  17.9 596.8 %reduce-scatter.7.cloned.1.call-start = ((), (), s32[]{:S(2)}) async-start(), calls=%async_computation.8 | async-start | bytes 2359296 | tf_op jit(solution)/shard_map/reduce_scatter | solution.py:496
  18.0 92.5 %collective-permute-start = (bf16[128,2048]{1,0:T(8,128)(2,1)S(1)}, bf16[128,2048]{1,0:T(8,128)(2,1)S(1)}, u32[]{:S(2)}, u32[]{:S(2)}) collective-permute-start(bf16[128,2048]{1,0:T(8,128)(2,1)S(1)} %bitcast.85), channel_id=1, source_target_pairs={{0,1},{1,0},{2,3},{3,2},{4,5},{5,4},{6,7},{7,6},{8,9},{9,8},{10,11... | collective-permute-start | bytes 1572872 | tf_op jit(solution)/shard_map/ppermute | solution.py:29
  21.0 89.5 %collective-permute-start.1 = (bf16[128,2048]{1,0:T(8,128)(2,1)S(1)}, bf16[128,2048]{1,0:T(8,128)(2,1)S(1)}, u32[]{:S(2)}, u32[]{:S(2)}) collective-permute-start(bf16[128,2048]{1,0:T(8,128)(2,1)S(1)} %bitcast.86), channel_id=1, source_target_pairs={{0,2},{1,3},{2,0},{3,1},{4,6},{5,7},{6,4},{7,5},{8,10},{9,11},{10,... | collective-permute-start | bytes 1572872 | tf_op jit(solution)/shard_map/ppermute | solution.py:29
  22.5 88.0 %collective-permute-start.2 = (bf16[128,2048]{1,0:T(8,128)(2,1)S(1)}, bf16[128,2048]{1,0:T(8,128)(2,1)S(1)}, u32[]{:S(2)}, u32[]{:S(2)}) collective-permute-start(bf16[128,2048]{1,0:T(8,128)(2,1)S(1)} %bitcast.87), channel_id=1, source_target_pairs={{0,3},{1,2},{2,1},{3,0},{4,7},{5,6},{6,5},{7,4},{8,11},{9,10},{10,... | collective-permute-start | bytes 1572872 | tf_op jit(solution)/shard_map/ppermute | solution.py:29
  120.5 25.4 %collective-permute-start.4 = (bf16[128,768]{1,0:T(8,128)(2,1)S(1)}, bf16[128,768]{1,0:T(8,128)(2,1)S(1)}, u32[]{:S(2)}, u32[]{:S(2)}) collective-permute-start(bf16[128,768]{1,0:T(8,128)(2,1)S(1)} %get-tuple-element.165), channel_id=1, source_target_pairs={{0,8},{4,12},{8,0},{12,4},{16,24},{20,28},{24,16},{28,20},{1,9},{5... | collective-permute-start | bytes 589832 | tf_op jit(solution)/shard_map/ppermute | solution.py:29
  120.5 38.5 %collective-permute-start.5 = (bf16[128,768]{1,0:T(8,128)(2,1)}, bf16[128,768]{1,0:T(8,128)(2,1)S(1)}, u32[]{:S(2)}, u32[]{:S(2)}) collective-permute-start(bf16[128,768]{1,0:T(8,128)(2,1)} %get-tuple-element.164), channel_id=1, source_target_pairs={{0,12},{4,8},{8,4},{12,0},{16,28},{20,24},{24,20},{28,16},{1,13},{... | collective-permute-start | bytes 589832 | tf_op jit(solution)/shard_map/ppermute | solution.py:29
  122.1 36.9 %collective-permute-start.6 = (bf16[128,768]{1,0:T(8,128)(2,1)}, bf16[128,768]{1,0:T(8,128)(2,1)S(1)}, u32[]{:S(2)}, u32[]{:S(2)}) collective-permute-start(bf16[128,768]{1,0:T(8,128)(2,1)} %get-tuple-element.163), channel_id=1, source_target_pairs={{0,16},{4,20},{8,24},{12,28},{16,0},{20,4},{24,8},{28,12},{1,17},{... | collective-permute-start | bytes 589832 | tf_op jit(solution)/shard_map/ppermute | solution.py:29
  122.7 46.1 %collective-permute-start.7 = (bf16[128,768]{1,0:T(8,128)(2,1)S(1)}, bf16[128,768]{1,0:T(8,128)(2,1)S(1)}, u32[]{:S(2)}, u32[]{:S(2)}) collective-permute-start(bf16[128,768]{1,0:T(8,128)(2,1)S(1)} %get-tuple-element.162), channel_id=1, source_target_pairs={{0,20},{4,16},{8,28},{12,24},{16,4},{20,0},{24,12},{28,8},{1,21},{... | collective-permute-start | bytes 589832 | tf_op jit(solution)/shard_map/ppermute | solution.py:29
  124.9 43.9 %collective-permute-start.8 = (bf16[128,768]{1,0:T(8,128)(2,1)S(1)}, bf16[128,768]{1,0:T(8,128)(2,1)S(1)}, u32[]{:S(2)}, u32[]{:S(2)}) collective-permute-start(bf16[128,768]{1,0:T(8,128)(2,1)S(1)} %get-tuple-element.161), channel_id=1, source_target_pairs={{0,24},{4,28},{8,16},{12,20},{16,8},{20,12},{24,0},{28,4},{1,25},{... | collective-permute-start | bytes 589832 | tf_op jit(solution)/shard_map/ppermute | solution.py:29
  145.9 28.0 %collective-permute-start.9 = (bf16[128,768]{1,0:T(8,128)(2,1)S(1)}, bf16[128,768]{1,0:T(8,128)(2,1)S(1)}, u32[]{:S(2)}, u32[]{:S(2)}) collective-permute-start(bf16[128,768]{1,0:T(8,128)(2,1)S(1)} %get-tuple-element.160), channel_id=1, source_target_pairs={{0,28},{4,24},{8,20},{12,16},{16,12},{20,8},{24,4},{28,0},{1,29},{... | collective-permute-start | bytes 589832 | tf_op jit(solution)/shard_map/ppermute | solution.py:29
  180.0 33.1 %collective-permute-start.10 = (bf16[128,256]{1,0:T(8,128)(2,1)S(1)}, bf16[128,256]{1,0:T(8,128)(2,1)S(1)}, u32[]{:S(2)}, u32[]{:S(2)}) collective-permute-start(bf16[128,256]{1,0:T(8,128)(2,1)S(1)} %get-tuple-element.188), channel_id=1, source_target_pairs={{0,4},{4,0},{8,12},{12,8},{16,20},{20,16},{24,28},{28,24},{1,5},{5... | collective-permute-start | bytes 196616 | tf_op jit(solution)/shard_map/ppermute | solution.py:29
  180.5 36.7 %collective-permute-start.11 = (bf16[128,256]{1,0:T(8,128)(2,1)S(1)}, bf16[128,256]{1,0:T(8,128)(2,1)S(1)}, u32[]{:S(2)}, u32[]{:S(2)}) collective-permute-start(bf16[128,256]{1,0:T(8,128)(2,1)S(1)} %get-tuple-element.187), channel_id=1, source_target_pairs={{0,8},{4,12},{8,0},{12,4},{16,24},{20,28},{24,16},{28,20},{1,9},{5... | collective-permute-start | bytes 196616 | tf_op jit(solution)/shard_map/ppermute | solution.py:29
  262.0 32.9 %collective-permute-start.26 = (bf16[128,2048]{1,0:T(8,128)(2,1)}, bf16[128,2048]{1,0:T(8,128)(2,1)}, u32[]{:S(2)}, u32[]{:S(2)}) collective-permute-start(bf16[128,2048]{1,0:T(8,128)(2,1)} %bitcast.16), channel_id=1, source_target_pairs={{0,1},{1,0},{2,3},{3,2},{4,5},{5,4},{6,7},{7,6},{8,9},{9,8},{10,11... | collective-permute-start | bytes 1572872 | tf_op jit(solution)/shard_map/ppermute | solution.py:29
  263.4 35.5 %collective-permute-start.27 = (bf16[128,2048]{1,0:T(8,128)(2,1)}, bf16[128,2048]{1,0:T(8,128)(2,1)}, u32[]{:S(2)}, u32[]{:S(2)}) collective-permute-start(bf16[128,2048]{1,0:T(8,128)(2,1)} %bitcast.16), channel_id=1, source_target_pairs={{0,2},{1,3},{2,0},{3,1},{4,6},{5,7},{6,4},{7,5},{8,10},{9,11},{10,... | collective-permute-start | bytes 1572872 | tf_op jit(solution)/shard_map/ppermute | solution.py:29
  271.4 33.2 %collective-permute-start.28 = (bf16[128,2048]{1,0:T(8,128)(2,1)}, bf16[128,2048]{1,0:T(8,128)(2,1)}, u32[]{:S(2)}, u32[]{:S(2)}) collective-permute-start(bf16[128,2048]{1,0:T(8,128)(2,1)} %bitcast.16), channel_id=1, source_target_pairs={{0,3},{1,2},{2,1},{3,0},{4,7},{5,6},{6,5},{7,4},{8,11},{9,10},{10,... | collective-permute-start | bytes 1572872 | tf_op jit(solution)/shard_map/ppermute | solution.py:29
  335.3 26.0 %collective-permute-start.30 = (bf16[128,2048]{1,0:T(8,128)(2,1)S(1)}, bf16[128,2048]{1,0:T(8,128)(2,1)S(1)}, u32[]{:S(2)}, u32[]{:S(2)}) collective-permute-start(bf16[128,2048]{1,0:T(8,128)(2,1)S(1)} %get-tuple-element.145), channel_id=1, source_target_pairs={{0,2},{1,3},{2,0},{3,1},{4,6},{5,7},{6,4},{7,5},{8,10},{9,11},{10,... | collective-permute-start | bytes 1572872 | tf_op jit(solution)/shard_map/ppermute | solution.py:29
  336.8 24.6 %collective-permute-start.31 = (bf16[128,2048]{1,0:T(8,128)(2,1)S(1)}, bf16[128,2048]{1,0:T(8,128)(2,1)S(1)}, u32[]{:S(2)}, u32[]{:S(2)}) collective-permute-start(bf16[128,2048]{1,0:T(8,128)(2,1)S(1)} %get-tuple-element.144), channel_id=1, source_target_pairs={{0,3},{1,2},{2,1},{3,0},{4,7},{5,6},{6,5},{7,4},{8,11},{9,10},{10,... | collective-permute-start | bytes 1572872 | tf_op jit(solution)/shard_map/ppermute | solution.py:29
  343.9 27.3 %collective-permute-start.23 = (bf16[128,2048]{1,0:T(8,128)(2,1)S(1)}, bf16[128,2048]{1,0:T(8,128)(2,1)S(1)}, u32[]{:S(2)}, u32[]{:S(2)}) collective-permute-start(bf16[128,2048]{1,0:T(8,128)(2,1)S(1)} %get-tuple-element.146), channel_id=1, source_target_pairs={{0,1},{1,0},{2,3},{3,2},{4,5},{5,4},{6,7},{7,6},{8,9},{9,8},{10,11... | collective-permute-start | bytes 1572872 | tf_op jit(solution)/shard_map/ppermute | solution.py:29
  345.4 37.4 %collective-permute-start.24 = (bf16[128,2048]{1,0:T(8,128)(2,1)S(1)}, bf16[128,2048]{1,0:T(8,128)(2,1)S(1)}, u32[]{:S(2)}, u32[]{:S(2)}) collective-permute-start(bf16[128,2048]{1,0:T(8,128)(2,1)S(1)} %get-tuple-element.148), channel_id=1, source_target_pairs={{0,2},{1,3},{2,0},{3,1},{4,6},{5,7},{6,4},{7,5},{8,10},{9,11},{10,... | collective-permute-start | bytes 1572872 | tf_op jit(solution)/shard_map/ppermute | solution.py:29
  348.6 34.2 %collective-permute-start.25 = (bf16[128,2048]{1,0:T(8,128)(2,1)S(1)}, bf16[128,2048]{1,0:T(8,128)(2,1)S(1)}, u32[]{:S(2)}, u32[]{:S(2)}) collective-permute-start(bf16[128,2048]{1,0:T(8,128)(2,1)S(1)} %get-tuple-element.147), channel_id=1, source_target_pairs={{0,3},{1,2},{2,1},{3,0},{4,7},{5,6},{6,5},{7,4},{8,11},{9,10},{10,... | collective-permute-start | bytes 1572872 | tf_op jit(solution)/shard_map/ppermute | solution.py:29
  414.8 202.6 %reduce-scatter.11.cloned.1.call-start = ((), (), s32[]{:S(2)}) async-start(), calls=%async_computation.10 | async-start | bytes 6488064 | tf_op jit(solution)/shard_map/reduce_scatter | solution.py:480
  422.5 206.1 %reduce-scatter.5.cloned.1.call-start = ((), (), s32[]{:S(2)}) async-start(), calls=%async_computation.7 | async-start | bytes 7077888 | tf_op jit(solution)/shard_map/reduce_scatter | solution.py:507
  461.7 26.8 %collective-permute-start.43 = (bf16[128,768]{1,0:T(8,128)(2,1)S(1)}, bf16[128,768]{1,0:T(8,128)(2,1)S(1)}, u32[]{:S(2)}, u32[]{:S(2)}) collective-permute-start(bf16[128,768]{1,0:T(8,128)(2,1)S(1)} %get-tuple-element.157), channel_id=1, source_target_pairs={{0,8},{4,12},{8,0},{12,4},{16,24},{20,28},{24,16},{28,20},{1,9},{5... | collective-permute-start | bytes 589832 | tf_op jit(solution)/shard_map/ppermute | solution.py:29
  467.7 29.8 %collective-permute-start.44 = (bf16[128,768]{1,0:T(8,128)(2,1)S(1)}, bf16[128,768]{1,0:T(8,128)(2,1)S(1)}, u32[]{:S(2)}, u32[]{:S(2)}) collective-permute-start(bf16[128,768]{1,0:T(8,128)(2,1)S(1)} %get-tuple-element.156), channel_id=1, source_target_pairs={{0,12},{4,8},{8,4},{12,0},{16,28},{20,24},{24,20},{28,16},{1,13},{... | collective-permute-start | bytes 589832 | tf_op jit(solution)/shard_map/ppermute | solution.py:29
  467.7 29.8 %collective-permute-start.45 = (bf16[128,768]{1,0:T(8,128)(2,1)S(1)}, bf16[128,768]{1,0:T(8,128)(2,1)S(1)}, u32[]{:S(2)}, u32[]{:S(2)}) collective-permute-start(bf16[128,768]{1,0:T(8,128)(2,1)S(1)} %get-tuple-element.155), channel_id=1, source_target_pairs={{0,16},{4,20},{8,24},{12,28},{16,0},{20,4},{24,8},{28,12},{1,17},{... | collective-permute-start | bytes 589832 | tf_op jit(solution)/shard_map/ppermute | solution.py:29
  469.1 32.1 %collective-permute-start.46 = (bf16[128,768]{1,0:T(8,128)(2,1)S(1)}, bf16[128,768]{1,0:T(8,128)(2,1)S(1)}, u32[]{:S(2)}, u32[]{:S(2)}) collective-permute-start(bf16[128,768]{1,0:T(8,128)(2,1)S(1)} %get-tuple-element.154), channel_id=1, source_target_pairs={{0,20},{4,16},{8,28},{12,24},{16,4},{20,0},{24,12},{28,8},{1,21},{... | collective-permute-start | bytes 589832 | tf_op jit(solution)/shard_map/ppermute | solution.py:29
  470.1 41.4 %collective-permute-start.47 = (bf16[128,768]{1,0:T(8,128)(2,1)S(1)}, bf16[128,768]{1,0:T(8,128)(2,1)S(1)}, u32[]{:S(2)}, u32[]{:S(2)}) collective-permute-start(bf16[128,768]{1,0:T(8,128)(2,1)S(1)} %get-tuple-element.153), channel_id=1, source_target_pairs={{0,24},{4,28},{8,16},{12,20},{16,8},{20,12},{24,0},{28,4},{1,25},{... | collective-permute-start | bytes 589832 | tf_op jit(solution)/shard_map/ppermute | solution.py:29
  488.4 30.9 %collective-permute-start.48 = (bf16[128,768]{1,0:T(8,128)(2,1)S(1)}, bf16[128,768]{1,0:T(8,128)(2,1)S(1)}, u32[]{:S(2)}, u32[]{:S(2)}) collective-permute-start(bf16[128,768]{1,0:T(8,128)(2,1)S(1)} %get-tuple-element.152), channel_id=1, source_target_pairs={{0,28},{4,24},{8,20},{12,16},{16,12},{20,8},{24,4},{28,0},{1,29},{... | collective-permute-start | bytes 589832 | tf_op jit(solution)/shard_map/ppermute | solution.py:29
  525.5 223.1 %reduce-scatter.9.cloned.1.call-start = ((), (), s32[]{:S(2)}) async-start(), calls=%async_computation.9 | async-start | bytes 12976128 | tf_op jit(solution)/shard_map/reduce_scatter | solution.py:487
  (67 other events, 989.8 us)
Sparse Core Ops, SparseCore 0:
  14.1 89.0 all-gather.3
  105.5 151.0 all-gather.5
  258.7 58.9 all-gather.7
  414.9 38.0 reduce-scatter.6
  455.2 93.5 reduce-scatter.10
  550.9 77.6 reduce-scatter.4
  630.9 117.6 reduce-scatter.8

commit v2 on v1

--- a/solution.py
+++ b/solution.py
@@ -6,6 +6,7 @@
 from jax.experimental import pallas as pl
 from jax.experimental.pallas import tpu as pltpu
 from jax.sharding import PartitionSpec as P
+
 
 HD = 64
 ROT = 16
@@ -118,7 +119,7 @@
     return pltpu.CompilerParams(vmem_limit_bytes=megabytes * 1024 * 1024)
 
 
-def project_kernel(count, groups, *refs):
+def project_kernel(count, *refs):
     blocks = refs[:count]
     gain, shift, bias_q, bias_v, cosine, from_right, from_left, wq, wk, wv = refs[count : count + 10]
     normed_ref, out_ref = refs[count + 10 :]
@@ -162,7 +163,7 @@
     specs += [whole(table) for table in tables]
     specs += [column(0), column(1), column(2)]
     return pl.pallas_call(
-        functools.partial(project_kernel, count, groups),
+        functools.partial(project_kernel, count),
         grid=(groups,),
         in_specs=specs,
         out_specs=[
@@ -342,6 +343,68 @@
     )(me, ids_row, ids_col, *tables, *pieces, att, everything, lse)
 
 
+def pack_kernel(qkv_ref, out_ref, vec_ref, packed_ref):
+    head_cols = qkv_ref.shape[2]
+    for which in range(3):
+        packed_ref[:, which * head_cols : (which + 1) * head_cols] = qkv_ref[which].astype(BF16)
+    packed_ref[:, 3 * head_cols : 4 * head_cols] = out_ref[...].T.astype(BF16)
+    vectors = vec_ref[...]
+    padding = jnp.zeros((vectors.shape[0], 128 - vectors.shape[1]), F32)
+    packed_ref[:, 4 * head_cols :] = jnp.concatenate([vectors, padding], axis=1).astype(BF16)
+
+
+def pack(w_qkv, w_out, norm_vecs):
+    _, rows, head_cols = w_qkv.shape
+    vmem = pl.BlockSpec(memory_space=pltpu.VMEM)
+    return pl.pallas_call(
+        pack_kernel,
+        in_specs=[vmem] * 3,
+        out_specs=vmem,
+        out_shape=jax.ShapeDtypeStruct((rows, 4 * head_cols + 128), BF16),
+        compiler_params=kernel_params(),
+        name="pack",
+    )(w_qkv, w_out, norm_vecs)
+
+
+def adam_kernel(leading, share_ref, master_ref, first_ref, second_ref, *outs):
+    parts = master_ref.shape[0 if leading else 1]
+    cols = master_ref.shape[2]
+    for part in range(parts):
+        spot = (part,) if leading else (slice(None), part)
+        gradient = share_ref[:, part * cols : (part + 1) * cols].astype(F32)
+        updates = adam_step(
+            master_ref[spot], gradient, first_ref[spot], second_ref[spot], weight_decay
+        )
+        for out_ref, value in zip(outs, (gradient, *updates)):
+            out_ref[spot] = value
+
+
+def adam_parts(leading, share, *arrays):
+    shape = arrays[0].shape
+    rows, width = share.shape
+    step_rows = max(
+        size
+        for size in range(16, rows + 1, 16)
+        if rows % size == 0 and (size == 16 or size * width <= 100000)
+    )
+    if leading:
+        block = pl.BlockSpec((shape[0], step_rows, shape[2]), lambda step: (0, step, 0))
+    else:
+        block = pl.BlockSpec((step_rows, shape[1], shape[2]), lambda step: (step, 0, 0))
+    return pl.pallas_call(
+        functools.partial(adam_kernel, leading),
+        grid=(rows // step_rows,),
+        in_specs=[pl.BlockSpec((step_rows, width), lambda step: (step, 0))] + [block] * 3,
+        out_specs=[block] * 4,
+        out_shape=[jax.ShapeDtypeStruct(shape, F32)] * 4,
+        compiler_params=kernel_params(),
+        cost_estimate=pl.CostEstimate(
+            flops=0, bytes_accessed=30 * rows * width, transcendentals=0
+        ),
+        name="adam",
+    )(share, *arrays)
+
+
 def place_kernel(count, groups, parts, me_ref, *refs):
     pieces = refs[:count]
     out_ref = refs[count]
@@ -410,14 +473,10 @@
     ctx_scalar = ctx_place.astype(jnp.int32).reshape(1)
     places = jnp.stack([ctx_place, shard_place]).astype(jnp.int32)
 
-    vec_cols = jnp.pad(norm_vecs.astype(BF16), ((0, 0), (0, 128 - norm_vecs.shape[1])))
-    first_weights = jnp.concatenate(
-        [w_qkv.astype(BF16).reshape(own_rows, 3 * head_cols), w_out.astype(BF16).T, vec_cols], axis=1
-    )
+    first_weights = pack(w_qkv.transpose(1, 0, 2), w_out, norm_vecs)
     first_all = lax.all_gather(first_weights, "ctx", axis=0, tiled=True)
-    gu_flat = lax.all_gather(
-        w_gu.astype(BF16).reshape(own_rows, 2 * unit_cols), "ctx", axis=0, tiled=True
-    )
+    gu_part = w_gu.astype(BF16).reshape(own_rows, 2 * unit_cols)
+    gu_flat = lax.all_gather(gu_part, "ctx", axis=0, tiled=True)
     down_weight = lax.all_gather(w_down.astype(BF16), "ctx", axis=1, tiled=True)
 
     hidden_blocks = gather_rows(hidden[0], "wsh")
@@ -473,18 +532,20 @@
     gathered_two = jnp.concatenate(gather_rows(normed_two.astype(BF16), "wsh"), axis=0)
     gate_up = dot(gathered_two, gu_flat)
     gate_part = gate_up[:, :unit_cols]
+    activated = (gate_part * jax.nn.sigmoid(gate_part) * gate_up[:, unit_cols:]).astype(BF16)
+    grad_down = dot_rows(activated, cot_all).astype(BF16)
+    share_down = lax.psum_scatter(grad_down, "ctx", scatter_dimension=1, tiled=True)
+
+    gate_up = lax.optimization_barrier(gate_up)
+    gate_part = gate_up[:, :unit_cols]
     up_part = gate_up[:, unit_cols:]
     sigmoid_gate = jax.nn.sigmoid(gate_part)
-    activated = (gate_part * sigmoid_gate * up_part).astype(BF16)
-    grad_down = dot_rows(activated, cot_all).astype(BF16)
-    share_down = lax.psum_scatter(grad_down, "ctx", scatter_dimension=1, tiled=True).astype(F32)
-
     grad_act = dot_back(cot_all, down_weight)
     grad_gate = grad_act * up_part * sigmoid_gate * (1.0 + gate_part * (1.0 - sigmoid_gate))
     grad_up = grad_act * gate_part * sigmoid_gate
     grad_gate_up = jnp.concatenate([grad_gate, grad_up], axis=1).astype(BF16)
     grad_gu = dot_rows(gathered_two, grad_gate_up).astype(BF16)
-    share_gu = lax.psum_scatter(grad_gu, "ctx", scatter_dimension=0, tiled=True).astype(F32)
+    share_gu = lax.psum_scatter(grad_gu, "ctx", scatter_dimension=0, tiled=True)
     normed_two_terms = dot_back(grad_gate_up, gu_flat).astype(BF16)
     grad_normed_two = scatter_sum(row_blocks(normed_two_terms), "wsh")
     grad_middle, grad_gain_two, grad_shift_two = norm_back(
@@ -493,7 +554,7 @@
     grad_middle = grad_middle + cotangent[0].astype(F32)
     middle_all = jnp.concatenate(gather_rows(grad_middle.astype(BF16), "wsh"), axis=0)
     grad_out = dot_rows(attended, middle_all).astype(BF16)
-    share_out = lax.psum_scatter(grad_out, "ctx", scatter_dimension=1, tiled=True).astype(F32)
+    share_out = lax.psum_scatter(grad_out, "ctx", scatter_dimension=1, tiled=True)
     grad_att = dot(middle_all, out_turned).astype(BF16)
     grad_att = grad_att.reshape(shard_count, tok_rows, groups, width).transpose(0, 2, 1, 3)
     grad_pieces = [exchange_out(grad_att, bits) for bits in range(ctx_size)]
@@ -504,7 +565,7 @@
         places, [exchange_back(grad_own, bits) for bits in range(ctx_size)], groups, 3
     )
     grad_qkv = dot_rows(gathered_one, grad_rows).astype(BF16)
-    share_qkv = lax.psum_scatter(grad_qkv, "ctx", scatter_dimension=0, tiled=True).astype(F32)
+    share_qkv = lax.psum_scatter(grad_qkv, "ctx", scatter_dimension=0, tiled=True)
 
     ffn_terms = dot(activated, down_weight).astype(BF16)
     block_out = (middle + scatter_sum(row_blocks(ffn_terms), "wsh")).astype(BF16)
@@ -535,20 +596,25 @@
     vec_sums = butterfly(butterfly(vec_terms, "ctx"), "wsh")
     share_vecs = lax.dynamic_slice_in_dim(vec_sums, ctx_place * own_rows, own_rows, 1).T[:, :6]
 
-    share_qkv = share_qkv.reshape(w_qkv.shape)
-    share_gu = share_gu.reshape(w_gu.shape)
-    new_qkv, new_first_qkv, new_second_qkv = adam_step(
-        w_qkv, share_qkv, first_qkv, second_qkv, weight_decay
-    )
-    new_out, new_first_out, new_second_out = adam_step(
-        w_out, share_out, first_out, second_out, weight_decay
-    )
-    new_gu, new_first_gu, new_second_gu = adam_step(
-        w_gu, share_gu, first_gu, second_gu, weight_decay
-    )
-    new_down, new_first_down, new_second_down = adam_step(
-        w_down, share_down, first_down, second_down, weight_decay
-    )
+    share_qkv, new_qkv, new_first_qkv, new_second_qkv = [
+        array.transpose(1, 0, 2)
+        for array in adam_parts(
+            True,
+            share_qkv,
+            *[array.transpose(1, 0, 2) for array in (w_qkv, first_qkv, second_qkv)],
+        )
+    ]
+    share_gu, new_gu, new_first_gu, new_second_gu = adam_parts(
+        False, share_gu, w_gu, first_gu, second_gu
+    )
+    share_down, new_down, new_first_down, new_second_down = [
+        array[0]
+        for array in adam_parts(True, share_down, w_down[None], first_down[None], second_down[None])
+    ]
+    share_out, new_out, new_first_out, new_second_out = [
+        array[0]
+        for array in adam_parts(True, share_out, w_out[None], first_out[None], second_out[None])
+    ]
     new_vecs, new_first_vecs, new_second_vecs = adam_step(
         norm_vecs, share_vecs, first_vecs, second_vecs, 0.0
     )

time: 781 us -> 781 us (level)
  Pallas kernels: 26.4 us -> 47.6 us
  other arithmetic: 45.8 us -> 26.6 us
  waiting for transfers between devices: 457 us -> 445 us
  local copies, waits for them, and re-layouts: 48.3 us -> 58.7 us
    sub x5 -> x1, other arithmetic: 27.4 us -> 1.36 us  [adam_step(): master - learn_rate * (corrected / (spread + adam_epsilon) + decay_rate *...]
    pallas_call x1 -> x6, Pallas kernels: 8.23 us -> 27.9 us  [the longest x4 19.4 us: adam_parts(): pl.pallas_call(functools.partial(adam_kernel, leading), grid=(rows // ste...]
    all_gather x1, waiting for transfers between devices: 13.2 us -> 0.01 us  [local(): down_weight = lax.all_gather(w_down.astype(BF16), 'ctx', axis=1, tiled=True)]
    reshape x3 -> x0, local copies, waits for them, and re-layouts: 8.03 us -> none  [the longest x1 4.33 us: local(): share_gu = share_gu.reshape(w_gu.shape)]
    unnamed x87 -> x142, local copies, waits for them, and re-layouts: 28.4 us -> 36.3 us
  transfers between devices with their start and end apart: 64 -> 64, of which waited for: 42 -> 36; matrix products, arithmetic and copies ran while one was open for 15% -> 13% of each run, Pallas kernels for 3% -> 5%
where the time goes in v2:
time: 781 us; the launch traced here: 773 us
  waiting for transfers between devices  445 us (57%)
  starting transfers between devices  106 us (14%)
  matrix products  74.6 us (10%)
  local copies, waits for them, and re-layouts  58.7 us (8%)
  Pallas kernels  47.6 us (6%)
  other arithmetic  26.6 us (3%)
  between operations  15.2 us (2%)
    ppermute x57, waiting for transfers between devices, swapped(): lax.ppermute(value, axis, [(source, source ^ bits) for source in range(co...  261 us
    reduce_scatter x1, waiting for transfers between devices, local(): share_gu = lax.psum_scatter(grad_gu, 'ctx', scatter_dimension=0, tiled=True)  106 us
    ppermute x57, starting transfers between devices, swapped(): lax.ppermute(value, axis, [(source, source ^ bits) for source in range(co...  106 us
    all_gather x1, waiting for transfers between devices, local(): first_all = lax.all_gather(first_weights, 'ctx', axis=0, tiled=True)  78 us
    unnamed x142, local copies, waits for them, and re-layouts  36.3 us
    dot_general x4, matrix products, dot_back(): lax.dot_general(left_side, right_side, (((1,), (1,)), ((), ())), preferre...  29.1 us
    dot_general x4, matrix products, dot_rows(): lax.dot_general(left_side, right_side, (((0,), (0,)), ((), ())), preferre...  26.8 us
    pallas_call x4, Pallas kernels, adam_parts(): pl.pallas_call(functools.partial(adam_kernel, leading), grid=(rows // ste...  19.4 us
  transfers between devices with their start and end apart: 64, of which 36 were waited for; matrix products, arithmetic and copies ran while one was open for 13% of the time, Pallas kernels for 5%

profile of v2, /device:TPU:0, one launch (start us, length us, event | category | flops | bytes accessed | tf_op | source)
XLA Modules:
  0.0 773.3 jit_solution(2747121328322302721)
XLA Ops:
  23.2 78.0 %all-gather.4.cloned.1.call-done.refs_11_.refs_12_.refs_13_ = bf16[2048,2176]{1,0:T(8,128)(2,1)} async-done(((bf16[256,2176]{1,0:T(8,128)(2,1)}), bf16[2048,2176]{1,0:T(8,128)(2,1)}) %all-gather.4.cloned.1.call-update) | async-done | bytes 8912912 | tf_op jit(solution)/shard_map/all_gather | solution.py:477
  118.9 8.3 %project.1 = (bf16[512,2048]{1,0:T(8,128)(2,1)S(1)}, bf16[4,2,128,768]{3,2,1,0:T(8,128)(2,1)S(1)}) custom-call(bf16[128,2048]{1,0:T(8,128)(2,1)S(1)} %bitcast.104, bf16[128,2048]{1,0:T(8,128)(2,1)} %collective-permute-done.refs_1_, bf16[128,2048]{1,0:T(8,128)(2,1)} %collective-permute-done.1.refs_2_, bf16[128,2048]{1,0:T(8,128)(2,1)} %collective-permute-done.2.refs_3_, ...), custom_call_target="tpu_custom_call" | custom-call | flops 3221225472 | bytes 10485760 | tf_op jit(solution)/shard_map/project/pallas_call | solution.py:165
  134.1 21.6 %collective-permute-done.4.refs_2_ = bf16[128,768]{1,0:T(8,128)(2,1)} collective-permute-done((bf16[128,768]{1,0:T(8,128)(2,1)}, bf16[128,768]{1,0:T(8,128)(2,1)}, u32[]{:S(2)}, u32[]{:S(2)}) %collective-permute-start.4) | collective-permute-done | bytes 196640 | tf_op jit(solution)/shard_map/ppermute | solution.py:30
  157.4 7.9 %collective-permute-done.5.refs_3_ = bf16[128,768]{1,0:T(8,128)(2,1)} collective-permute-done((bf16[128,768]{1,0:T(8,128)(2,1)}, bf16[128,768]{1,0:T(8,128)(2,1)}, u32[]{:S(2)}, u32[]{:S(2)}) %collective-permute-start.5) | collective-permute-done | bytes 196640 | tf_op jit(solution)/shard_map/ppermute | solution.py:30
  175.5 7.7 collective-permute-done.9.refs_7_
  193.2 26.6 %collective-permute-start.11 = (bf16[128,256]{1,0:T(8,128)(2,1)S(1)}, bf16[128,256]{1,0:T(8,128)(2,1)S(1)}, u32[]{:S(2)}, u32[]{:S(2)}) collective-permute-start(bf16[128,256]{1,0:T(8,128)(2,1)S(1)} %get-tuple-element.138), channel_id=1, source_target_pairs={{0,8},{4,12},{8,0},{12,4},{16,24},{20,28},{24,16},{28,20},{1,9},{5... | collective-permute-start | bytes 196616 | tf_op jit(solution)/shard_map/ppermute | solution.py:30
  230.1 8.2 %collective-permute-done.14.refs_5_ = bf16[128,256]{1,0:T(8,128)(2,1)S(1)} collective-permute-done((bf16[128,256]{1,0:T(8,128)(2,1)S(1)}, bf16[128,256]{1,0:T(8,128)(2,1)S(1)}, u32[]{:S(2)}, u32[]{:S(2)}) %collective-permute-start.14) | collective-permute-done | bytes 65568 | tf_op jit(solution)/shard_map/ppermute | solution.py:30
  246.0 10.9 %collective-permute-done.17 = bf16[128,2048]{1,0:T(8,128)(2,1)S(1)} collective-permute-done((bf16[128,2048]{1,0:T(8,128)(2,1)S(1)}, bf16[128,2048]{1,0:T(8,128)(2,1)S(1)}, u32[]{:S(2)}, u32[]{:S(2)}) %collective-permute-start.17) | collective-permute-done | bytes 524320 | tf_op jit(solution)/shard_map/ppermute | solution.py:30
  256.8 12.9 %collective-permute-done.18 = bf16[128,2048]{1,0:T(8,128)(2,1)S(1)} collective-permute-done((bf16[128,2048]{1,0:T(8,128)(2,1)S(1)}, bf16[128,2048]{1,0:T(8,128)(2,1)S(1)}, u32[]{:S(2)}, u32[]{:S(2)}) %collective-permute-start.18) | collective-permute-done | bytes 524320 | tf_op jit(solution)/shard_map/ppermute | solution.py:30
  277.2 9.3 %collective-permute-done.20 = bf16[128,2048]{1,0:T(8,128)(2,1)S(1)} collective-permute-done((bf16[128,2048]{1,0:T(8,128)(2,1)S(1)}, bf16[128,2048]{1,0:T(8,128)(2,1)S(1)}, u32[]{:S(2)}, u32[]{:S(2)}) %collective-permute-start.20) | collective-permute-done | bytes 524320 | tf_op jit(solution)/shard_map/ppermute | solution.py:30
  287.9 10.0 %collective-permute-done.21 = bf16[128,2048]{1,0:T(8,128)(2,1)S(1)} collective-permute-done((bf16[128,2048]{1,0:T(8,128)(2,1)S(1)}, bf16[128,2048]{1,0:T(8,128)(2,1)S(1)}, u32[]{:S(2)}, u32[]{:S(2)}) %collective-permute-start.21) | collective-permute-done | bytes 524320 | tf_op jit(solution)/shard_map/ppermute | solution.py:30
  298.8 10.7 %fusion.34 = f32[512,2816]{1,0:T(8,128)S(1)} fusion(bf16[2048,2816]{1,0:T(8,128)(2,1)} %all-gather.6.cloned.1.call-done, bf16[128,2048]{1,0:T(8,128)(2,1)} %collective-permute-done.22, bf16[128,2048]{1,0:T(8,128)(2,1)} %copy-done.58, bf16[128,2048]{1,0:T(8,128)(2,1)} %copy-done.57, bf16[128,2048]{1,0:T(8,128)(2,1)} %copy-done.45), kind=kOutput, calls=%fused_computation.64 | convolution fusion | flops 5913968640 | bytes 19398656 | tf_op jit(solution)/shard_map/dot_general | solution.py:106
  312.5 8.0 %collective-permute-done.28 = bf16[128,2048]{1,0:T(8,128)(2,1)} collective-permute-done((bf16[128,2048]{1,0:T(8,128)(2,1)}, bf16[128,2048]{1,0:T(8,128)(2,1)}, u32[]{:S(2)}, u32[]{:S(2)}) %collective-permute-start.28) | collective-permute-done | bytes 524320 | tf_op jit(solution)/shard_map/ppermute | solution.py:30
  320.5 9.2 %fusion.7 = (bf16[512,1408]{1,0:T(8,128)(2,1)S(1)}, bf16[512,1408]{1,0:T(8,128)(2,1)S(1)}) fusion(f32[512,2816]{1,0:T(8,128)} %copy-done.41, bf16[1408,2048]{1,0:T(8,128)(2,1)} %all-gather.8.cloned.1.call-done, bf16[128,2048]{1,0:T(8,128)(2,1)} %collective-permute-done.28, bf16[128,2048]{1,0:T(8,128)(2,1)} %collective-permute-done.27, ...), kind=kOutput, calls=%fused_computation.13 | convolution fusion | flops 2970550272 | bytes 16515072 | tf_op jit(solution)/shard_map/dot_general | solution.py:100
  329.8 10.1 %convolution_convert_fusion.4 = bf16[512,2048]{1,0:T(8,128)(2,1)S(1)} fusion(bf16[2048,2816]{1,0:T(8,128)(2,1)} %all-gather.6.cloned.1.call-done, bf16[512,1408]{1,0:T(8,128)(2,1)S(1)} %get-tuple-element.90, bf16[512,1408]{1,0:T(8,128)(2,1)S(1)} %get-tuple-element.89), kind=kOutput, calls=%fused_computation.7 | convolution fusion | flops 5912395776 | bytes 16515072 | tf_op jit(solution)/shard_map/dot_general | solution.py:100
  356.6 10.3 %collective-permute-done.30 = bf16[128,2048]{1,0:T(8,128)(2,1)S(1)} collective-permute-done((bf16[128,2048]{1,0:T(8,128)(2,1)S(1)}, bf16[128,2048]{1,0:T(8,128)(2,1)S(1)}, u32[]{:S(2)}, u32[]{:S(2)}) %collective-permute-start.30) | collective-permute-done | bytes 524320 | tf_op jit(solution)/shard_map/ppermute | solution.py:30
  367.7 9.7 %collective-permute-done.23 = bf16[128,2048]{1,0:T(8,128)(2,1)S(1)} collective-permute-done((bf16[128,2048]{1,0:T(8,128)(2,1)S(1)}, bf16[128,2048]{1,0:T(8,128)(2,1)S(1)}, u32[]{:S(2)}, u32[]{:S(2)}) %collective-permute-start.23) | collective-permute-done | bytes 524320 | tf_op jit(solution)/shard_map/ppermute | solution.py:30
  377.4 9.9 %collective-permute-done.24 = bf16[128,2048]{1,0:T(8,128)(2,1)S(1)} collective-permute-done((bf16[128,2048]{1,0:T(8,128)(2,1)S(1)}, bf16[128,2048]{1,0:T(8,128)(2,1)S(1)}, u32[]{:S(2)}, u32[]{:S(2)}) %collective-permute-start.24) | collective-permute-done | bytes 524320 | tf_op jit(solution)/shard_map/ppermute | solution.py:30
  394.0 11.3 %collective-permute-done.32 = bf16[128,2048]{1,0:T(8,128)(2,1)S(1)} collective-permute-done((bf16[128,2048]{1,0:T(8,128)(2,1)S(1)}, bf16[128,2048]{1,0:T(8,128)(2,1)S(1)}, u32[]{:S(2)}, u32[]{:S(2)}) %collective-permute-start.32) | collective-permute-done | bytes 524320 | tf_op jit(solution)/shard_map/ppermute | solution.py:30
  405.3 7.7 collective-permute-done.33
  418.2 7.6 convolution_convert_fusion.1
  456.4 11.9 %attend_back.1 = (bf16[1024,768]{1,0:T(8,128)(2,1)}, f32[8,256]{1,0:T(8,128)S(1)}) custom-call(s32[1]{0:T(128)} %bitcast.1.me_ref, s32[1,1024]{1,0:T(1,128)S(1)} %constant_dynamic-slice_fusion.28.ids_row_ref, s32[1024,1]{1,0:T(8,128)S(1)} %copy-done.23, f32[1024,256]{1,0:T(8,128)S(1)} %get-tuple-element.143.cos_ref, ...), custom_call_target="tpu_custom_call" | custom-call | flops 5368709120 | bytes 4194304 | tf_op jit(solution)/shard_map/attend_back/pallas_call | solution.py:323
  479.9 17.1 %collective-permute-done.43.refs_2_ = bf16[128,768]{1,0:T(8,128)(2,1)S(1)} collective-permute-done((bf16[128,768]{1,0:T(8,128)(2,1)S(1)}, bf16[128,768]{1,0:T(8,128)(2,1)S(1)}, u32[]{:S(2)}, u32[]{:S(2)}) %collective-permute-start.43) | collective-permute-done | bytes 196640 | tf_op jit(solution)/shard_map/ppermute | solution.py:30
  498.6 7.3 collective-permute-done.44.refs_3_
  509.0 11.2 %collective-permute-done.47.refs_6_ = bf16[128,768]{1,0:T(8,128)(2,1)S(1)} collective-permute-done((bf16[128,768]{1,0:T(8,128)(2,1)S(1)}, bf16[128,768]{1,0:T(8,128)(2,1)S(1)}, u32[]{:S(2)}, u32[]{:S(2)}) %collective-permute-start.47) | collective-permute-done | bytes 196640 | tf_op jit(solution)/shard_map/ppermute | solution.py:30
  520.2 7.9 %collective-permute-done.48.refs_7_ = bf16[128,768]{1,0:T(8,128)(2,1)S(1)} collective-permute-done((bf16[128,768]{1,0:T(8,128)(2,1)S(1)}, bf16[128,768]{1,0:T(8,128)(2,1)S(1)}, u32[]{:S(2)}, u32[]{:S(2)}) %collective-permute-start.48) | collective-permute-done | bytes 196640 | tf_op jit(solution)/shard_map/ppermute | solution.py:30
  535.4 11.2 %convolution_convert_fusion = bf16[2048,2816]{1,0:T(8,128)(2,1)} fusion(bf16[512,1408]{1,0:T(8,128)(2,1)} %copy-done.63, bf16[512,1408]{1,0:T(8,128)(2,1)} %copy-done.62, bf16[128,2048]{1,0:T(8,128)(2,1)} %collective-permute-done.22, bf16[128,2048]{1,0:T(8,128)(2,1)} %copy-done.58, bf16[128,2048]{1,0:T(8,128)(2,1)} %copy-done.57, bf16[128,2048]{1,0:T(8,128)(2,1)} %copy-done.45), kind=kOutput, calls=%fused_computation | convolution fusion | flops 5925502976 | bytes 16515072 | tf_op jit(solution)/shard_map/dot_general | solution.py:94
  559.3 11.6 %collective-permute-done.49 = bf16[128,2048]{1,0:T(8,128)(2,1)} collective-permute-done((bf16[128,2048]{1,0:T(8,128)(2,1)}, bf16[128,2048]{1,0:T(8,128)(2,1)}, u32[]{:S(2)}, u32[]{:S(2)}) %collective-permute-start.49) | collective-permute-done | bytes 524320 | tf_op jit(solution)/shard_map/ppermute | solution.py:30
  570.9 12.3 %collective-permute-done.50 = bf16[128,2048]{1,0:T(8,128)(2,1)} collective-permute-done((bf16[128,2048]{1,0:T(8,128)(2,1)}, bf16[128,2048]{1,0:T(8,128)(2,1)}, u32[]{:S(2)}, u32[]{:S(2)}) %collective-permute-start.50) | collective-permute-done | bytes 524320 | tf_op jit(solution)/shard_map/ppermute | solution.py:30
  588.3 11.4 %collective-permute-start.53 = (f32[8,2048]{1,0:T(8,128)S(1)}, f32[8,2048]{1,0:T(8,128)S(1)}, u32[]{:S(2)}, u32[]{:S(2)}) collective-permute-start(f32[8,2048]{1,0:T(8,128)S(1)} %add.397), channel_id=1, source_target_pairs={{0,8},{4,12},{8,0},{12,4},{16,24},{20,28},{24,16},{28,20},{1,9},{5... | collective-permute-start | bytes 196616 | tf_op jit(solution)/shard_map/ppermute | solution.py:30
  648.2 105.8 %reduce-scatter.9.cloned.1.call-done.share_ref = bf16[256,2816]{1,0:T(8,128)(2,1)} async-done(((bf16[2048,2816]{1,0:T(8,128)(2,1)}), bf16[256,2816]{1,0:T(8,128)(2,1)}) %reduce-scatter.9.cloned.1.call-update) | async-done | bytes 1441808 | tf_op jit(solution)/shard_map/reduce_scatter | solution.py:548
  755.3 10.7 %adam.6 = (f32[256,2,1408]{2,1,0:T(2,128)}, f32[256,2,1408]{2,1,0:T(2,128)}, f32[256,2,1408]{2,1,0:T(2,128)}, f32[256,2,1408]{2,1,0:T(2,128)}) custom-call(bf16[256,2816]{1,0:T(8,128)(2,1)S(1)} %copy-done.13, f32[256,2,1408]{2,1,0:T(2,128)S(1)} %copy-done.3, f32[256,2,1408]{2,1,0:T(2,128)} %first_ref.1, f32[256,2,1408]{2,1,0:T(2,128)} %second_ref.1), custom_call_target="tpu_custom_call" | custom-call | bytes 21626880 | tf_op jit(solution)/shard_map/adam/pallas_call | solution.py:394
  (322 shorter events, 243.7 us)
Async XLA Ops:
  7.2 93.9 %all-gather.4.cloned.1.call-start = ((), (), s32[]{:S(2)}) async-start(), calls=%async_computation.4 | async-start | bytes 10027008 | tf_op jit(solution)/shard_map/all_gather | solution.py:477
  11.9 286.9 %all-gather.6.cloned.1.call-start = ((), (), s32[]{:S(2)}) async-start(), calls=%async_computation.5 | async-start | bytes 12976128 | tf_op jit(solution)/shard_map/all_gather | solution.py:479
  14.2 306.3 %all-gather.8.cloned.1.call-start = ((), (), s32[]{:S(2)}) async-start(), calls=%async_computation.6 | async-start | bytes 6488064 | tf_op jit(solution)/shard_map/all_gather | solution.py:480
  16.6 607.7 %reduce-scatter.7.cloned.1.call-start = ((), (), s32[]{:S(2)}) async-start(), calls=%async_computation.8 | async-start | bytes 2359296 | tf_op jit(solution)/shard_map/reduce_scatter | solution.py:557
  16.7 97.6 %collective-permute-start = (bf16[128,2048]{1,0:T(8,128)(2,1)S(1)}, bf16[128,2048]{1,0:T(8,128)(2,1)}, u32[]{:S(2)}, u32[]{:S(2)}) collective-permute-start(bf16[128,2048]{1,0:T(8,128)(2,1)S(1)} %bitcast.101), channel_id=1, source_target_pairs={{0,1},{1,0},{2,3},{3,2},{4,5},{5,4},{6,7},{7,6},{8,9},{9,8},{10,11... | collective-permute-start | bytes 1572872 | tf_op jit(solution)/shard_map/ppermute | solution.py:30
  19.7 94.5 %collective-permute-start.1 = (bf16[128,2048]{1,0:T(8,128)(2,1)S(1)}, bf16[128,2048]{1,0:T(8,128)(2,1)}, u32[]{:S(2)}, u32[]{:S(2)}) collective-permute-start(bf16[128,2048]{1,0:T(8,128)(2,1)S(1)} %bitcast.102), channel_id=1, source_target_pairs={{0,2},{1,3},{2,0},{3,1},{4,6},{5,7},{6,4},{7,5},{8,10},{9,11},{10,... | collective-permute-start | bytes 1572872 | tf_op jit(solution)/shard_map/ppermute | solution.py:30
  21.3 93.0 %collective-permute-start.2 = (bf16[128,2048]{1,0:T(8,128)(2,1)S(1)}, bf16[128,2048]{1,0:T(8,128)(2,1)}, u32[]{:S(2)}, u32[]{:S(2)}) collective-permute-start(bf16[128,2048]{1,0:T(8,128)(2,1)S(1)} %bitcast.103), channel_id=1, source_target_pairs={{0,3},{1,2},{2,1},{3,0},{4,7},{5,6},{6,5},{7,4},{8,11},{9,10},{10,... | collective-permute-start | bytes 1572872 | tf_op jit(solution)/shard_map/ppermute | solution.py:30
  129.2 26.5 %collective-permute-start.4 = (bf16[128,768]{1,0:T(8,128)(2,1)}, bf16[128,768]{1,0:T(8,128)(2,1)}, u32[]{:S(2)}, u32[]{:S(2)}) collective-permute-start(bf16[128,768]{1,0:T(8,128)(2,1)} %get-tuple-element.116), channel_id=1, source_target_pairs={{0,8},{4,12},{8,0},{12,4},{16,24},{20,28},{24,16},{28,20},{1,9},{5... | collective-permute-start | bytes 589832 | tf_op jit(solution)/shard_map/ppermute | solution.py:30
  129.2 36.1 %collective-permute-start.5 = (bf16[128,768]{1,0:T(8,128)(2,1)}, bf16[128,768]{1,0:T(8,128)(2,1)}, u32[]{:S(2)}, u32[]{:S(2)}) collective-permute-start(bf16[128,768]{1,0:T(8,128)(2,1)} %get-tuple-element.115), channel_id=1, source_target_pairs={{0,12},{4,8},{8,4},{12,0},{16,28},{20,24},{24,20},{28,16},{1,13},{... | collective-permute-start | bytes 589832 | tf_op jit(solution)/shard_map/ppermute | solution.py:30
  130.9 34.5 %collective-permute-start.6 = (bf16[128,768]{1,0:T(8,128)(2,1)}, bf16[128,768]{1,0:T(8,128)(2,1)}, u32[]{:S(2)}, u32[]{:S(2)}) collective-permute-start(bf16[128,768]{1,0:T(8,128)(2,1)} %get-tuple-element.114), channel_id=1, source_target_pairs={{0,16},{4,20},{8,24},{12,28},{16,0},{20,4},{24,8},{28,12},{1,17},{... | collective-permute-start | bytes 589832 | tf_op jit(solution)/shard_map/ppermute | solution.py:30
  131.7 39.1 %collective-permute-start.7 = (bf16[128,768]{1,0:T(8,128)(2,1)}, bf16[128,768]{1,0:T(8,128)(2,1)}, u32[]{:S(2)}, u32[]{:S(2)}) collective-permute-start(bf16[128,768]{1,0:T(8,128)(2,1)} %get-tuple-element.113), channel_id=1, source_target_pairs={{0,20},{4,16},{8,28},{12,24},{16,4},{20,0},{24,12},{28,8},{1,21},{... | collective-permute-start | bytes 589832 | tf_op jit(solution)/shard_map/ppermute | solution.py:30
  133.6 41.9 %collective-permute-start.8 = (bf16[128,768]{1,0:T(8,128)(2,1)}, bf16[128,768]{1,0:T(8,128)(2,1)}, u32[]{:S(2)}, u32[]{:S(2)}) collective-permute-start(bf16[128,768]{1,0:T(8,128)(2,1)} %get-tuple-element.112), channel_id=1, source_target_pairs={{0,24},{4,28},{8,16},{12,20},{16,8},{20,12},{24,0},{28,4},{1,25},{... | collective-permute-start | bytes 589832 | tf_op jit(solution)/shard_map/ppermute | solution.py:30
  155.8 27.4 %collective-permute-start.9 = (bf16[128,768]{1,0:T(8,128)(2,1)}, bf16[128,768]{1,0:T(8,128)(2,1)}, u32[]{:S(2)}, u32[]{:S(2)}) collective-permute-start(bf16[128,768]{1,0:T(8,128)(2,1)} %get-tuple-element.111), channel_id=1, source_target_pairs={{0,28},{4,24},{8,20},{12,16},{16,12},{20,8},{24,4},{28,0},{1,29},{... | collective-permute-start | bytes 589832 | tf_op jit(solution)/shard_map/ppermute | solution.py:30
  192.9 29.3 %collective-permute-start.10 = (bf16[128,256]{1,0:T(8,128)(2,1)S(1)}, bf16[128,256]{1,0:T(8,128)(2,1)S(1)}, u32[]{:S(2)}, u32[]{:S(2)}) collective-permute-start(bf16[128,256]{1,0:T(8,128)(2,1)S(1)} %get-tuple-element.139), channel_id=1, source_target_pairs={{0,4},{4,0},{8,12},{12,8},{16,20},{20,16},{24,28},{28,24},{1,5},{5... | collective-permute-start | bytes 196616 | tf_op jit(solution)/shard_map/ppermute | solution.py:30
  193.2 35.8 %collective-permute-start.11 = (bf16[128,256]{1,0:T(8,128)(2,1)S(1)}, bf16[128,256]{1,0:T(8,128)(2,1)S(1)}, u32[]{:S(2)}, u32[]{:S(2)}) collective-permute-start(bf16[128,256]{1,0:T(8,128)(2,1)S(1)} %get-tuple-element.138), channel_id=1, source_target_pairs={{0,8},{4,12},{8,0},{12,4},{16,24},{20,28},{24,16},{28,20},{1,9},{5... | collective-permute-start | bytes 196616 | tf_op jit(solution)/shard_map/ppermute | solution.py:30
  243.8 26.0 %collective-permute-start.18 = (bf16[128,2048]{1,0:T(8,128)(2,1)S(1)}, bf16[128,2048]{1,0:T(8,128)(2,1)S(1)}, u32[]{:S(2)}, u32[]{:S(2)}) collective-permute-start(bf16[128,2048]{1,0:T(8,128)(2,1)S(1)} %get-tuple-element.102), channel_id=1, source_target_pairs={{0,2},{1,3},{2,0},{3,1},{4,6},{5,7},{6,4},{7,5},{8,10},{9,11},{10,... | collective-permute-start | bytes 1572872 | tf_op jit(solution)/shard_map/ppermute | solution.py:30
  275.2 37.3 %collective-permute-start.26 = (bf16[128,2048]{1,0:T(8,128)(2,1)}, bf16[128,2048]{1,0:T(8,128)(2,1)}, u32[]{:S(2)}, u32[]{:S(2)}) collective-permute-start(bf16[128,2048]{1,0:T(8,128)(2,1)} %bitcast.15), channel_id=1, source_target_pairs={{0,1},{1,0},{2,3},{3,2},{4,5},{5,4},{6,7},{7,6},{8,9},{9,8},{10,11... | collective-permute-start | bytes 1572872 | tf_op jit(solution)/shard_map/ppermute | solution.py:30
  275.8 36.7 %collective-permute-start.27 = (bf16[128,2048]{1,0:T(8,128)(2,1)}, bf16[128,2048]{1,0:T(8,128)(2,1)}, u32[]{:S(2)}, u32[]{:S(2)}) collective-permute-start(bf16[128,2048]{1,0:T(8,128)(2,1)} %bitcast.15), channel_id=1, source_target_pairs={{0,2},{1,3},{2,0},{3,1},{4,6},{5,7},{6,4},{7,5},{8,10},{9,11},{10,... | collective-permute-start | bytes 1572872 | tf_op jit(solution)/shard_map/ppermute | solution.py:30
  286.5 34.0 %collective-permute-start.28 = (bf16[128,2048]{1,0:T(8,128)(2,1)}, bf16[128,2048]{1,0:T(8,128)(2,1)}, u32[]{:S(2)}, u32[]{:S(2)}) collective-permute-start(bf16[128,2048]{1,0:T(8,128)(2,1)} %bitcast.15), channel_id=1, source_target_pairs={{0,3},{1,2},{2,1},{3,0},{4,7},{5,6},{6,5},{7,4},{8,11},{9,10},{10,... | collective-permute-start | bytes 1572872 | tf_op jit(solution)/shard_map/ppermute | solution.py:30
  340.9 26.0 %collective-permute-start.30 = (bf16[128,2048]{1,0:T(8,128)(2,1)S(1)}, bf16[128,2048]{1,0:T(8,128)(2,1)S(1)}, u32[]{:S(2)}, u32[]{:S(2)}) collective-permute-start(bf16[128,2048]{1,0:T(8,128)(2,1)S(1)} %get-tuple-element.96), channel_id=1, source_target_pairs={{0,2},{1,3},{2,0},{3,1},{4,6},{5,7},{6,4},{7,5},{8,10},{9,11},{10,... | collective-permute-start | bytes 1572872 | tf_op jit(solution)/shard_map/ppermute | solution.py:30
  347.4 30.0 %collective-permute-start.23 = (bf16[128,2048]{1,0:T(8,128)(2,1)S(1)}, bf16[128,2048]{1,0:T(8,128)(2,1)S(1)}, u32[]{:S(2)}, u32[]{:S(2)}) collective-permute-start(bf16[128,2048]{1,0:T(8,128)(2,1)S(1)} %get-tuple-element.97), channel_id=1, source_target_pairs={{0,1},{1,0},{2,3},{3,2},{4,5},{5,4},{6,7},{7,6},{8,9},{9,8},{10,11... | collective-permute-start | bytes 1572872 | tf_op jit(solution)/shard_map/ppermute | solution.py:30
  348.3 39.0 %collective-permute-start.24 = (bf16[128,2048]{1,0:T(8,128)(2,1)S(1)}, bf16[128,2048]{1,0:T(8,128)(2,1)S(1)}, u32[]{:S(2)}, u32[]{:S(2)}) collective-permute-start(bf16[128,2048]{1,0:T(8,128)(2,1)S(1)} %get-tuple-element.99), channel_id=1, source_target_pairs={{0,2},{1,3},{2,0},{3,1},{4,6},{5,7},{6,4},{7,5},{8,10},{9,11},{10,... | collective-permute-start | bytes 1572872 | tf_op jit(solution)/shard_map/ppermute | solution.py:30
  354.9 32.4 %collective-permute-start.25 = (bf16[128,2048]{1,0:T(8,128)(2,1)S(1)}, bf16[128,2048]{1,0:T(8,128)(2,1)S(1)}, u32[]{:S(2)}, u32[]{:S(2)}) collective-permute-start(bf16[128,2048]{1,0:T(8,128)(2,1)S(1)} %get-tuple-element.98), channel_id=1, source_target_pairs={{0,3},{1,2},{2,1},{3,0},{4,7},{5,6},{6,5},{7,4},{8,11},{9,10},{10,... | collective-permute-start | bytes 1572872 | tf_op jit(solution)/shard_map/ppermute | solution.py:30
  418.1 211.9 %reduce-scatter.11.cloned.1.call-start = ((), (), s32[]{:S(2)}) async-start(), calls=%async_computation.10 | async-start | bytes 6488064 | tf_op jit(solution)/shard_map/reduce_scatter | solution.py:537
  425.8 212.8 %reduce-scatter.5.cloned.1.call-start = ((), (), s32[]{:S(2)}) async-start(), calls=%async_computation.7 | async-start | bytes 7077888 | tf_op jit(solution)/shard_map/reduce_scatter | solution.py:568
  475.5 30.3 %collective-permute-start.44 = (bf16[128,768]{1,0:T(8,128)(2,1)S(1)}, bf16[128,768]{1,0:T(8,128)(2,1)S(1)}, u32[]{:S(2)}, u32[]{:S(2)}) collective-permute-start(bf16[128,768]{1,0:T(8,128)(2,1)S(1)} %get-tuple-element.107), channel_id=1, source_target_pairs={{0,12},{4,8},{8,4},{12,0},{16,28},{20,24},{24,20},{28,16},{1,13},{... | collective-permute-start | bytes 589832 | tf_op jit(solution)/shard_map/ppermute | solution.py:30
  475.5 30.3 %collective-permute-start.45 = (bf16[128,768]{1,0:T(8,128)(2,1)S(1)}, bf16[128,768]{1,0:T(8,128)(2,1)S(1)}, u32[]{:S(2)}, u32[]{:S(2)}) collective-permute-start(bf16[128,768]{1,0:T(8,128)(2,1)S(1)} %get-tuple-element.106), channel_id=1, source_target_pairs={{0,16},{4,20},{8,24},{12,28},{16,0},{20,4},{24,8},{28,12},{1,17},{... | collective-permute-start | bytes 589832 | tf_op jit(solution)/shard_map/ppermute | solution.py:30
  477.8 31.1 %collective-permute-start.46 = (bf16[128,768]{1,0:T(8,128)(2,1)S(1)}, bf16[128,768]{1,0:T(8,128)(2,1)S(1)}, u32[]{:S(2)}, u32[]{:S(2)}) collective-permute-start(bf16[128,768]{1,0:T(8,128)(2,1)S(1)} %get-tuple-element.105), channel_id=1, source_target_pairs={{0,20},{4,16},{8,28},{12,24},{16,4},{20,0},{24,12},{28,8},{1,21},{... | collective-permute-start | bytes 589832 | tf_op jit(solution)/shard_map/ppermute | solution.py:30
  477.9 42.3 %collective-permute-start.47 = (bf16[128,768]{1,0:T(8,128)(2,1)S(1)}, bf16[128,768]{1,0:T(8,128)(2,1)S(1)}, u32[]{:S(2)}, u32[]{:S(2)}) collective-permute-start(bf16[128,768]{1,0:T(8,128)(2,1)S(1)} %get-tuple-element.104), channel_id=1, source_target_pairs={{0,24},{4,28},{8,16},{12,20},{16,8},{20,12},{24,0},{28,4},{1,25},{... | collective-permute-start | bytes 589832 | tf_op jit(solution)/shard_map/ppermute | solution.py:30
  497.0 31.1 %collective-permute-start.48 = (bf16[128,768]{1,0:T(8,128)(2,1)S(1)}, bf16[128,768]{1,0:T(8,128)(2,1)S(1)}, u32[]{:S(2)}, u32[]{:S(2)}) collective-permute-start(bf16[128,768]{1,0:T(8,128)(2,1)S(1)} %get-tuple-element.103), channel_id=1, source_target_pairs={{0,28},{4,24},{8,20},{12,16},{16,12},{20,8},{24,4},{28,0},{1,29},{... | collective-permute-start | bytes 589832 | tf_op jit(solution)/shard_map/ppermute | solution.py:30
  535.3 218.7 %reduce-scatter.9.cloned.1.call-start = ((), (), s32[]{:S(2)}) async-start(), calls=%async_computation.9 | async-start | bytes 12976128 | tf_op jit(solution)/shard_map/reduce_scatter | solution.py:548
  557.2 26.1 %collective-permute-start.50 = (bf16[128,2048]{1,0:T(8,128)(2,1)}, bf16[128,2048]{1,0:T(8,128)(2,1)}, u32[]{:S(2)}, u32[]{:S(2)}) collective-permute-start(bf16[128,2048]{1,0:T(8,128)(2,1)} %get-tuple-element.93), channel_id=1, source_target_pairs={{0,2},{1,3},{2,0},{3,1},{4,6},{5,7},{6,4},{7,5},{8,10},{9,11},{10,... | collective-permute-start | bytes 1572872 | tf_op jit(solution)/shard_map/ppermute | solution.py:30
  (98 other events, 1661.6 us)
Sparse Core Ops, SparseCore 0:
  12.0 89.0 all-gather.3
  103.4 151.0 all-gather.5
  256.6 58.9 all-gather.7
  418.2 40.8 reduce-scatter.6
  461.3 93.5 reduce-scatter.10
  557.0 76.8 reduce-scatter.4
  636.3 117.6 reduce-scatter.8

commit v3 on v2

--- a/solution.py
+++ b/solution.py
@@ -49,6 +49,20 @@
         value = value + swapped(value, axis, bits)
         bits *= 2
     return value
+
+
+def chip_scatter(product, halves, axis):
+    count = lax.axis_size("ctx")
+    own, other = halves
+    sent = product(other).astype(BF16)
+    total = (product(own) + swapped(sent, "ctx", 1).astype(F32)).astype(BF16)
+    return lax.psum_scatter(
+        total,
+        "ctx",
+        scatter_dimension=axis,
+        tiled=True,
+        axis_index_groups=[list(range(first, count, 2)) for first in range(2)],
+    )
 
 
 def layer_norm(matrix, gain_vec, shift_vec):
@@ -343,27 +357,50 @@
     )(me, ids_row, ids_col, *tables, *pieces, att, everything, lse)
 
 
-def pack_kernel(qkv_ref, out_ref, vec_ref, packed_ref):
+def halve_kernel(chips, me_ref, matrix_ref, own_ref, other_ref):
+    core = me_ref[0] % 2
+    cols = matrix_ref.shape[1] // (2 * chips)
+    for chip in range(chips):
+        into = slice(chip * cols, (chip + 1) * cols)
+        for out_ref, which in ((own_ref, core), (other_ref, 1 - core)):
+            start = pl.multiple_of((2 * chip + which) * cols, cols)
+            out_ref[:, into] = matrix_ref[:, pl.ds(start, cols)]
+
+
+def halve(me, matrix, chips):
+    rows, cols = matrix.shape
+    vmem = pl.BlockSpec(memory_space=pltpu.VMEM)
+    return pl.pallas_call(
+        functools.partial(halve_kernel, chips),
+        in_specs=[pl.BlockSpec(memory_space=pltpu.SMEM), vmem],
+        out_specs=[vmem] * 2,
+        out_shape=[jax.ShapeDtypeStruct((rows, cols // 2), BF16)] * 2,
+        compiler_params=kernel_params(),
+        cost_estimate=pl.CostEstimate(
+            flops=0, bytes_accessed=4 * rows * cols, transcendentals=0
+        ),
+        name="halve",
+    )(me, matrix)
+
+
+def pack_kernel(qkv_ref, out_ref, packed_ref):
     head_cols = qkv_ref.shape[2]
     for which in range(3):
         packed_ref[:, which * head_cols : (which + 1) * head_cols] = qkv_ref[which].astype(BF16)
     packed_ref[:, 3 * head_cols : 4 * head_cols] = out_ref[...].T.astype(BF16)
-    vectors = vec_ref[...]
-    padding = jnp.zeros((vectors.shape[0], 128 - vectors.shape[1]), F32)
-    packed_ref[:, 4 * head_cols :] = jnp.concatenate([vectors, padding], axis=1).astype(BF16)
-
-
-def pack(w_qkv, w_out, norm_vecs):
+
+
+def pack(w_qkv, w_out):
     _, rows, head_cols = w_qkv.shape
     vmem = pl.BlockSpec(memory_space=pltpu.VMEM)
     return pl.pallas_call(
         pack_kernel,
-        in_specs=[vmem] * 3,
+        in_specs=[vmem] * 2,
         out_specs=vmem,
-        out_shape=jax.ShapeDtypeStruct((rows, 4 * head_cols + 128), BF16),
+        out_shape=jax.ShapeDtypeStruct((rows, 4 * head_cols), BF16),
         compiler_params=kernel_params(),
         name="pack",
-    )(w_qkv, w_out, norm_vecs)
+    )(w_qkv, w_out)
 
 
 def adam_kernel(leading, share_ref, master_ref, first_ref, second_ref, *outs):
@@ -473,7 +510,7 @@
     ctx_scalar = ctx_place.astype(jnp.int32).reshape(1)
     places = jnp.stack([ctx_place, shard_place]).astype(jnp.int32)
 
-    first_weights = pack(w_qkv.transpose(1, 0, 2), w_out, norm_vecs)
+    first_weights = pack(w_qkv.transpose(1, 0, 2), w_out)
     first_all = lax.all_gather(first_weights, "ctx", axis=0, tiled=True)
     gu_part = w_gu.astype(BF16).reshape(own_rows, 2 * unit_cols)
     gu_flat = lax.all_gather(gu_part, "ctx", axis=0, tiled=True)
@@ -489,13 +526,19 @@
     tables = rotary_tables(positions, width)
     tables_all = rotary_tables(jnp.arange(length, dtype=jnp.int32), width)
 
-    vectors = first_all[:, 4 * head_cols : 4 * head_cols + 8].astype(F32).T
+    own_vectors = jnp.pad(norm_vecs.astype(BF16).astype(F32).T, ((0, 2), (0, 0)))
+    vectors = butterfly(
+        lax.dynamic_update_slice(
+            jnp.zeros((8, depth), F32), own_vectors, (0, ctx_place * own_rows)
+        ),
+        "ctx",
+    )
     gain_one, shift_one, gain_two, shift_two = [vectors[row : row + 1] for row in range(4)]
     col_start = shard_place * head_cols
     bias_query = lax.dynamic_slice_in_dim(vectors[4:5], col_start, head_cols, 1)
     bias_value = lax.dynamic_slice_in_dim(vectors[5:6], col_start, head_cols, 1)
     qkv_flat = first_all[:, : 3 * head_cols]
-    out_turned = first_all[:, 3 * head_cols : 4 * head_cols]
+    out_turned = first_all[:, 3 * head_cols :]
 
     gathered_one, projected = project(
         hidden_blocks, gain_one, shift_one, bias_query, bias_value, tables, first_all, groups
@@ -533,8 +576,7 @@
     gate_up = dot(gathered_two, gu_flat)
     gate_part = gate_up[:, :unit_cols]
     activated = (gate_part * jax.nn.sigmoid(gate_part) * gate_up[:, unit_cols:]).astype(BF16)
-    grad_down = dot_rows(activated, cot_all).astype(BF16)
-    share_down = lax.psum_scatter(grad_down, "ctx", scatter_dimension=1, tiled=True)
+    share_down = chip_scatter(lambda half: dot_rows(activated, half), halve(ctx_scalar, cot_all, ctx_size // 2), 1)
 
     gate_up = lax.optimization_barrier(gate_up)
     gate_part = gate_up[:, :unit_cols]
@@ -544,8 +586,7 @@
     grad_gate = grad_act * up_part * sigmoid_gate * (1.0 + gate_part * (1.0 - sigmoid_gate))
     grad_up = grad_act * gate_part * sigmoid_gate
     grad_gate_up = jnp.concatenate([grad_gate, grad_up], axis=1).astype(BF16)
-    grad_gu = dot_rows(gathered_two, grad_gate_up).astype(BF16)
-    share_gu = lax.psum_scatter(grad_gu, "ctx", scatter_dimension=0, tiled=True)
+    share_gu = chip_scatter(lambda half: dot_rows(half, grad_gate_up), halve(ctx_scalar, gathered_two, ctx_size // 2), 0)
     normed_two_terms = dot_back(grad_gate_up, gu_flat).astype(BF16)
     grad_normed_two = scatter_sum(row_blocks(normed_two_terms), "wsh")
     grad_middle, grad_gain_two, grad_shift_two = norm_back(
@@ -553,22 +594,29 @@
     )
     grad_middle = grad_middle + cotangent[0].astype(F32)
     middle_all = jnp.concatenate(gather_rows(grad_middle.astype(BF16), "wsh"), axis=0)
-    grad_out = dot_rows(attended, middle_all).astype(BF16)
-    share_out = lax.psum_scatter(grad_out, "ctx", scatter_dimension=1, tiled=True)
+    share_out = chip_scatter(lambda half: dot_rows(attended, half), halve(ctx_scalar, middle_all, ctx_size // 2), 1)
     grad_att = dot(middle_all, out_turned).astype(BF16)
-    grad_att = grad_att.reshape(shard_count, tok_rows, groups, width).transpose(0, 2, 1, 3)
-    grad_pieces = [exchange_out(grad_att, bits) for bits in range(ctx_size)]
+
+    def exchange_grad(bits):
+        target = ctx_place ^ bits
+        row = ((target // groups) ^ shard_place) * tok_rows
+        picked = lax.dynamic_slice(
+            grad_att, (row, target % groups * width), (tok_rows, width)
+        )
+        return picked if bits == 0 else swapped(picked, "ctx", bits)
+
+    grad_pieces = [exchange_grad(bits) for bits in range(ctx_size)]
     grad_own, bias_sums = attend_back(
         ctx_scalar, ids_own, ids_col, tables_all, grad_pieces, att_own, qkv_own, log_sums, most
     )
     grad_rows = place(
         places, [exchange_back(grad_own, bits) for bits in range(ctx_size)], groups, 3
     )
-    grad_qkv = dot_rows(gathered_one, grad_rows).astype(BF16)
-    share_qkv = lax.psum_scatter(grad_qkv, "ctx", scatter_dimension=0, tiled=True)
-
-    ffn_terms = dot(activated, down_weight).astype(BF16)
-    block_out = (middle + scatter_sum(row_blocks(ffn_terms), "wsh")).astype(BF16)
+    share_qkv = chip_scatter(lambda half: dot_rows(half, grad_rows), halve(ctx_scalar, gathered_one, ctx_size // 2), 0)
+
+    late_activated, late_middle, _ = lax.optimization_barrier((activated, middle, grad_rows))
+    ffn_terms = dot(late_activated, down_weight).astype(BF16)
+    block_out = (late_middle + scatter_sum(row_blocks(ffn_terms), "wsh")).astype(BF16)
 
     normed_one_terms = dot_back(grad_rows, qkv_flat).astype(BF16)
     grad_normed_one = scatter_sum(row_blocks(normed_one_terms), "wsh")
@@ -613,7 +661,9 @@
     ]
     share_out, new_out, new_first_out, new_second_out = [
         array[0]
-        for array in adam_parts(True, share_out, w_out[None], first_out[None], second_out[None])
+        for array in adam_parts(
+            True, share_out, w_out[None], first_out[None], second_out[None]
+        )
     ]
     new_vecs, new_first_vecs, new_second_vecs = adam_step(
         norm_vecs, share_vecs, first_vecs, second_vecs, 0.0

time: 781 us -> 724 us (0.927)
  waiting for transfers between devices: 445 us -> 391 us
  local copies, waits for them, and re-layouts: 58.7 us -> 40.1 us
  matrix products: 74.6 us -> 83.5 us
    reduce_scatter x4, waiting for transfers between devices: 106 us -> 68.1 us  [chip_scatter(): lax.psum_scatter(total, 'ctx', scatter_dimension=axis, tiled=True, axis_i...]
    all_gather x1, waiting for transfers between devices: 78 us -> 51.9 us  [local(): first_all = lax.all_gather(first_weights, 'ctx', axis=0, tiled=True)]
    dot_general x4 -> x8, matrix products: 26.8 us -> 34.9 us  [dot_rows(): lax.dot_general(left_side, right_side, (((0,), (0,)), ((), ())), preferre...]
    all_gather x1, waiting for transfers between devices: 0.01 us -> 7.91 us  [local(): down_weight = lax.all_gather(w_down.astype(BF16), 'ctx', axis=1, tiled=True)]
    ppermute x57 -> x64, starting transfers between devices: 106 us -> 110 us  [swapped(): lax.ppermute(value, axis, [(source, source ^ bits) for source in range(co...]
    unnamed x142 -> x163, local copies, waits for them, and re-layouts: 36.3 us -> 32.7 us
    ppermute x57 -> x64, waiting for transfers between devices: 261 us -> 263 us  [swapped(): lax.ppermute(value, axis, [(source, source ^ bits) for source in range(co...]
  transfers between devices with their start and end apart: 64 -> 71, of which waited for: 36 -> 39; matrix products, arithmetic and copies ran while one was open for 13% -> 14% of each run, Pallas kernels for 5% -> 5%
where the time goes in v3:
time: 724 us; the launch traced here: 718 us
  waiting for transfers between devices  391 us (54%)
  starting transfers between devices  111 us (15%)
  matrix products  83.5 us (12%)
  Pallas kernels  49 us (7%)
  local copies, waits for them, and re-layouts  40.1 us (6%)
  other arithmetic  27.2 us (4%)
  between operations  15.8 us (2%)
    ppermute x64, waiting for transfers between devices, swapped(): lax.ppermute(value, axis, [(source, source ^ bits) for source in range(co...  263 us
    ppermute x64, starting transfers between devices, swapped(): lax.ppermute(value, axis, [(source, source ^ bits) for source in range(co...  110 us
    reduce_scatter x4, waiting for transfers between devices, chip_scatter(): lax.psum_scatter(total, 'ctx', scatter_dimension=axis, tiled=True, axis_i...  68.1 us
    all_gather x1, waiting for transfers between devices, local(): first_all = lax.all_gather(first_weights, 'ctx', axis=0, tiled=True)  51.9 us
    dot_general x8, matrix products, dot_rows(): lax.dot_general(left_side, right_side, (((0,), (0,)), ((), ())), preferre...  34.9 us
    unnamed x163, local copies, waits for them, and re-layouts  32.7 us
    dot_general x4, matrix products, dot_back(): lax.dot_general(left_side, right_side, (((1,), (1,)), ((), ())), preferre...  25.4 us
    dot_general x3, matrix products, dot(): return jnp.dot(left_side, right_side, preferred_element_type=F32)  23.2 us
  transfers between devices with their start and end apart: 71, of which 39 were waited for; matrix products, arithmetic and copies ran while one was open for 14% of the time, Pallas kernels for 5%

profile of v3, /device:TPU:0, one launch (start us, length us, event | category | flops | bytes accessed | tf_op | source)
XLA Modules:
  0.0 717.6 jit_solution(11713029906216942921)
XLA Ops:
  37.1 7.6 %collective-permute-done.5 = f32[8,2048]{1,0:T(8,128)} collective-permute-done((f32[8,2048]{1,0:T(8,128)}, f32[8,2048]{1,0:T(8,128)}, u32[]{:S(2)}, u32[]{:S(2)}) %collective-permute-start.5) | collective-permute-done | bytes 65568 | tf_op jit(solution)/shard_map/ppermute | solution.py:30
  46.8 51.9 %all-gather.4.cloned.1.call-done.refs_11_.refs_12_.refs_13_ = bf16[2048,2048]{1,0:T(8,128)(2,1)} async-done(((bf16[256,2048]{1,0:T(8,128)(2,1)}), bf16[2048,2048]{1,0:T(8,128)(2,1)}) %all-gather.4.cloned.1.call-update) | async-done | bytes 8388624 | tf_op jit(solution)/shard_map/all_gather | solution.py:514
  103.3 8.7 %project.1 = (bf16[512,2048]{1,0:T(8,128)(2,1)S(1)}, bf16[4,2,128,768]{3,2,1,0:T(8,128)(2,1)S(1)}) custom-call(bf16[128,2048]{1,0:T(8,128)(2,1)S(1)} %bitcast.93, bf16[128,2048]{1,0:T(8,128)(2,1)} %collective-permute-done.refs_1_, bf16[128,2048]{1,0:T(8,128)(2,1)} %collective-permute-done.1.refs_2_, bf16[128,2048]{1,0:T(8,128)(2,1)} %collective-permute-done.2.refs_3_, ...), custom_call_target="tpu_custom_call" | custom-call | flops 3221225472 | bytes 10485760 | tf_op jit(solution)/shard_map/project/pallas_call | solution.py:179
  119.0 27.4 %collective-permute-done.10.refs_5_ = bf16[128,768]{1,0:T(8,128)(2,1)} collective-permute-done((bf16[128,768]{1,0:T(8,128)(2,1)}, bf16[128,768]{1,0:T(8,128)(2,1)}, u32[]{:S(2)}, u32[]{:S(2)}) %collective-permute-start.10) | collective-permute-done | bytes 196640 | tf_op jit(solution)/shard_map/ppermute | solution.py:30
  146.4 13.4 %collective-permute-start.9 = (bf16[128,768]{1,0:T(8,128)(2,1)}, bf16[128,768]{1,0:T(8,128)(2,1)}, u32[]{:S(2)}, u32[]{:S(2)}) collective-permute-start(bf16[128,768]{1,0:T(8,128)(2,1)} %get-tuple-element.131), channel_id=1, source_target_pairs={{0,16},{4,20},{8,24},{12,28},{16,0},{20,4},{24,8},{28,12},{1,17},{... | collective-permute-start | bytes 589832 | tf_op jit(solution)/shard_map/ppermute | solution.py:30
  162.1 29.8 %collective-permute-done.9.refs_4_ = bf16[128,768]{1,0:T(8,128)(2,1)} collective-permute-done((bf16[128,768]{1,0:T(8,128)(2,1)}, bf16[128,768]{1,0:T(8,128)(2,1)}, u32[]{:S(2)}, u32[]{:S(2)}) %collective-permute-start.9) | collective-permute-done | bytes 196640 | tf_op jit(solution)/shard_map/ppermute | solution.py:30
  232.8 11.1 %collective-permute-done.20 = bf16[128,2048]{1,0:T(8,128)(2,1)S(1)} collective-permute-done((bf16[128,2048]{1,0:T(8,128)(2,1)S(1)}, bf16[128,2048]{1,0:T(8,128)(2,1)S(1)}, u32[]{:S(2)}, u32[]{:S(2)}) %collective-permute-start.20) | collective-permute-done | bytes 524320 | tf_op jit(solution)/shard_map/ppermute | solution.py:30
  244.0 11.7 %collective-permute-done.21 = bf16[128,2048]{1,0:T(8,128)(2,1)S(1)} collective-permute-done((bf16[128,2048]{1,0:T(8,128)(2,1)S(1)}, bf16[128,2048]{1,0:T(8,128)(2,1)S(1)}, u32[]{:S(2)}, u32[]{:S(2)}) %collective-permute-start.21) | collective-permute-done | bytes 524320 | tf_op jit(solution)/shard_map/ppermute | solution.py:30
  263.1 9.3 %collective-permute-done.23 = bf16[128,2048]{1,0:T(8,128)(2,1)S(1)} collective-permute-done((bf16[128,2048]{1,0:T(8,128)(2,1)S(1)}, bf16[128,2048]{1,0:T(8,128)(2,1)S(1)}, u32[]{:S(2)}, u32[]{:S(2)}) %collective-permute-start.23) | collective-permute-done | bytes 524320 | tf_op jit(solution)/shard_map/ppermute | solution.py:30
  273.9 11.0 %collective-permute-done.24 = bf16[128,2048]{1,0:T(8,128)(2,1)S(1)} collective-permute-done((bf16[128,2048]{1,0:T(8,128)(2,1)S(1)}, bf16[128,2048]{1,0:T(8,128)(2,1)S(1)}, u32[]{:S(2)}, u32[]{:S(2)}) %collective-permute-start.24) | collective-permute-done | bytes 524320 | tf_op jit(solution)/shard_map/ppermute | solution.py:30
  285.6 12.1 %fusion.49 = f32[512,2816]{1,0:T(8,128)} fusion(bf16[2048,2816]{1,0:T(8,128)(2,1)} %all-gather.6.cloned.1.call-done, bf16[128,2048]{1,0:T(8,128)(2,1)} %collective-permute-done.25, bf16[128,2048]{1,0:T(8,128)(2,1)} %copy-done.55, bf16[128,2048]{1,0:T(8,128)(2,1)} %copy-done.53, bf16[128,2048]{1,0:T(8,128)(2,1)} %copy-done.48), kind=kOutput, calls=%fused_computation.137 | convolution fusion | flops 5913968640 | bytes 19398656 | tf_op jit(solution)/shard_map/dot_general | solution.py:120
  297.7 7.7 %collective-permute-done.27 = bf16[128,2048]{1,0:T(8,128)(2,1)} collective-permute-done((bf16[128,2048]{1,0:T(8,128)(2,1)}, bf16[128,2048]{1,0:T(8,128)(2,1)}, u32[]{:S(2)}, u32[]{:S(2)}) %collective-permute-start.27) | collective-permute-done | bytes 524320 | tf_op jit(solution)/shard_map/ppermute | solution.py:30
  305.4 7.9 %all-gather.8.cloned.1.call-done = bf16[1408,2048]{1,0:T(8,128)(2,1)} async-done(((bf16[1408,256]{1,0:T(8,128)(2,1)}), bf16[1408,2048]{1,0:T(8,128)(2,1)}) %all-gather.8.cloned.1.call-update) | async-done | bytes 5767184 | tf_op jit(solution)/shard_map/all_gather | solution.py:517
  313.3 9.2 %fusion.7 = (bf16[512,1408]{1,0:T(8,128)(2,1)S(1)}, bf16[512,1408]{1,0:T(8,128)(2,1)S(1)}) fusion(f32[512,2816]{1,0:T(8,128)} %fusion.49, bf16[1408,2048]{1,0:T(8,128)(2,1)} %all-gather.8.cloned.1.call-done, bf16[128,2048]{1,0:T(8,128)(2,1)} %collective-permute-done.28, bf16[128,2048]{1,0:T(8,128)(2,1)} %collective-permute-done.27, ...), kind=kOutput, calls=%fused_computation.15 | convolution fusion | flops 2970550272 | bytes 16515072 | tf_op jit(solution)/shard_map/dot_general | solution.py:114
  322.6 6.4 convolution_convert_fusion.3
  334.8 9.2 %collective-permute-done.29 = bf16[128,2048]{1,0:T(8,128)(2,1)S(1)} collective-permute-done((bf16[128,2048]{1,0:T(8,128)(2,1)S(1)}, bf16[128,2048]{1,0:T(8,128)(2,1)S(1)}, u32[]{:S(2)}, u32[]{:S(2)}) %collective-permute-start.29) | collective-permute-done | bytes 524320 | tf_op jit(solution)/shard_map/ppermute | solution.py:30
  344.0 11.8 %collective-permute-done.30 = bf16[128,2048]{1,0:T(8,128)(2,1)} collective-permute-done((bf16[128,2048]{1,0:T(8,128)(2,1)S(1)}, bf16[128,2048]{1,0:T(8,128)(2,1)}, u32[]{:S(2)}, u32[]{:S(2)}) %collective-permute-start.30) | collective-permute-done | bytes 524320 | tf_op jit(solution)/shard_map/ppermute | solution.py:30
  364.8 10.5 %collective-permute-done.32 = bf16[128,2048]{1,0:T(8,128)(2,1)S(1)} collective-permute-done((bf16[128,2048]{1,0:T(8,128)(2,1)S(1)}, bf16[128,2048]{1,0:T(8,128)(2,1)S(1)}, u32[]{:S(2)}, u32[]{:S(2)}) %collective-permute-start.32) | collective-permute-done | bytes 524320 | tf_op jit(solution)/shard_map/ppermute | solution.py:30
  375.2 10.6 %collective-permute-done.33 = bf16[128,2048]{1,0:T(8,128)(2,1)S(1)} collective-permute-done((bf16[128,2048]{1,0:T(8,128)(2,1)S(1)}, bf16[128,2048]{1,0:T(8,128)(2,1)S(1)}, u32[]{:S(2)}, u32[]{:S(2)}) %collective-permute-start.33) | collective-permute-done | bytes 524320 | tf_op jit(solution)/shard_map/ppermute | solution.py:30
  426.5 11.9 %attend_back.1 = (bf16[1024,768]{1,0:T(8,128)(2,1)}, f32[8,256]{1,0:T(8,128)S(1)}) custom-call(s32[1]{0:T(128)} %bitcast.1.me_ref, s32[1,1024]{1,0:T(1,128)S(1)} %constant_dynamic-slice_fusion.21.ids_row_ref, s32[1024,1]{1,0:T(8,128)S(1)} %copy-done.25, f32[1024,256]{1,0:T(8,128)S(1)} %get-tuple-element.161.cos_ref, ...), custom_call_target="tpu_custom_call" | custom-call | flops 5368709120 | bytes 4194304 | tf_op jit(solution)/shard_map/attend_back/pallas_call | solution.py:337
  446.9 16.1 %collective-permute-done.43.refs_2_ = bf16[128,768]{1,0:T(8,128)(2,1)S(1)} collective-permute-done((bf16[128,768]{1,0:T(8,128)(2,1)S(1)}, bf16[128,768]{1,0:T(8,128)(2,1)S(1)}, u32[]{:S(2)}, u32[]{:S(2)}) %collective-permute-start.43) | collective-permute-done | bytes 196640 | tf_op jit(solution)/shard_map/ppermute | solution.py:30
  465.9 10.7 %collective-permute-done.44.refs_3_ = bf16[128,768]{1,0:T(8,128)(2,1)S(1)} collective-permute-done((bf16[128,768]{1,0:T(8,128)(2,1)S(1)}, bf16[128,768]{1,0:T(8,128)(2,1)S(1)}, u32[]{:S(2)}, u32[]{:S(2)}) %collective-permute-start.44) | collective-permute-done | bytes 196640 | tf_op jit(solution)/shard_map/ppermute | solution.py:30
  476.6 6.7 collective-permute-done.46.refs_5_
  487.9 7.8 %collective-permute-done.48.refs_7_ = bf16[128,768]{1,0:T(8,128)(2,1)S(1)} collective-permute-done((bf16[128,768]{1,0:T(8,128)(2,1)S(1)}, bf16[128,768]{1,0:T(8,128)(2,1)S(1)}, u32[]{:S(2)}, u32[]{:S(2)}) %collective-permute-start.48) | collective-permute-done | bytes 196640 | tf_op jit(solution)/shard_map/ppermute | solution.py:30
  502.4 6.7 convolution_convert_fusion
  518.9 9.5 %add_convert_fusion = bf16[1024,2816]{1,0:T(8,128)(2,1)} fusion(bf16[1024,2816]{1,0:T(8,128)(2,1)} %collective-permute-done.57, bf16[512,1024]{1,0:T(8,128)(2,1)} %copy-done.38, bf16[512,1408]{1,0:T(8,128)(2,1)} %copy-done.78, bf16[512,1408]{1,0:T(8,128)(2,1)} %copy-done.76), kind=kOutput, calls=%fused_computation | convolution fusion | flops 2967207936 | bytes 15466496 | tf_op jit(solution)/shard_map/dot_general | solution.py:108
  528.4 6.7 fusion.2
  538.8 7.7 %convolution_convert_fusion.5 = bf16[512,2048]{1,0:T(8,128)(2,1)} fusion(bf16[512,1408]{1,0:T(8,128)(2,1)S(1)} %copy-done.52, bf16[1408,2048]{1,0:T(8,128)(2,1)} %all-gather.8.cloned.1.call-done), kind=kOutput, calls=%fused_computation.11 | convolution fusion | flops 2953838592 | bytes 9306112 | tf_op jit(solution)/shard_map/dot_general | solution.py:120
  550.1 11.6 %collective-permute-done.53 = bf16[128,2048]{1,0:T(8,128)(2,1)S(1)} collective-permute-done((bf16[128,2048]{1,0:T(8,128)(2,1)S(1)}, bf16[128,2048]{1,0:T(8,128)(2,1)S(1)}, u32[]{:S(2)}, u32[]{:S(2)}) %collective-permute-start.53) | collective-permute-done | bytes 524320 | tf_op jit(solution)/shard_map/ppermute | solution.py:30
  569.3 21.5 %collective-permute-start.60 = (f32[8,2048]{1,0:T(8,128)S(1)}, f32[8,2048]{1,0:T(8,128)S(1)}, u32[]{:S(2)}, u32[]{:S(2)}) collective-permute-start(f32[8,2048]{1,0:T(8,128)S(1)} %add.478), channel_id=1, source_target_pairs={{0,8},{4,12},{8,0},{12,4},{16,24},{20,28},{24,16},{28,20},{1,9},{5... | collective-permute-start | bytes 196616 | tf_op jit(solution)/shard_map/ppermute | solution.py:30
  630.0 68.1 %reduce-scatter.9.cloned.1.call-done.share_ref = bf16[256,2816]{1,0:T(8,128)(2,1)} async-done(((bf16[1024,2816]{1,0:T(8,128)(2,1)}), bf16[256,2816]{1,0:T(8,128)(2,1)}) %reduce-scatter.9.cloned.1.call-update) | async-done | bytes 1441808 | tf_op jit(solution)/shard_map/reduce_scatter | solution.py:59
  699.5 10.7 %adam.6 = (f32[256,2,1408]{2,1,0:T(2,128)}, f32[256,2,1408]{2,1,0:T(2,128)}, f32[256,2,1408]{2,1,0:T(2,128)}, f32[256,2,1408]{2,1,0:T(2,128)}) custom-call(bf16[256,2816]{1,0:T(8,128)(2,1)S(1)} %copy-done.15, f32[256,2,1408]{2,1,0:T(2,128)S(1)} %copy-done.3, f32[256,2,1408]{2,1,0:T(2,128)} %first_ref.1, f32[256,2,1408]{2,1,0:T(2,128)} %second_ref.1), custom_call_target="tpu_custom_call" | custom-call | bytes 21626880 | tf_op jit(solution)/shard_map/adam/pallas_call | solution.py:431
  (369 shorter events, 238.8 us)
Async XLA Ops:
  7.2 91.5 %all-gather.4.cloned.1.call-start = ((), (), s32[]{:S(2)}) async-start(), calls=%async_computation.4 | async-start | bytes 9437184 | tf_op jit(solution)/shard_map/all_gather | solution.py:514
  11.0 274.6 %all-gather.6.cloned.1.call-start = ((), (), s32[]{:S(2)}) async-start(), calls=%async_computation.5 | async-start | bytes 12976128 | tf_op jit(solution)/shard_map/all_gather | solution.py:516
  13.4 299.9 %all-gather.8.cloned.1.call-start = ((), (), s32[]{:S(2)}) async-start(), calls=%async_computation.6 | async-start | bytes 6488064 | tf_op jit(solution)/shard_map/all_gather | solution.py:517
  15.8 591.9 %reduce-scatter.7.cloned.1.call-start = ((), (), s32[]{:S(2)}) async-start(), calls=%async_computation.8 | async-start | bytes 1310720 | tf_op jit(solution)/shard_map/reduce_scatter | solution.py:59
  15.8 30.9 %collective-permute-start = (bf16[128,2048]{1,0:T(8,128)(2,1)S(1)}, bf16[128,2048]{1,0:T(8,128)(2,1)}, u32[]{:S(2)}, u32[]{:S(2)}) collective-permute-start(bf16[128,2048]{1,0:T(8,128)(2,1)S(1)} %bitcast.90), channel_id=1, source_target_pairs={{0,1},{1,0},{2,3},{3,2},{4,5},{5,4},{6,7},{7,6},{8,9},{9,8},{10,11... | collective-permute-start | bytes 1572872 | tf_op jit(solution)/shard_map/ppermute | solution.py:30
  18.9 27.9 %collective-permute-start.1 = (bf16[128,2048]{1,0:T(8,128)(2,1)S(1)}, bf16[128,2048]{1,0:T(8,128)(2,1)}, u32[]{:S(2)}, u32[]{:S(2)}) collective-permute-start(bf16[128,2048]{1,0:T(8,128)(2,1)S(1)} %bitcast.91), channel_id=1, source_target_pairs={{0,2},{1,3},{2,0},{3,1},{4,6},{5,7},{6,4},{7,5},{8,10},{9,11},{10,... | collective-permute-start | bytes 1572872 | tf_op jit(solution)/shard_map/ppermute | solution.py:30
  20.4 26.4 %collective-permute-start.2 = (bf16[128,2048]{1,0:T(8,128)(2,1)S(1)}, bf16[128,2048]{1,0:T(8,128)(2,1)}, u32[]{:S(2)}, u32[]{:S(2)}) collective-permute-start(bf16[128,2048]{1,0:T(8,128)(2,1)S(1)} %bitcast.92), channel_id=1, source_target_pairs={{0,3},{1,2},{2,1},{3,0},{4,7},{5,6},{6,5},{7,4},{8,11},{9,10},{10,... | collective-permute-start | bytes 1572872 | tf_op jit(solution)/shard_map/ppermute | solution.py:30
  114.4 32.0 %collective-permute-start.10 = (bf16[128,768]{1,0:T(8,128)(2,1)}, bf16[128,768]{1,0:T(8,128)(2,1)}, u32[]{:S(2)}, u32[]{:S(2)}) collective-permute-start(bf16[128,768]{1,0:T(8,128)(2,1)} %get-tuple-element.130), channel_id=1, source_target_pairs={{0,20},{4,16},{8,28},{12,24},{16,4},{20,0},{24,12},{28,8},{1,21},{... | collective-permute-start | bytes 589832 | tf_op jit(solution)/shard_map/ppermute | solution.py:30
  115.1 31.3 %collective-permute-start.11 = (bf16[128,768]{1,0:T(8,128)(2,1)}, bf16[128,768]{1,0:T(8,128)(2,1)}, u32[]{:S(2)}, u32[]{:S(2)}) collective-permute-start(bf16[128,768]{1,0:T(8,128)(2,1)} %get-tuple-element.129), channel_id=1, source_target_pairs={{0,24},{4,28},{8,16},{12,20},{16,8},{20,12},{24,0},{28,4},{1,25},{... | collective-permute-start | bytes 589832 | tf_op jit(solution)/shard_map/ppermute | solution.py:30
  115.4 45.4 %collective-permute-start.12 = (bf16[128,768]{1,0:T(8,128)(2,1)}, bf16[128,768]{1,0:T(8,128)(2,1)}, u32[]{:S(2)}, u32[]{:S(2)}) collective-permute-start(bf16[128,768]{1,0:T(8,128)(2,1)} %get-tuple-element.128), channel_id=1, source_target_pairs={{0,28},{4,24},{8,20},{12,16},{16,12},{20,8},{24,4},{28,0},{1,29},{... | collective-permute-start | bytes 589832 | tf_op jit(solution)/shard_map/ppermute | solution.py:30
  118.5 42.3 %collective-permute-start.6 = (bf16[128,768]{1,0:T(8,128)(2,1)}, bf16[128,768]{1,0:T(8,128)(2,1)}, u32[]{:S(2)}, u32[]{:S(2)}) collective-permute-start(bf16[128,768]{1,0:T(8,128)(2,1)} %get-tuple-element.134), channel_id=1, source_target_pairs={{0,4},{4,0},{8,12},{12,8},{16,20},{20,16},{24,28},{28,24},{1,5},{5... | collective-permute-start | bytes 589832 | tf_op jit(solution)/shard_map/ppermute | solution.py:30
  119.0 41.8 %collective-permute-start.7 = (bf16[128,768]{1,0:T(8,128)(2,1)}, bf16[128,768]{1,0:T(8,128)(2,1)}, u32[]{:S(2)}, u32[]{:S(2)}) collective-permute-start(bf16[128,768]{1,0:T(8,128)(2,1)} %get-tuple-element.133), channel_id=1, source_target_pairs={{0,8},{4,12},{8,0},{12,4},{16,24},{20,28},{24,16},{28,20},{1,9},{5... | collective-permute-start | bytes 589832 | tf_op jit(solution)/shard_map/ppermute | solution.py:30
  146.4 45.5 %collective-permute-start.9 = (bf16[128,768]{1,0:T(8,128)(2,1)}, bf16[128,768]{1,0:T(8,128)(2,1)}, u32[]{:S(2)}, u32[]{:S(2)}) collective-permute-start(bf16[128,768]{1,0:T(8,128)(2,1)} %get-tuple-element.131), channel_id=1, source_target_pairs={{0,16},{4,20},{8,24},{12,28},{16,0},{20,4},{24,8},{28,12},{1,17},{... | collective-permute-start | bytes 589832 | tf_op jit(solution)/shard_map/ppermute | solution.py:30
  230.8 24.9 %collective-permute-start.21 = (bf16[128,2048]{1,0:T(8,128)(2,1)S(1)}, bf16[128,2048]{1,0:T(8,128)(2,1)S(1)}, u32[]{:S(2)}, u32[]{:S(2)}) collective-permute-start(bf16[128,2048]{1,0:T(8,128)(2,1)S(1)} %get-tuple-element.119), channel_id=1, source_target_pairs={{0,2},{1,3},{2,0},{3,1},{4,6},{5,7},{6,4},{7,5},{8,10},{9,11},{10,... | collective-permute-start | bytes 1572872 | tf_op jit(solution)/shard_map/ppermute | solution.py:30
  258.8 26.0 %collective-permute-start.24 = (bf16[128,2048]{1,0:T(8,128)(2,1)S(1)}, bf16[128,2048]{1,0:T(8,128)(2,1)S(1)}, u32[]{:S(2)}, u32[]{:S(2)}) collective-permute-start(bf16[128,2048]{1,0:T(8,128)(2,1)S(1)} %add_convert_fusion.5), channel_id=1, source_target_pairs={{0,2},{1,3},{2,0},{3,1},{4,6},{5,7},{6,4},{7,5},{8,10},{9,11},{10,... | collective-permute-start | bytes 1572872 | tf_op jit(solution)/shard_map/ppermute | solution.py:30
  259.6 26.0 %collective-permute-start.25 = (bf16[128,2048]{1,0:T(8,128)(2,1)S(1)}, bf16[128,2048]{1,0:T(8,128)(2,1)}, u32[]{:S(2)}, u32[]{:S(2)}) collective-permute-start(bf16[128,2048]{1,0:T(8,128)(2,1)S(1)} %add_convert_fusion.5), channel_id=1, source_target_pairs={{0,3},{1,2},{2,1},{3,0},{4,7},{5,6},{6,5},{7,4},{8,11},{9,10},{10,... | collective-permute-start | bytes 1572872 | tf_op jit(solution)/shard_map/ppermute | solution.py:30
  261.1 36.6 %collective-permute-start.26 = (bf16[128,2048]{1,0:T(8,128)(2,1)}, bf16[128,2048]{1,0:T(8,128)(2,1)}, u32[]{:S(2)}, u32[]{:S(2)}) collective-permute-start(bf16[128,2048]{1,0:T(8,128)(2,1)} %bitcast.16), channel_id=1, source_target_pairs={{0,1},{1,0},{2,3},{3,2},{4,5},{5,4},{6,7},{7,6},{8,9},{9,8},{10,11... | collective-permute-start | bytes 1572872 | tf_op jit(solution)/shard_map/ppermute | solution.py:30
  262.3 43.1 %collective-permute-start.27 = (bf16[128,2048]{1,0:T(8,128)(2,1)}, bf16[128,2048]{1,0:T(8,128)(2,1)}, u32[]{:S(2)}, u32[]{:S(2)}) collective-permute-start(bf16[128,2048]{1,0:T(8,128)(2,1)} %bitcast.16), channel_id=1, source_target_pairs={{0,2},{1,3},{2,0},{3,1},{4,6},{5,7},{6,4},{7,5},{8,10},{9,11},{10,... | collective-permute-start | bytes 1572872 | tf_op jit(solution)/shard_map/ppermute | solution.py:30
  272.4 33.0 %collective-permute-start.28 = (bf16[128,2048]{1,0:T(8,128)(2,1)}, bf16[128,2048]{1,0:T(8,128)(2,1)}, u32[]{:S(2)}, u32[]{:S(2)}) collective-permute-start(bf16[128,2048]{1,0:T(8,128)(2,1)} %bitcast.16), channel_id=1, source_target_pairs={{0,3},{1,2},{2,1},{3,0},{4,7},{5,6},{6,5},{7,4},{8,11},{9,10},{10,... | collective-permute-start | bytes 1572872 | tf_op jit(solution)/shard_map/ppermute | solution.py:30
  330.7 25.1 %collective-permute-start.30 = (bf16[128,2048]{1,0:T(8,128)(2,1)S(1)}, bf16[128,2048]{1,0:T(8,128)(2,1)}, u32[]{:S(2)}, u32[]{:S(2)}) collective-permute-start(bf16[128,2048]{1,0:T(8,128)(2,1)S(1)} %get-tuple-element.116), channel_id=1, source_target_pairs={{0,2},{1,3},{2,0},{3,1},{4,6},{5,7},{6,4},{7,5},{8,10},{9,11},{10,... | collective-permute-start | bytes 1572872 | tf_op jit(solution)/shard_map/ppermute | solution.py:30
  394.3 218.0 %reduce-scatter.11.cloned.1.call-start = ((), (), s32[]{:S(2)}) async-start(), calls=%async_computation.10 | async-start | bytes 3604480 | tf_op jit(solution)/shard_map/reduce_scatter | solution.py:59
  403.7 217.1 %reduce-scatter.5.cloned.1.call-start = ((), (), s32[]{:S(2)}) async-start(), calls=%async_computation.7 | async-start | bytes 3932160 | tf_op jit(solution)/shard_map/reduce_scatter | solution.py:59
  442.8 33.8 %collective-permute-start.44 = (bf16[128,768]{1,0:T(8,128)(2,1)S(1)}, bf16[128,768]{1,0:T(8,128)(2,1)S(1)}, u32[]{:S(2)}, u32[]{:S(2)}) collective-permute-start(bf16[128,768]{1,0:T(8,128)(2,1)S(1)} %get-tuple-element.124), channel_id=1, source_target_pairs={{0,12},{4,8},{8,4},{12,0},{16,28},{20,24},{24,20},{28,16},{1,13},{... | collective-permute-start | bytes 589832 | tf_op jit(solution)/shard_map/ppermute | solution.py:30
  442.8 33.8 %collective-permute-start.45 = (bf16[128,768]{1,0:T(8,128)(2,1)S(1)}, bf16[128,768]{1,0:T(8,128)(2,1)S(1)}, u32[]{:S(2)}, u32[]{:S(2)}) collective-permute-start(bf16[128,768]{1,0:T(8,128)(2,1)S(1)} %get-tuple-element.123), channel_id=1, source_target_pairs={{0,16},{4,20},{8,24},{12,28},{16,0},{20,4},{24,8},{28,12},{1,17},{... | collective-permute-start | bytes 589832 | tf_op jit(solution)/shard_map/ppermute | solution.py:30
  444.6 38.8 %collective-permute-start.46 = (bf16[128,768]{1,0:T(8,128)(2,1)S(1)}, bf16[128,768]{1,0:T(8,128)(2,1)S(1)}, u32[]{:S(2)}, u32[]{:S(2)}) collective-permute-start(bf16[128,768]{1,0:T(8,128)(2,1)S(1)} %get-tuple-element.122), channel_id=1, source_target_pairs={{0,20},{4,16},{8,28},{12,24},{16,4},{20,0},{24,12},{28,8},{1,21},{... | collective-permute-start | bytes 589832 | tf_op jit(solution)/shard_map/ppermute | solution.py:30
  445.2 42.7 %collective-permute-start.47 = (bf16[128,768]{1,0:T(8,128)(2,1)S(1)}, bf16[128,768]{1,0:T(8,128)(2,1)S(1)}, u32[]{:S(2)}, u32[]{:S(2)}) collective-permute-start(bf16[128,768]{1,0:T(8,128)(2,1)S(1)} %get-tuple-element.121), channel_id=1, source_target_pairs={{0,24},{4,28},{8,16},{12,20},{16,8},{20,12},{24,0},{28,4},{1,25},{... | collective-permute-start | bytes 589832 | tf_op jit(solution)/shard_map/ppermute | solution.py:30
  463.0 32.8 %collective-permute-start.48 = (bf16[128,768]{1,0:T(8,128)(2,1)S(1)}, bf16[128,768]{1,0:T(8,128)(2,1)S(1)}, u32[]{:S(2)}, u32[]{:S(2)}) collective-permute-start(bf16[128,768]{1,0:T(8,128)(2,1)S(1)} %get-tuple-element.120), channel_id=1, source_target_pairs={{0,28},{4,24},{8,20},{12,16},{16,12},{20,8},{24,4},{28,0},{1,29},{... | collective-permute-start | bytes 589832 | tf_op jit(solution)/shard_map/ppermute | solution.py:30
  512.9 185.3 %reduce-scatter.9.cloned.1.call-start = ((), (), s32[]{:S(2)}) async-start(), calls=%async_computation.9 | async-start | bytes 7208960 | tf_op jit(solution)/shard_map/reduce_scatter | solution.py:59
  536.8 24.9 %collective-permute-start.53 = (bf16[128,2048]{1,0:T(8,128)(2,1)S(1)}, bf16[128,2048]{1,0:T(8,128)(2,1)S(1)}, u32[]{:S(2)}, u32[]{:S(2)}) collective-permute-start(bf16[128,2048]{1,0:T(8,128)(2,1)S(1)} %get-tuple-element.110), channel_id=1, source_target_pairs={{0,2},{1,3},{2,0},{3,1},{4,6},{5,7},{6,4},{7,5},{8,10},{9,11},{10,... | collective-permute-start | bytes 1572872 | tf_op jit(solution)/shard_map/ppermute | solution.py:30
  565.8 38.6 %collective-permute-start.49 = (bf16[128,2048]{1,0:T(8,128)(2,1)S(1)}, bf16[128,2048]{1,0:T(8,128)(2,1)S(1)}, u32[]{:S(2)}, u32[]{:S(2)}) collective-permute-start(bf16[128,2048]{1,0:T(8,128)(2,1)S(1)} %get-tuple-element.111), channel_id=1, source_target_pairs={{0,1},{1,0},{2,3},{3,2},{4,5},{5,4},{6,7},{7,6},{8,9},{9,8},{10,11... | collective-permute-start | bytes 1572872 | tf_op jit(solution)/shard_map/ppermute | solution.py:30
  567.0 37.4 %collective-permute-start.50 = (bf16[128,2048]{1,0:T(8,128)(2,1)S(1)}, bf16[128,2048]{1,0:T(8,128)(2,1)S(1)}, u32[]{:S(2)}, u32[]{:S(2)}) collective-permute-start(bf16[128,2048]{1,0:T(8,128)(2,1)S(1)} %get-tuple-element.113), channel_id=1, source_target_pairs={{0,2},{1,3},{2,0},{3,1},{4,6},{5,7},{6,4},{7,5},{8,10},{9,11},{10,... | collective-permute-start | bytes 1572872 | tf_op jit(solution)/shard_map/ppermute | solution.py:30
  567.8 36.5 %collective-permute-start.51 = (bf16[128,2048]{1,0:T(8,128)(2,1)S(1)}, bf16[128,2048]{1,0:T(8,128)(2,1)S(1)}, u32[]{:S(2)}, u32[]{:S(2)}) collective-permute-start(bf16[128,2048]{1,0:T(8,128)(2,1)S(1)} %get-tuple-element.112), channel_id=1, source_target_pairs={{0,3},{1,2},{2,1},{3,0},{4,7},{5,6},{6,5},{7,4},{8,11},{9,10},{10,... | collective-permute-start | bytes 1572872 | tf_op jit(solution)/shard_map/ppermute | solution.py:30
  (120 other events, 1542.0 us)
Sparse Core Ops, SparseCore 0:
  11.1 87.5 all-gather.3
  100.9 151.1 all-gather.5
  254.3 58.9 all-gather.7
  394.4 30.8 reduce-scatter.6
  428.0 81.8 reduce-scatter.10
  513.0 79.7 reduce-scatter.4
  595.1 103.0 reduce-scatter.8

commit v4 on v3

--- a/solution.py
+++ b/solution.py
@@ -51,11 +51,14 @@
     return value
 
 
-def chip_scatter(product, halves, axis):
-    count = lax.axis_size("ctx")
+def core_sum(product, halves):
     own, other = halves
     sent = product(other).astype(BF16)
-    total = (product(own) + swapped(sent, "ctx", 1).astype(F32)).astype(BF16)
+    return (product(own) + swapped(sent, "ctx", 1).astype(F32)).astype(BF16)
+
+
+def chip_scatter(total, axis):
+    count = lax.axis_size("ctx")
     return lax.psum_scatter(
         total,
         "ctx",
@@ -383,6 +386,42 @@
     )(me, matrix)
 
 
+def join_kernel(blocks, left_ref, rows_ref, other_ref, out_sum_ref, out_ref):
+    @pl.when(pl.program_id(0) < blocks)
+    def _():
+        kept = dot(left_ref[...], rows_ref[...]) + other_ref[...].astype(F32)
+        out_ref[...] = kept.astype(BF16)
+
+    @pl.when(pl.program_id(0) >= blocks)
+    def _():
+        out_ref[...] = out_sum_ref[...]
+
+
+def join(left, rows, other, out_sum, width):
+    half, count = left.shape
+    blocks = rows.shape[1] // width
+    total = blocks + out_sum.shape[1] // width
+    return pl.pallas_call(
+        functools.partial(join_kernel, blocks),
+        grid=(total,),
+        in_specs=[
+            pl.BlockSpec((half, count), lambda b: (0, 0)),
+            pl.BlockSpec((count, width), lambda b: (0, jnp.minimum(b, blocks - 1))),
+            pl.BlockSpec((half, width), lambda b: (0, jnp.minimum(b, blocks - 1))),
+            pl.BlockSpec((half, width), lambda b: (0, jnp.maximum(b - blocks, 0))),
+        ],
+        out_specs=pl.BlockSpec((half, width), lambda b: (0, b)),
+        out_shape=jax.ShapeDtypeStruct((half, total * width), BF16),
+        compiler_params=kernel_params(),
+        cost_estimate=pl.CostEstimate(
+            flops=2 * half * count * blocks * width,
+            bytes_accessed=4 * half * total * width,
+            transcendentals=0,
+        ),
+        name="join",
+    )(left, rows, other, out_sum)
+
+
 def pack_kernel(qkv_ref, out_ref, packed_ref):
     head_cols = qkv_ref.shape[2]
     for which in range(3):
@@ -401,6 +440,32 @@
         compiler_params=kernel_params(),
         name="pack",
     )(w_qkv, w_out)
+
+
+def adam_turned_kernel(share_ref, master_ref, first_ref, second_ref, *outs):
+    gradient = share_ref[...].astype(F32).T
+    updates = adam_step(
+        master_ref[...], gradient, first_ref[...], second_ref[...], weight_decay
+    )
+    for out_ref, value in zip(outs, (gradient, *updates)):
+        out_ref[...] = value
+
+
+def adam_turned(share, *arrays):
+    heads, own = arrays[0].shape
+    whole = pl.BlockSpec((heads, own), lambda step: (0, 0))
+    return pl.pallas_call(
+        adam_turned_kernel,
+        grid=(1,),
+        in_specs=[pl.BlockSpec((own, heads), lambda step: (0, 3))] + [whole] * 3,
+        out_specs=[whole] * 4,
+        out_shape=[jax.ShapeDtypeStruct((heads, own), F32)] * 4,
+        compiler_params=kernel_params(),
+        cost_estimate=pl.CostEstimate(
+            flops=0, bytes_accessed=30 * heads * own, transcendentals=0
+        ),
+        name="adam_turned",
+    )(share, *arrays)
 
 
 def adam_kernel(leading, share_ref, master_ref, first_ref, second_ref, *outs):
@@ -418,7 +483,8 @@
 
 def adam_parts(leading, share, *arrays):
     shape = arrays[0].shape
-    rows, width = share.shape
+    rows = share.shape[0]
+    width = arrays[0].size // rows
     step_rows = max(
         size
         for size in range(16, rows + 1, 16)
@@ -576,7 +642,10 @@
     gate_up = dot(gathered_two, gu_flat)
     gate_part = gate_up[:, :unit_cols]
     activated = (gate_part * jax.nn.sigmoid(gate_part) * gate_up[:, unit_cols:]).astype(BF16)
-    share_down = chip_scatter(lambda half: dot_rows(activated, half), halve(ctx_scalar, cot_all, ctx_size // 2), 1)
+    down_sum = core_sum(
+        lambda half: dot_rows(activated, half), halve(ctx_scalar, cot_all, ctx_size // 2)
+    )
+    share_down = chip_scatter(down_sum, 1)
 
     gate_up = lax.optimization_barrier(gate_up)
     gate_part = gate_up[:, :unit_cols]
@@ -586,7 +655,11 @@
     grad_gate = grad_act * up_part * sigmoid_gate * (1.0 + gate_part * (1.0 - sigmoid_gate))
     grad_up = grad_act * gate_part * sigmoid_gate
     grad_gate_up = jnp.concatenate([grad_gate, grad_up], axis=1).astype(BF16)
-    share_gu = chip_scatter(lambda half: dot_rows(half, grad_gate_up), halve(ctx_scalar, gathered_two, ctx_size // 2), 0)
+    gu_sum = core_sum(
+        lambda half: dot_rows(half, grad_gate_up),
+        halve(ctx_scalar, gathered_two, ctx_size // 2),
+    )
+    share_gu = chip_scatter(gu_sum, 0)
     normed_two_terms = dot_back(grad_gate_up, gu_flat).astype(BF16)
     grad_normed_two = scatter_sum(row_blocks(normed_two_terms), "wsh")
     grad_middle, grad_gain_two, grad_shift_two = norm_back(
@@ -594,7 +667,9 @@
     )
     grad_middle = grad_middle + cotangent[0].astype(F32)
     middle_all = jnp.concatenate(gather_rows(grad_middle.astype(BF16), "wsh"), axis=0)
-    share_out = chip_scatter(lambda half: dot_rows(attended, half), halve(ctx_scalar, middle_all, ctx_size // 2), 1)
+    out_sum = core_sum(
+        lambda half: dot_rows(half, attended), halve(ctx_scalar, middle_all, ctx_size // 2)
+    )
     grad_att = dot(middle_all, out_turned).astype(BF16)
 
     def exchange_grad(bits):
@@ -612,7 +687,10 @@
     grad_rows = place(
         places, [exchange_back(grad_own, bits) for bits in range(ctx_size)], groups, 3
     )
-    share_qkv = chip_scatter(lambda half: dot_rows(half, grad_rows), halve(ctx_scalar, gathered_one, ctx_size // 2), 0)
+    own_one, other_one = halve(ctx_scalar, gathered_one, ctx_size // 2)
+    sent_qkv = dot_rows(other_one, grad_rows).astype(BF16)
+    first_sum = join(own_one.T, grad_rows, swapped(sent_qkv, "ctx", 1), out_sum, width)
+    share_first = chip_scatter(first_sum, 0)
 
     late_activated, late_middle, _ = lax.optimization_barrier((activated, middle, grad_rows))
     ffn_terms = dot(late_activated, down_weight).astype(BF16)
@@ -648,7 +726,7 @@
         array.transpose(1, 0, 2)
         for array in adam_parts(
             True,
-            share_qkv,
+            share_first,
             *[array.transpose(1, 0, 2) for array in (w_qkv, first_qkv, second_qkv)],
         )
     ]
@@ -659,12 +737,9 @@
         array[0]
         for array in adam_parts(True, share_down, w_down[None], first_down[None], second_down[None])
     ]
-    share_out, new_out, new_first_out, new_second_out = [
-        array[0]
-        for array in adam_parts(
-            True, share_out, w_out[None], first_out[None], second_out[None]
-        )
-    ]
+    share_out, new_out, new_first_out, new_second_out = adam_turned(
+        share_first, w_out, first_out, second_out
+    )
     new_vecs, new_first_vecs, new_second_vecs = adam_step(
         norm_vecs, share_vecs, first_vecs, second_vecs, 0.0
     )

time: 724 us -> 724 us (level)
  waiting for transfers between devices: 391 us -> 382 us
  matrix products: 83.5 us -> 74.9 us
  Pallas kernels: 49 us -> 56.6 us
    dot_general x8 -> x7, matrix products: 34.9 us -> 24.5 us  [dot_rows(): lax.dot_general(left_side, right_side, (((0,), (0,)), ((), ())), preferre...]
    ppermute x64, waiting for transfers between devices: 263 us -> 253 us  [swapped(): lax.ppermute(value, axis, [(source, source ^ bits) for source in range(co...]
    pallas_call x0 -> x2, Pallas kernels: none -> 9.11 us  [the longest x1 7.32 us: join(): pl.pallas_call(functools.partial(join_kernel, blocks), grid=(total,), in_...]
    reduce_scatter x4 -> x3, waiting for transfers between devices: 68.1 us -> 76.1 us  [chip_scatter(): lax.psum_scatter(total, 'ctx', scatter_dimension=axis, tiled=True, axis_i...]
    all_gather x1, waiting for transfers between devices: 7.91 us -> 0.01 us  [local(): down_weight = lax.all_gather(w_down.astype(BF16), 'ctx', axis=1, tiled=True)]
    pallas_call x4 -> x3, Pallas kernels: 19.4 us -> 17.9 us  [adam_parts(): pl.pallas_call(functools.partial(adam_kernel, leading), grid=(rows // ste...]
    unnamed x163 -> x169, local copies, waits for them, and re-layouts: 32.7 us -> 33.9 us
  transfers between devices with their start and end apart: 71 -> 70, of which waited for: 39 -> 39; matrix products, arithmetic and copies ran while one was open for 14% -> 16% of each run, Pallas kernels for 5% -> 6%
where the time goes in v4:
time: 724 us; the launch traced here: 717 us
  waiting for transfers between devices  382 us (53%)
  starting transfers between devices  116 us (16%)
  matrix products  74.9 us (10%)
  Pallas kernels  56.6 us (8%)
  local copies, waits for them, and re-layouts  44.5 us (6%)
  other arithmetic  27.6 us (4%)
  between operations  15.6 us (2%)
    ppermute x64, waiting for transfers between devices, swapped(): lax.ppermute(value, axis, [(source, source ^ bits) for source in range(co...  253 us
    ppermute x64, starting transfers between devices, swapped(): lax.ppermute(value, axis, [(source, source ^ bits) for source in range(co...  116 us
    reduce_scatter x3, waiting for transfers between devices, chip_scatter(): lax.psum_scatter(total, 'ctx', scatter_dimension=axis, tiled=True, axis_i...  76.1 us
    all_gather x1, waiting for transfers between devices, local(): first_all = lax.all_gather(first_weights, 'ctx', axis=0, tiled=True)  51.9 us
    unnamed x169, local copies, waits for them, and re-layouts  33.9 us
    dot_general x4, matrix products, dot_back(): lax.dot_general(left_side, right_side, (((1,), (1,)), ((), ())), preferre...  29 us
    dot_general x7, matrix products, dot_rows(): lax.dot_general(left_side, right_side, (((0,), (0,)), ((), ())), preferre...  24.5 us
    dot_general x3, matrix products, dot(): return jnp.dot(left_side, right_side, preferred_element_type=F32)  21.4 us
  transfers between devices with their start and end apart: 70, of which 39 were waited for; matrix products, arithmetic and copies ran while one was open for 16% of the time, Pallas kernels for 6%

profile of v4, /device:TPU:0, one launch (start us, length us, event | category | flops | bytes accessed | tf_op | source)
XLA Modules:
  0.0 717.3 jit_solution(2843781023076160488)
XLA Ops:
  37.1 7.6 %collective-permute-done.5 = f32[8,2048]{1,0:T(8,128)} collective-permute-done((f32[8,2048]{1,0:T(8,128)}, f32[8,2048]{1,0:T(8,128)}, u32[]{:S(2)}, u32[]{:S(2)}) %collective-permute-start.5) | collective-permute-done | bytes 65568 | tf_op jit(solution)/shard_map/ppermute | solution.py:30
  46.8 51.9 %all-gather.4.cloned.1.call-done.refs_11_.refs_12_.refs_13_ = bf16[2048,2048]{1,0:T(8,128)(2,1)} async-done(((bf16[256,2048]{1,0:T(8,128)(2,1)}), bf16[2048,2048]{1,0:T(8,128)(2,1)}) %all-gather.4.cloned.1.call-update) | async-done | bytes 8388624 | tf_op jit(solution)/shard_map/all_gather | solution.py:580
  103.3 8.7 %project.1 = (bf16[512,2048]{1,0:T(8,128)(2,1)S(1)}, bf16[4,2,128,768]{3,2,1,0:T(8,128)(2,1)S(1)}) custom-call(bf16[128,2048]{1,0:T(8,128)(2,1)S(1)} %bitcast.85, bf16[128,2048]{1,0:T(8,128)(2,1)} %collective-permute-done.refs_1_, bf16[128,2048]{1,0:T(8,128)(2,1)} %collective-permute-done.1.refs_2_, bf16[128,2048]{1,0:T(8,128)(2,1)} %collective-permute-done.2.refs_3_, ...), custom_call_target="tpu_custom_call" | custom-call | flops 3221225472 | bytes 10485760 | tf_op jit(solution)/shard_map/project/pallas_call | solution.py:182
  119.0 27.3 %collective-permute-done.10.refs_5_ = bf16[128,768]{1,0:T(8,128)(2,1)} collective-permute-done((bf16[128,768]{1,0:T(8,128)(2,1)}, bf16[128,768]{1,0:T(8,128)(2,1)}, u32[]{:S(2)}, u32[]{:S(2)}) %collective-permute-start.10) | collective-permute-done | bytes 196640 | tf_op jit(solution)/shard_map/ppermute | solution.py:30
  146.4 13.4 %collective-permute-start.9 = (bf16[128,768]{1,0:T(8,128)(2,1)}, bf16[128,768]{1,0:T(8,128)(2,1)}, u32[]{:S(2)}, u32[]{:S(2)}) collective-permute-start(bf16[128,768]{1,0:T(8,128)(2,1)} %get-tuple-element.131), channel_id=1, source_target_pairs={{0,16},{4,20},{8,24},{12,28},{16,0},{20,4},{24,8},{28,12},{1,17},{... | collective-permute-start | bytes 589832 | tf_op jit(solution)/shard_map/ppermute | solution.py:30
  162.1 29.8 %collective-permute-done.9.refs_4_ = bf16[128,768]{1,0:T(8,128)(2,1)} collective-permute-done((bf16[128,768]{1,0:T(8,128)(2,1)}, bf16[128,768]{1,0:T(8,128)(2,1)}, u32[]{:S(2)}, u32[]{:S(2)}) %collective-permute-start.9) | collective-permute-done | bytes 196640 | tf_op jit(solution)/shard_map/ppermute | solution.py:30
  235.9 8.1 %collective-permute-done.20 = bf16[128,2048]{1,0:T(8,128)(2,1)S(1)} collective-permute-done((bf16[128,2048]{1,0:T(8,128)(2,1)S(1)}, bf16[128,2048]{1,0:T(8,128)(2,1)S(1)}, u32[]{:S(2)}, u32[]{:S(2)}) %collective-permute-start.20) | collective-permute-done | bytes 524320 | tf_op jit(solution)/shard_map/ppermute | solution.py:30
  246.5 10.3 %collective-permute-done.21 = bf16[128,2048]{1,0:T(8,128)(2,1)S(1)} collective-permute-done((bf16[128,2048]{1,0:T(8,128)(2,1)S(1)}, bf16[128,2048]{1,0:T(8,128)(2,1)S(1)}, u32[]{:S(2)}, u32[]{:S(2)}) %collective-permute-start.21) | collective-permute-done | bytes 524320 | tf_op jit(solution)/shard_map/ppermute | solution.py:30
  260.1 6.4 collective-permute-done.26
  269.0 10.3 %collective-permute-done.27 = bf16[128,2048]{1,0:T(8,128)(2,1)S(1)} collective-permute-done((bf16[128,2048]{1,0:T(8,128)(2,1)S(1)}, bf16[128,2048]{1,0:T(8,128)(2,1)S(1)}, u32[]{:S(2)}, u32[]{:S(2)}) %collective-permute-start.27) | collective-permute-done | bytes 524320 | tf_op jit(solution)/shard_map/ppermute | solution.py:30
  289.0 11.6 %collective-permute-done.24 = bf16[128,2048]{1,0:T(8,128)(2,1)S(1)} collective-permute-done((bf16[128,2048]{1,0:T(8,128)(2,1)S(1)}, bf16[128,2048]{1,0:T(8,128)(2,1)S(1)}, u32[]{:S(2)}, u32[]{:S(2)}) %collective-permute-start.24) | collective-permute-done | bytes 524320 | tf_op jit(solution)/shard_map/ppermute | solution.py:30
  301.4 10.5 %fusion.49 = f32[512,2816]{1,0:T(8,128)S(1)} fusion(bf16[2048,2816]{1,0:T(8,128)(2,1)} %all-gather.6.cloned.1.call-done, bf16[128,2048]{1,0:T(8,128)(2,1)} %collective-permute-done.25, bf16[128,2048]{1,0:T(8,128)(2,1)} %copy-done.61, bf16[128,2048]{1,0:T(8,128)(2,1)} %copy-done.60, bf16[128,2048]{1,0:T(8,128)(2,1)} %copy-done.54), kind=kOutput, calls=%fused_computation.136 | convolution fusion | flops 5913968640 | bytes 19398656 | tf_op jit(solution)/shard_map/dot_general | solution.py:123
  317.7 9.1 %fusion.7 = (bf16[512,1408]{1,0:T(8,128)(2,1)S(1)}, bf16[512,1408]{1,0:T(8,128)(2,1)S(1)}) fusion(f32[512,2816]{1,0:T(8,128)} %copy-done.50, bf16[1408,2048]{1,0:T(8,128)(2,1)} %all-gather.8.cloned.1.call-done, bf16[128,2048]{1,0:T(8,128)(2,1)} %copy-done.64, bf16[128,2048]{1,0:T(8,128)(2,1)} %copy-done.63, bf16[128,2048]{1,0:T(8,128)(2,1)} %copy-done.62, ...), kind=kOutput, calls=%fused_computation.14 | convolution fusion | flops 2970550272 | bytes 16515072 | tf_op jit(solution)/shard_map/dot_general | solution.py:117
  326.8 10.1 %convolution_convert_fusion.3 = bf16[512,2048]{1,0:T(8,128)(2,1)S(1)} fusion(bf16[2048,2816]{1,0:T(8,128)(2,1)} %all-gather.6.cloned.1.call-done, bf16[512,1408]{1,0:T(8,128)(2,1)S(1)} %get-tuple-element.107, bf16[512,1408]{1,0:T(8,128)(2,1)S(1)} %get-tuple-element.106), kind=kOutput, calls=%fused_computation.8 | convolution fusion | flops 5912395776 | bytes 16515072 | tf_op jit(solution)/shard_map/dot_general | solution.py:117
  342.9 11.6 %collective-permute-done.29 = bf16[128,2048]{1,0:T(8,128)(2,1)} collective-permute-done((bf16[128,2048]{1,0:T(8,128)(2,1)}, bf16[128,2048]{1,0:T(8,128)(2,1)}, u32[]{:S(2)}, u32[]{:S(2)}) %collective-permute-start.29) | collective-permute-done | bytes 524320 | tf_op jit(solution)/shard_map/ppermute | solution.py:30
  354.5 10.1 %collective-permute-done.30 = bf16[128,2048]{1,0:T(8,128)(2,1)} collective-permute-done((bf16[128,2048]{1,0:T(8,128)(2,1)}, bf16[128,2048]{1,0:T(8,128)(2,1)}, u32[]{:S(2)}, u32[]{:S(2)}) %collective-permute-start.30) | collective-permute-done | bytes 524320 | tf_op jit(solution)/shard_map/ppermute | solution.py:30
  385.7 10.2 %collective-permute-done.33 = bf16[128,2048]{1,0:T(8,128)(2,1)} collective-permute-done((bf16[128,2048]{1,0:T(8,128)(2,1)}, bf16[128,2048]{1,0:T(8,128)(2,1)}, u32[]{:S(2)}, u32[]{:S(2)}) %collective-permute-start.33) | collective-permute-done | bytes 524320 | tf_op jit(solution)/shard_map/ppermute | solution.py:30
  399.6 11.9 %collective-permute-start.36 = (bf16[128,256]{1,0:T(8,128)(2,1)S(1)}, bf16[128,256]{1,0:T(8,128)(2,1)S(1)}, u32[]{:S(2)}, u32[]{:S(2)}) collective-permute-start(bf16[128,256]{1,0:T(8,128)(2,1)S(1)} %get-tuple-element.142), channel_id=1, source_target_pairs={{0,8},{4,12},{8,0},{12,4},{16,24},{20,28},{24,16},{28,20},{1,9},{5... | collective-permute-start | bytes 196616 | tf_op jit(solution)/shard_map/ppermute | solution.py:30
  431.6 11.9 %attend_back.1 = (bf16[1024,768]{1,0:T(8,128)(2,1)}, f32[8,256]{1,0:T(8,128)S(1)}) custom-call(s32[1]{0:T(128)} %bitcast.1.me_ref, s32[1,1024]{1,0:T(1,128)S(1)} %constant_dynamic-slice_fusion.21.ids_row_ref, s32[1024,1]{1,0:T(8,128)S(1)} %copy-done.28, f32[1024,256]{1,0:T(8,128)S(1)} %get-tuple-element.161.cos_ref, ...), custom_call_target="tpu_custom_call" | custom-call | flops 5368709120 | bytes 4194304 | tf_op jit(solution)/shard_map/attend_back/pallas_call | solution.py:340
  446.0 9.8 %collective-permute-start.43 = (bf16[128,768]{1,0:T(8,128)(2,1)S(1)}, bf16[128,768]{1,0:T(8,128)(2,1)S(1)}, u32[]{:S(2)}, u32[]{:S(2)}) collective-permute-start(bf16[128,768]{1,0:T(8,128)(2,1)S(1)} %get-tuple-element.125), channel_id=1, source_target_pairs={{0,8},{4,12},{8,0},{12,4},{16,24},{20,28},{24,16},{28,20},{1,9},{5... | collective-permute-start | bytes 589832 | tf_op jit(solution)/shard_map/ppermute | solution.py:30
  460.7 8.5 %collective-permute-done.43.refs_2_ = bf16[128,768]{1,0:T(8,128)(2,1)S(1)} collective-permute-done((bf16[128,768]{1,0:T(8,128)(2,1)S(1)}, bf16[128,768]{1,0:T(8,128)(2,1)S(1)}, u32[]{:S(2)}, u32[]{:S(2)}) %collective-permute-start.43) | collective-permute-done | bytes 196640 | tf_op jit(solution)/shard_map/ppermute | solution.py:30
  472.1 12.6 %collective-permute-done.46.refs_5_ = bf16[128,768]{1,0:T(8,128)(2,1)S(1)} collective-permute-done((bf16[128,768]{1,0:T(8,128)(2,1)S(1)}, bf16[128,768]{1,0:T(8,128)(2,1)S(1)}, u32[]{:S(2)}, u32[]{:S(2)}) %collective-permute-start.46) | collective-permute-done | bytes 196640 | tf_op jit(solution)/shard_map/ppermute | solution.py:30
  499.2 7.3 %join.1 = bf16[1024,2048]{1,0:T(8,128)(2,1)} custom-call(bf16[1024,512]{1,0:T(8,128)(2,1)S(1)} %bitcast.89, bf16[512,1536]{1,0:T(8,128)(2,1)S(1)} %copy-done.7, bf16[1024,1536]{1,0:T(8,128)(2,1)} %collective-permute-done.55.other_ref, bf16[1024,512]{1,0:T(8,128)(2,1)S(1)} %add_convert_fusion.2.out_sum_ref), custom_call_target="tpu_custom_call" | custom-call | flops 1610612736 | bytes 8388608 | tf_op jit(solution)/shard_map/join/pallas_call | solution.py:404
  513.2 9.0 %collective-permute-done.57 = bf16[1024,2816]{1,0:T(8,128)(2,1)S(1)} collective-permute-done((bf16[1024,2816]{1,0:T(8,128)(2,1)S(1)}, bf16[1024,2816]{1,0:T(8,128)(2,1)S(1)}, u32[]{:S(2)}, u32[]{:S(2)}) %collective-permute-start.57) | collective-permute-done | bytes 5767200 | tf_op jit(solution)/shard_map/ppermute | solution.py:30
  527.3 6.8 fusion.2
  537.8 7.4 %convolution_convert_fusion.5 = bf16[512,2048]{1,0:T(8,128)(2,1)} fusion(bf16[512,1408]{1,0:T(8,128)(2,1)S(1)} %copy-done.59, bf16[1408,2048]{1,0:T(8,128)(2,1)} %all-gather.8.cloned.1.call-done), kind=kOutput, calls=%fused_computation.10 | convolution fusion | flops 2953838592 | bytes 9306112 | tf_op jit(solution)/shard_map/dot_general | solution.py:123
  549.1 11.8 %collective-permute-done.53 = bf16[128,2048]{1,0:T(8,128)(2,1)S(1)} collective-permute-done((bf16[128,2048]{1,0:T(8,128)(2,1)S(1)}, bf16[128,2048]{1,0:T(8,128)(2,1)S(1)}, u32[]{:S(2)}, u32[]{:S(2)}) %collective-permute-start.53) | collective-permute-done | bytes 524320 | tf_op jit(solution)/shard_map/ppermute | solution.py:30
  568.4 8.9 %collective-permute-start.60 = (f32[8,2048]{1,0:T(8,128)S(1)}, f32[8,2048]{1,0:T(8,128)S(1)}, u32[]{:S(2)}, u32[]{:S(2)}) collective-permute-start(f32[8,2048]{1,0:T(8,128)S(1)} %add.472), channel_id=1, source_target_pairs={{0,8},{4,12},{8,0},{12,4},{16,24},{20,28},{24,16},{28,20},{1,9},{5... | collective-permute-start | bytes 196616 | tf_op jit(solution)/shard_map/ppermute | solution.py:30
  577.3 6.5 collective-permute-done.60
  583.9 8.6 %collective-permute-done.61 = f32[8,2048]{1,0:T(8,128)S(1)} collective-permute-done((f32[8,2048]{1,0:T(8,128)S(1)}, f32[8,2048]{1,0:T(8,128)S(1)}, u32[]{:S(2)}, u32[]{:S(2)}) %collective-permute-start.61) | collective-permute-done | bytes 65568 | tf_op jit(solution)/shard_map/ppermute | solution.py:30
  621.8 76.0 %reduce-scatter.6.cloned.1.call-done.share_ref = bf16[256,2816]{1,0:T(8,128)(2,1)} async-done(((bf16[1024,2816]{1,0:T(8,128)(2,1)}), bf16[256,2816]{1,0:T(8,128)(2,1)}) %reduce-scatter.6.cloned.1.call-update) | async-done | bytes 1441808 | tf_op jit(solution)/shard_map/reduce_scatter | solution.py:62
  699.2 10.7 %adam.4 = (f32[256,2,1408]{2,1,0:T(2,128)}, f32[256,2,1408]{2,1,0:T(2,128)}, f32[256,2,1408]{2,1,0:T(2,128)}, f32[256,2,1408]{2,1,0:T(2,128)}) custom-call(bf16[256,2816]{1,0:T(8,128)(2,1)S(1)} %copy-done.18, f32[256,2,1408]{2,1,0:T(2,128)S(1)} %copy-done.3, f32[256,2,1408]{2,1,0:T(2,128)} %first_ref.3, f32[256,2,1408]{2,1,0:T(2,128)} %second_ref.3), custom_call_target="tpu_custom_call" | custom-call | bytes 21626880 | tf_op jit(solution)/shard_map/adam/pallas_call | solution.py:497
  (372 shorter events, 246.8 us)
Async XLA Ops:
  7.2 91.5 %all-gather.4.cloned.1.call-start = ((), (), s32[]{:S(2)}) async-start(), calls=%async_computation.3 | async-start | bytes 9437184 | tf_op jit(solution)/shard_map/all_gather | solution.py:580
  11.0 290.4 %all-gather.6.cloned.1.call-start = ((), (), s32[]{:S(2)}) async-start(), calls=%async_computation.4 | async-start | bytes 12976128 | tf_op jit(solution)/shard_map/all_gather | solution.py:582
  13.4 304.3 %all-gather.8.cloned.1.call-start = ((), (), s32[]{:S(2)}) async-start(), calls=%async_computation.5 | async-start | bytes 6488064 | tf_op jit(solution)/shard_map/all_gather | solution.py:583
  15.8 586.1 %reduce-scatter.8.cloned.1.call-start = ((), (), s32[]{:S(2)}) async-start(), calls=%async_computation.8 | async-start | bytes 3604480 | tf_op jit(solution)/shard_map/reduce_scatter | solution.py:62
  15.8 30.9 %collective-permute-start = (bf16[128,2048]{1,0:T(8,128)(2,1)S(1)}, bf16[128,2048]{1,0:T(8,128)(2,1)}, u32[]{:S(2)}, u32[]{:S(2)}) collective-permute-start(bf16[128,2048]{1,0:T(8,128)(2,1)S(1)} %bitcast.82), channel_id=1, source_target_pairs={{0,1},{1,0},{2,3},{3,2},{4,5},{5,4},{6,7},{7,6},{8,9},{9,8},{10,11... | collective-permute-start | bytes 1572872 | tf_op jit(solution)/shard_map/ppermute | solution.py:30
  18.9 27.9 %collective-permute-start.1 = (bf16[128,2048]{1,0:T(8,128)(2,1)S(1)}, bf16[128,2048]{1,0:T(8,128)(2,1)}, u32[]{:S(2)}, u32[]{:S(2)}) collective-permute-start(bf16[128,2048]{1,0:T(8,128)(2,1)S(1)} %bitcast.83), channel_id=1, source_target_pairs={{0,2},{1,3},{2,0},{3,1},{4,6},{5,7},{6,4},{7,5},{8,10},{9,11},{10,... | collective-permute-start | bytes 1572872 | tf_op jit(solution)/shard_map/ppermute | solution.py:30
  20.4 26.4 %collective-permute-start.2 = (bf16[128,2048]{1,0:T(8,128)(2,1)S(1)}, bf16[128,2048]{1,0:T(8,128)(2,1)}, u32[]{:S(2)}, u32[]{:S(2)}) collective-permute-start(bf16[128,2048]{1,0:T(8,128)(2,1)S(1)} %bitcast.84), channel_id=1, source_target_pairs={{0,3},{1,2},{2,1},{3,0},{4,7},{5,6},{6,5},{7,4},{8,11},{9,10},{10,... | collective-permute-start | bytes 1572872 | tf_op jit(solution)/shard_map/ppermute | solution.py:30
  114.4 32.0 %collective-permute-start.10 = (bf16[128,768]{1,0:T(8,128)(2,1)}, bf16[128,768]{1,0:T(8,128)(2,1)}, u32[]{:S(2)}, u32[]{:S(2)}) collective-permute-start(bf16[128,768]{1,0:T(8,128)(2,1)} %get-tuple-element.130), channel_id=1, source_target_pairs={{0,20},{4,16},{8,28},{12,24},{16,4},{20,0},{24,12},{28,8},{1,21},{... | collective-permute-start | bytes 589832 | tf_op jit(solution)/shard_map/ppermute | solution.py:30
  115.1 31.3 %collective-permute-start.11 = (bf16[128,768]{1,0:T(8,128)(2,1)}, bf16[128,768]{1,0:T(8,128)(2,1)}, u32[]{:S(2)}, u32[]{:S(2)}) collective-permute-start(bf16[128,768]{1,0:T(8,128)(2,1)} %get-tuple-element.129), channel_id=1, source_target_pairs={{0,24},{4,28},{8,16},{12,20},{16,8},{20,12},{24,0},{28,4},{1,25},{... | collective-permute-start | bytes 589832 | tf_op jit(solution)/shard_map/ppermute | solution.py:30
  115.4 45.5 %collective-permute-start.12 = (bf16[128,768]{1,0:T(8,128)(2,1)}, bf16[128,768]{1,0:T(8,128)(2,1)}, u32[]{:S(2)}, u32[]{:S(2)}) collective-permute-start(bf16[128,768]{1,0:T(8,128)(2,1)} %get-tuple-element.128), channel_id=1, source_target_pairs={{0,28},{4,24},{8,20},{12,16},{16,12},{20,8},{24,4},{28,0},{1,29},{... | collective-permute-start | bytes 589832 | tf_op jit(solution)/shard_map/ppermute | solution.py:30
  118.5 42.4 %collective-permute-start.6 = (bf16[128,768]{1,0:T(8,128)(2,1)}, bf16[128,768]{1,0:T(8,128)(2,1)}, u32[]{:S(2)}, u32[]{:S(2)}) collective-permute-start(bf16[128,768]{1,0:T(8,128)(2,1)} %get-tuple-element.134), channel_id=1, source_target_pairs={{0,4},{4,0},{8,12},{12,8},{16,20},{20,16},{24,28},{28,24},{1,5},{5... | collective-permute-start | bytes 589832 | tf_op jit(solution)/shard_map/ppermute | solution.py:30
  119.0 41.9 %collective-permute-start.7 = (bf16[128,768]{1,0:T(8,128)(2,1)}, bf16[128,768]{1,0:T(8,128)(2,1)}, u32[]{:S(2)}, u32[]{:S(2)}) collective-permute-start(bf16[128,768]{1,0:T(8,128)(2,1)} %get-tuple-element.133), channel_id=1, source_target_pairs={{0,8},{4,12},{8,0},{12,4},{16,24},{20,28},{24,16},{28,20},{1,9},{5... | collective-permute-start | bytes 589832 | tf_op jit(solution)/shard_map/ppermute | solution.py:30
  146.4 45.5 %collective-permute-start.9 = (bf16[128,768]{1,0:T(8,128)(2,1)}, bf16[128,768]{1,0:T(8,128)(2,1)}, u32[]{:S(2)}, u32[]{:S(2)}) collective-permute-start(bf16[128,768]{1,0:T(8,128)(2,1)} %get-tuple-element.131), channel_id=1, source_target_pairs={{0,16},{4,20},{8,24},{12,28},{16,0},{20,4},{24,8},{28,12},{1,17},{... | collective-permute-start | bytes 589832 | tf_op jit(solution)/shard_map/ppermute | solution.py:30
  230.8 26.0 %collective-permute-start.21 = (bf16[128,2048]{1,0:T(8,128)(2,1)S(1)}, bf16[128,2048]{1,0:T(8,128)(2,1)S(1)}, u32[]{:S(2)}, u32[]{:S(2)}) collective-permute-start(bf16[128,2048]{1,0:T(8,128)(2,1)S(1)} %get-tuple-element.119), channel_id=1, source_target_pairs={{0,2},{1,3},{2,0},{3,1},{4,6},{5,7},{6,4},{7,5},{8,10},{9,11},{10,... | collective-permute-start | bytes 1572872 | tf_op jit(solution)/shard_map/ppermute | solution.py:30
  232.3 24.6 %collective-permute-start.22 = (bf16[128,2048]{1,0:T(8,128)(2,1)S(1)}, bf16[128,2048]{1,0:T(8,128)(2,1)S(1)}, u32[]{:S(2)}, u32[]{:S(2)}) collective-permute-start(bf16[128,2048]{1,0:T(8,128)(2,1)S(1)} %get-tuple-element.118), channel_id=1, source_target_pairs={{0,3},{1,2},{2,1},{3,0},{4,7},{5,6},{6,5},{7,4},{8,11},{9,10},{10,... | collective-permute-start | bytes 1572872 | tf_op jit(solution)/shard_map/ppermute | solution.py:30
  232.7 33.8 %collective-permute-start.26 = (bf16[128,2048]{1,0:T(8,128)(2,1)S(1)}, bf16[128,2048]{1,0:T(8,128)(2,1)S(1)}, u32[]{:S(2)}, u32[]{:S(2)}) collective-permute-start(bf16[128,2048]{1,0:T(8,128)(2,1)S(1)} %bitcast.99), channel_id=1, source_target_pairs={{0,1},{1,0},{2,3},{3,2},{4,5},{5,4},{6,7},{7,6},{8,9},{9,8},{10,11... | collective-permute-start | bytes 1572872 | tf_op jit(solution)/shard_map/ppermute | solution.py:30
  234.3 45.0 %collective-permute-start.27 = (bf16[128,2048]{1,0:T(8,128)(2,1)S(1)}, bf16[128,2048]{1,0:T(8,128)(2,1)S(1)}, u32[]{:S(2)}, u32[]{:S(2)}) collective-permute-start(bf16[128,2048]{1,0:T(8,128)(2,1)S(1)} %bitcast.100), channel_id=1, source_target_pairs={{0,2},{1,3},{2,0},{3,1},{4,6},{5,7},{6,4},{7,5},{8,10},{9,11},{10,... | collective-permute-start | bytes 1572872 | tf_op jit(solution)/shard_map/ppermute | solution.py:30
  244.0 35.3 %collective-permute-start.28 = (bf16[128,2048]{1,0:T(8,128)(2,1)S(1)}, bf16[128,2048]{1,0:T(8,128)(2,1)S(1)}, u32[]{:S(2)}, u32[]{:S(2)}) collective-permute-start(bf16[128,2048]{1,0:T(8,128)(2,1)S(1)} %bitcast.101), channel_id=1, source_target_pairs={{0,3},{1,2},{2,1},{3,0},{4,7},{5,6},{6,5},{7,4},{8,11},{9,10},{10,... | collective-permute-start | bytes 1572872 | tf_op jit(solution)/shard_map/ppermute | solution.py:30
  258.0 31.0 %collective-permute-start.23 = (bf16[128,2048]{1,0:T(8,128)(2,1)S(1)}, bf16[128,2048]{1,0:T(8,128)(2,1)S(1)}, u32[]{:S(2)}, u32[]{:S(2)}) collective-permute-start(bf16[128,2048]{1,0:T(8,128)(2,1)S(1)} %add_convert_fusion.4), channel_id=1, source_target_pairs={{0,1},{1,0},{2,3},{3,2},{4,5},{5,4},{6,7},{7,6},{8,9},{9,8},{10,11... | collective-permute-start | bytes 1572872 | tf_op jit(solution)/shard_map/ppermute | solution.py:30
  259.0 41.6 %collective-permute-start.24 = (bf16[128,2048]{1,0:T(8,128)(2,1)S(1)}, bf16[128,2048]{1,0:T(8,128)(2,1)S(1)}, u32[]{:S(2)}, u32[]{:S(2)}) collective-permute-start(bf16[128,2048]{1,0:T(8,128)(2,1)S(1)} %add_convert_fusion.4), channel_id=1, source_target_pairs={{0,2},{1,3},{2,0},{3,1},{4,6},{5,7},{6,4},{7,5},{8,10},{9,11},{10,... | collective-permute-start | bytes 1572872 | tf_op jit(solution)/shard_map/ppermute | solution.py:30
  266.5 34.9 %collective-permute-start.25 = (bf16[128,2048]{1,0:T(8,128)(2,1)S(1)}, bf16[128,2048]{1,0:T(8,128)(2,1)}, u32[]{:S(2)}, u32[]{:S(2)}) collective-permute-start(bf16[128,2048]{1,0:T(8,128)(2,1)S(1)} %add_convert_fusion.4), channel_id=1, source_target_pairs={{0,3},{1,2},{2,1},{3,0},{4,7},{5,6},{6,5},{7,4},{8,11},{9,10},{10,... | collective-permute-start | bytes 1572872 | tf_op jit(solution)/shard_map/ppermute | solution.py:30
  317.7 56.4 %collective-permute-start.58 = (bf16[1408,1024]{1,0:T(8,128)(2,1)}, bf16[1408,1024]{1,0:T(8,128)(2,1)}, u32[]{:S(2)}, u32[]{:S(2)}) collective-permute-start(bf16[1408,1024]{1,0:T(8,128)(2,1)} %convolution_convert_fusion.1), channel_id=1, source_target_pairs={{0,4},{4,0},{8,12},{12,8},{16,20},{20,16},{24,28},{28,24},{1,5},{5... | collective-permute-start | bytes 8650760 | tf_op jit(solution)/shard_map/ppermute | solution.py:30
  340.0 24.6 %collective-permute-start.30 = (bf16[128,2048]{1,0:T(8,128)(2,1)}, bf16[128,2048]{1,0:T(8,128)(2,1)}, u32[]{:S(2)}, u32[]{:S(2)}) collective-permute-start(bf16[128,2048]{1,0:T(8,128)(2,1)} %get-tuple-element.116), channel_id=1, source_target_pairs={{0,2},{1,3},{2,0},{3,1},{4,6},{5,7},{6,4},{7,5},{8,10},{9,11},{10,... | collective-permute-start | bytes 1572872 | tf_op jit(solution)/shard_map/ppermute | solution.py:30
  341.4 24.8 %collective-permute-start.31 = (bf16[128,2048]{1,0:T(8,128)(2,1)}, bf16[128,2048]{1,0:T(8,128)(2,1)}, u32[]{:S(2)}, u32[]{:S(2)}) collective-permute-start(bf16[128,2048]{1,0:T(8,128)(2,1)} %get-tuple-element.115), channel_id=1, source_target_pairs={{0,3},{1,2},{2,1},{3,0},{4,7},{5,6},{6,5},{7,4},{8,11},{9,10},{10,... | collective-permute-start | bytes 1572872 | tf_op jit(solution)/shard_map/ppermute | solution.py:30
  379.2 231.5 %reduce-scatter.4.cloned.1.call-start = ((), (), s32[]{:S(2)}) async-start(), calls=%async_computation.6 | async-start | bytes 5242880 | tf_op jit(solution)/shard_map/reduce_scatter | solution.py:62
  458.3 26.5 %collective-permute-start.46 = (bf16[128,768]{1,0:T(8,128)(2,1)S(1)}, bf16[128,768]{1,0:T(8,128)(2,1)S(1)}, u32[]{:S(2)}, u32[]{:S(2)}) collective-permute-start(bf16[128,768]{1,0:T(8,128)(2,1)S(1)} %get-tuple-element.122), channel_id=1, source_target_pairs={{0,20},{4,16},{8,28},{12,24},{16,4},{20,0},{24,12},{28,8},{1,21},{... | collective-permute-start | bytes 589832 | tf_op jit(solution)/shard_map/ppermute | solution.py:30
  458.6 26.1 %collective-permute-start.47 = (bf16[128,768]{1,0:T(8,128)(2,1)S(1)}, bf16[128,768]{1,0:T(8,128)(2,1)S(1)}, u32[]{:S(2)}, u32[]{:S(2)}) collective-permute-start(bf16[128,768]{1,0:T(8,128)(2,1)S(1)} %get-tuple-element.121), channel_id=1, source_target_pairs={{0,24},{4,28},{8,16},{12,20},{16,8},{20,12},{24,0},{28,4},{1,25},{... | collective-permute-start | bytes 589832 | tf_op jit(solution)/shard_map/ppermute | solution.py:30
  506.6 191.3 %reduce-scatter.6.cloned.1.call-start = ((), (), s32[]{:S(2)}) async-start(), calls=%async_computation.7 | async-start | bytes 7208960 | tf_op jit(solution)/shard_map/reduce_scatter | solution.py:62
  535.9 25.0 %collective-permute-start.53 = (bf16[128,2048]{1,0:T(8,128)(2,1)S(1)}, bf16[128,2048]{1,0:T(8,128)(2,1)S(1)}, u32[]{:S(2)}, u32[]{:S(2)}) collective-permute-start(bf16[128,2048]{1,0:T(8,128)(2,1)S(1)} %get-tuple-element.110), channel_id=1, source_target_pairs={{0,2},{1,3},{2,0},{3,1},{4,6},{5,7},{6,4},{7,5},{8,10},{9,11},{10,... | collective-permute-start | bytes 1572872 | tf_op jit(solution)/shard_map/ppermute | solution.py:30
  564.8 33.3 %collective-permute-start.49 = (bf16[128,2048]{1,0:T(8,128)(2,1)S(1)}, bf16[128,2048]{1,0:T(8,128)(2,1)S(1)}, u32[]{:S(2)}, u32[]{:S(2)}) collective-permute-start(bf16[128,2048]{1,0:T(8,128)(2,1)S(1)} %get-tuple-element.111), channel_id=1, source_target_pairs={{0,1},{1,0},{2,3},{3,2},{4,5},{5,4},{6,7},{7,6},{8,9},{9,8},{10,11... | collective-permute-start | bytes 1572872 | tf_op jit(solution)/shard_map/ppermute | solution.py:30
  566.0 32.1 %collective-permute-start.50 = (bf16[128,2048]{1,0:T(8,128)(2,1)S(1)}, bf16[128,2048]{1,0:T(8,128)(2,1)S(1)}, u32[]{:S(2)}, u32[]{:S(2)}) collective-permute-start(bf16[128,2048]{1,0:T(8,128)(2,1)S(1)} %get-tuple-element.113), channel_id=1, source_target_pairs={{0,2},{1,3},{2,0},{3,1},{4,6},{5,7},{6,4},{7,5},{8,10},{9,11},{10,... | collective-permute-start | bytes 1572872 | tf_op jit(solution)/shard_map/ppermute | solution.py:30
  566.9 31.2 %collective-permute-start.51 = (bf16[128,2048]{1,0:T(8,128)(2,1)S(1)}, bf16[128,2048]{1,0:T(8,128)(2,1)S(1)}, u32[]{:S(2)}, u32[]{:S(2)}) collective-permute-start(bf16[128,2048]{1,0:T(8,128)(2,1)S(1)} %get-tuple-element.112), channel_id=1, source_target_pairs={{0,3},{1,2},{2,1},{3,0},{4,7},{5,6},{6,5},{7,4},{8,11},{9,10},{10,... | collective-permute-start | bytes 1572872 | tf_op jit(solution)/shard_map/ppermute | solution.py:30
  (122 other events, 1583.6 us)
Sparse Core Ops, SparseCore 0:
  11.1 87.5 all-gather.3
  100.9 151.1 all-gather.5
  254.3 58.9 all-gather.7
  379.3 74.2 reduce-scatter.7
  506.7 86.0 reduce-scatter.3
  595.0 102.8 reduce-scatter.5

commit v5 on v3

--- a/solution.py
+++ b/solution.py
@@ -616,7 +616,8 @@
 
     late_activated, late_middle, _ = lax.optimization_barrier((activated, middle, grad_rows))
     ffn_terms = dot(late_activated, down_weight).astype(BF16)
-    block_out = (late_middle + scatter_sum(row_blocks(ffn_terms), "wsh")).astype(BF16)
+    ffn_sum = scatter_sum(row_blocks(ffn_terms), "wsh")
+    block_out = (late_middle + ffn_sum).astype(BF16)
 
     normed_one_terms = dot_back(grad_rows, qkv_flat).astype(BF16)
     grad_normed_one = scatter_sum(row_blocks(normed_one_terms), "wsh")
@@ -641,8 +642,15 @@
         ],
         axis=0,
     )
-    vec_sums = butterfly(butterfly(vec_terms, "ctx"), "wsh")
-    share_vecs = lax.dynamic_slice_in_dim(vec_sums, ctx_place * own_rows, own_rows, 1).T[:, :6]
+    vec_share = scatter_sum(
+        [
+            lax.dynamic_slice_in_dim(vec_terms, (ctx_place ^ bits) * own_rows, own_rows, 1)
+            for bits in range(ctx_size)
+        ],
+        "ctx",
+    )
+    vec_share = scatter_sum([vec_share] * shard_count, "wsh")
+    share_vecs = vec_share.T[:, :6]
 
     share_qkv, new_qkv, new_first_qkv, new_second_qkv = [
         array.transpose(1, 0, 2)

time: 724 us -> 724 us (level)
    reduce_scatter x4, waiting for transfers between devices: 68.1 us -> 56.1 us  [chip_scatter(): lax.psum_scatter(total, 'ctx', scatter_dimension=axis, tiled=True, axis_i...]
    ppermute x64 -> x69, waiting for transfers between devices: 263 us -> 270 us  [swapped(): lax.ppermute(value, axis, [(source, source ^ bits) for source in range(co...]
    ppermute x64 -> x69, starting transfers between devices: 110 us -> 113 us  [swapped(): lax.ppermute(value, axis, [(source, source ^ bits) for source in range(co...]
    unnamed x163 -> x157, local copies, waits for them, and re-layouts: 32.7 us -> 32.7 us
  transfers between devices with their start and end apart: 71 -> 76, of which waited for: 39 -> 39; matrix products, arithmetic and copies ran while one was open for 14% -> 14% of each run, Pallas kernels for 5% -> 5%
where the time goes in v5:
time: 724 us; the launch traced here: 717 us
  waiting for transfers between devices  386 us (53%)
  starting transfers between devices  114 us (16%)
  matrix products  82.6 us (11%)
  Pallas kernels  49 us (7%)
  local copies, waits for them, and re-layouts  39.7 us (5%)
  other arithmetic  30.1 us (4%)
  between operations  15.8 us (2%)
    ppermute x69, waiting for transfers between devices, swapped(): lax.ppermute(value, axis, [(source, source ^ bits) for source in range(co...  270 us
    ppermute x69, starting transfers between devices, swapped(): lax.ppermute(value, axis, [(source, source ^ bits) for source in range(co...  113 us
    reduce_scatter x4, waiting for transfers between devices, chip_scatter(): lax.psum_scatter(total, 'ctx', scatter_dimension=axis, tiled=True, axis_i...  56.1 us
    all_gather x1, waiting for transfers between devices, local(): first_all = lax.all_gather(first_weights, 'ctx', axis=0, tiled=True)  51.9 us
    dot_general x8, matrix products, dot_rows(): lax.dot_general(left_side, right_side, (((0,), (0,)), ((), ())), preferre...  34.9 us
    unnamed x157, local copies, waits for them, and re-layouts  32.7 us
    dot_general x4, matrix products, dot_back(): lax.dot_general(left_side, right_side, (((1,), (1,)), ((), ())), preferre...  25.4 us
    dot_general x3, matrix products, dot(): return jnp.dot(left_side, right_side, preferred_element_type=F32)  22.4 us
  transfers between devices with their start and end apart: 76, of which 39 were waited for; matrix products, arithmetic and copies ran while one was open for 14% of the time, Pallas kernels for 5%

profile of v5, /device:TPU:0, one launch (start us, length us, event | category | flops | bytes accessed | tf_op | source)
XLA Modules:
  0.0 717.4 jit_solution(14021467419099924724)
XLA Ops:
  37.1 7.6 %collective-permute-done.5 = f32[8,2048]{1,0:T(8,128)} collective-permute-done((f32[8,2048]{1,0:T(8,128)}, f32[8,2048]{1,0:T(8,128)}, u32[]{:S(2)}, u32[]{:S(2)}) %collective-permute-start.5) | collective-permute-done | bytes 65568 | tf_op jit(solution)/shard_map/ppermute | solution.py:30
  46.8 51.9 %all-gather.4.cloned.1.call-done.refs_11_.refs_12_.refs_13_ = bf16[2048,2048]{1,0:T(8,128)(2,1)} async-done(((bf16[256,2048]{1,0:T(8,128)(2,1)}), bf16[2048,2048]{1,0:T(8,128)(2,1)}) %all-gather.4.cloned.1.call-update) | async-done | bytes 8388624 | tf_op jit(solution)/shard_map/all_gather | solution.py:514
  103.3 8.7 %project.1 = (bf16[512,2048]{1,0:T(8,128)(2,1)S(1)}, bf16[4,2,128,768]{3,2,1,0:T(8,128)(2,1)S(1)}) custom-call(bf16[128,2048]{1,0:T(8,128)(2,1)S(1)} %bitcast.93, bf16[128,2048]{1,0:T(8,128)(2,1)} %collective-permute-done.refs_1_, bf16[128,2048]{1,0:T(8,128)(2,1)} %collective-permute-done.1.refs_2_, bf16[128,2048]{1,0:T(8,128)(2,1)} %collective-permute-done.2.refs_3_, ...), custom_call_target="tpu_custom_call" | custom-call | flops 3221225472 | bytes 10485760 | tf_op jit(solution)/shard_map/project/pallas_call | solution.py:179
  119.0 27.4 %collective-permute-done.10.refs_5_ = bf16[128,768]{1,0:T(8,128)(2,1)} collective-permute-done((bf16[128,768]{1,0:T(8,128)(2,1)}, bf16[128,768]{1,0:T(8,128)(2,1)}, u32[]{:S(2)}, u32[]{:S(2)}) %collective-permute-start.10) | collective-permute-done | bytes 196640 | tf_op jit(solution)/shard_map/ppermute | solution.py:30
  146.4 13.4 %collective-permute-start.9 = (bf16[128,768]{1,0:T(8,128)(2,1)}, bf16[128,768]{1,0:T(8,128)(2,1)}, u32[]{:S(2)}, u32[]{:S(2)}) collective-permute-start(bf16[128,768]{1,0:T(8,128)(2,1)} %get-tuple-element.131), channel_id=1, source_target_pairs={{0,16},{4,20},{8,24},{12,28},{16,0},{20,4},{24,8},{28,12},{1,17},{... | collective-permute-start | bytes 589832 | tf_op jit(solution)/shard_map/ppermute | solution.py:30
  162.1 29.8 %collective-permute-done.9.refs_4_ = bf16[128,768]{1,0:T(8,128)(2,1)} collective-permute-done((bf16[128,768]{1,0:T(8,128)(2,1)}, bf16[128,768]{1,0:T(8,128)(2,1)}, u32[]{:S(2)}, u32[]{:S(2)}) %collective-permute-start.9) | collective-permute-done | bytes 196640 | tf_op jit(solution)/shard_map/ppermute | solution.py:30
  232.8 11.1 %collective-permute-done.20 = bf16[128,2048]{1,0:T(8,128)(2,1)S(1)} collective-permute-done((bf16[128,2048]{1,0:T(8,128)(2,1)S(1)}, bf16[128,2048]{1,0:T(8,128)(2,1)S(1)}, u32[]{:S(2)}, u32[]{:S(2)}) %collective-permute-start.20) | collective-permute-done | bytes 524320 | tf_op jit(solution)/shard_map/ppermute | solution.py:30
  244.0 11.7 %collective-permute-done.21 = bf16[128,2048]{1,0:T(8,128)(2,1)S(1)} collective-permute-done((bf16[128,2048]{1,0:T(8,128)(2,1)S(1)}, bf16[128,2048]{1,0:T(8,128)(2,1)S(1)}, u32[]{:S(2)}, u32[]{:S(2)}) %collective-permute-start.21) | collective-permute-done | bytes 524320 | tf_op jit(solution)/shard_map/ppermute | solution.py:30
  263.1 9.3 %collective-permute-done.23 = bf16[128,2048]{1,0:T(8,128)(2,1)S(1)} collective-permute-done((bf16[128,2048]{1,0:T(8,128)(2,1)S(1)}, bf16[128,2048]{1,0:T(8,128)(2,1)S(1)}, u32[]{:S(2)}, u32[]{:S(2)}) %collective-permute-start.23) | collective-permute-done | bytes 524320 | tf_op jit(solution)/shard_map/ppermute | solution.py:30
  273.9 11.0 %collective-permute-done.24 = bf16[128,2048]{1,0:T(8,128)(2,1)S(1)} collective-permute-done((bf16[128,2048]{1,0:T(8,128)(2,1)S(1)}, bf16[128,2048]{1,0:T(8,128)(2,1)S(1)}, u32[]{:S(2)}, u32[]{:S(2)}) %collective-permute-start.24) | collective-permute-done | bytes 524320 | tf_op jit(solution)/shard_map/ppermute | solution.py:30
  285.6 12.1 %fusion.54 = f32[512,2816]{1,0:T(8,128)} fusion(bf16[2048,2816]{1,0:T(8,128)(2,1)} %all-gather.6.cloned.1.call-done, bf16[128,2048]{1,0:T(8,128)(2,1)} %collective-permute-done.25, bf16[128,2048]{1,0:T(8,128)(2,1)} %copy-done.54, bf16[128,2048]{1,0:T(8,128)(2,1)} %copy-done.52, bf16[128,2048]{1,0:T(8,128)(2,1)} %copy-done.47), kind=kOutput, calls=%fused_computation.149 | convolution fusion | flops 5913968640 | bytes 19398656 | tf_op jit(solution)/shard_map/dot_general | solution.py:120
  297.8 7.6 %collective-permute-done.27 = bf16[128,2048]{1,0:T(8,128)(2,1)} collective-permute-done((bf16[128,2048]{1,0:T(8,128)(2,1)}, bf16[128,2048]{1,0:T(8,128)(2,1)}, u32[]{:S(2)}, u32[]{:S(2)}) %collective-permute-start.27) | collective-permute-done | bytes 524320 | tf_op jit(solution)/shard_map/ppermute | solution.py:30
  305.4 7.9 %all-gather.8.cloned.1.call-done = bf16[1408,2048]{1,0:T(8,128)(2,1)} async-done(((bf16[1408,256]{1,0:T(8,128)(2,1)}), bf16[1408,2048]{1,0:T(8,128)(2,1)}) %all-gather.8.cloned.1.call-update) | async-done | bytes 5767184 | tf_op jit(solution)/shard_map/all_gather | solution.py:517
  313.3 9.2 %fusion.7 = (bf16[512,1408]{1,0:T(8,128)(2,1)S(1)}, bf16[512,1408]{1,0:T(8,128)(2,1)S(1)}) fusion(f32[512,2816]{1,0:T(8,128)} %fusion.54, bf16[1408,2048]{1,0:T(8,128)(2,1)} %all-gather.8.cloned.1.call-done, bf16[128,2048]{1,0:T(8,128)(2,1)} %collective-permute-done.28, bf16[128,2048]{1,0:T(8,128)(2,1)} %collective-permute-done.27, ...), kind=kOutput, calls=%fused_computation.15 | convolution fusion | flops 2970550272 | bytes 16515072 | tf_op jit(solution)/shard_map/dot_general | solution.py:114
  334.8 9.2 %collective-permute-done.29 = bf16[128,2048]{1,0:T(8,128)(2,1)S(1)} collective-permute-done((bf16[128,2048]{1,0:T(8,128)(2,1)S(1)}, bf16[128,2048]{1,0:T(8,128)(2,1)S(1)}, u32[]{:S(2)}, u32[]{:S(2)}) %collective-permute-start.29) | collective-permute-done | bytes 524320 | tf_op jit(solution)/shard_map/ppermute | solution.py:30
  344.0 11.8 %collective-permute-done.30 = bf16[128,2048]{1,0:T(8,128)(2,1)} collective-permute-done((bf16[128,2048]{1,0:T(8,128)(2,1)S(1)}, bf16[128,2048]{1,0:T(8,128)(2,1)}, u32[]{:S(2)}, u32[]{:S(2)}) %collective-permute-start.30) | collective-permute-done | bytes 524320 | tf_op jit(solution)/shard_map/ppermute | solution.py:30
  364.8 10.5 %collective-permute-done.32 = bf16[128,2048]{1,0:T(8,128)(2,1)S(1)} collective-permute-done((bf16[128,2048]{1,0:T(8,128)(2,1)S(1)}, bf16[128,2048]{1,0:T(8,128)(2,1)S(1)}, u32[]{:S(2)}, u32[]{:S(2)}) %collective-permute-start.32) | collective-permute-done | bytes 524320 | tf_op jit(solution)/shard_map/ppermute | solution.py:30
  375.2 10.6 %collective-permute-done.33 = bf16[128,2048]{1,0:T(8,128)(2,1)S(1)} collective-permute-done((bf16[128,2048]{1,0:T(8,128)(2,1)S(1)}, bf16[128,2048]{1,0:T(8,128)(2,1)S(1)}, u32[]{:S(2)}, u32[]{:S(2)}) %collective-permute-start.33) | collective-permute-done | bytes 524320 | tf_op jit(solution)/shard_map/ppermute | solution.py:30
  426.5 11.9 %attend_back.1 = (bf16[1024,768]{1,0:T(8,128)(2,1)}, f32[8,256]{1,0:T(8,128)S(1)}) custom-call(s32[1]{0:T(128)} %bitcast.1.me_ref, s32[1,1024]{1,0:T(1,128)S(1)} %constant_dynamic-slice_fusion.27.ids_row_ref, s32[1024,1]{1,0:T(8,128)S(1)} %copy-done.25, f32[1024,256]{1,0:T(8,128)S(1)} %get-tuple-element.168.cos_ref, ...), custom_call_target="tpu_custom_call" | custom-call | flops 5368709120 | bytes 4194304 | tf_op jit(solution)/shard_map/attend_back/pallas_call | solution.py:337
  446.9 16.1 %collective-permute-done.43.refs_2_ = bf16[128,768]{1,0:T(8,128)(2,1)S(1)} collective-permute-done((bf16[128,768]{1,0:T(8,128)(2,1)S(1)}, bf16[128,768]{1,0:T(8,128)(2,1)S(1)}, u32[]{:S(2)}, u32[]{:S(2)}) %collective-permute-start.43) | collective-permute-done | bytes 196640 | tf_op jit(solution)/shard_map/ppermute | solution.py:30
  465.9 10.7 %collective-permute-done.44.refs_3_ = bf16[128,768]{1,0:T(8,128)(2,1)S(1)} collective-permute-done((bf16[128,768]{1,0:T(8,128)(2,1)S(1)}, bf16[128,768]{1,0:T(8,128)(2,1)S(1)}, u32[]{:S(2)}, u32[]{:S(2)}) %collective-permute-start.44) | collective-permute-done | bytes 196640 | tf_op jit(solution)/shard_map/ppermute | solution.py:30
  476.6 6.7 collective-permute-done.46.refs_5_
  487.9 7.8 %collective-permute-done.48.refs_7_ = bf16[128,768]{1,0:T(8,128)(2,1)S(1)} collective-permute-done((bf16[128,768]{1,0:T(8,128)(2,1)S(1)}, bf16[128,768]{1,0:T(8,128)(2,1)S(1)}, u32[]{:S(2)}, u32[]{:S(2)}) %collective-permute-start.48) | collective-permute-done | bytes 196640 | tf_op jit(solution)/shard_map/ppermute | solution.py:30
  502.4 6.7 convolution_convert_fusion
  518.8 9.5 %add_convert_fusion = bf16[1024,2816]{1,0:T(8,128)(2,1)} fusion(bf16[1024,2816]{1,0:T(8,128)(2,1)} %collective-permute-done.57, bf16[512,1024]{1,0:T(8,128)(2,1)} %copy-done.38, bf16[512,1408]{1,0:T(8,128)(2,1)} %copy-done.75, bf16[512,1408]{1,0:T(8,128)(2,1)} %copy-done.73), kind=kOutput, calls=%fused_computation | convolution fusion | flops 2967207936 | bytes 15466496 | tf_op jit(solution)/shard_map/dot_general | solution.py:108
  528.5 6.7 fusion.2
  538.9 6.7 convolution_convert_fusion.5
  550.2 11.6 %collective-permute-done.53 = bf16[128,2048]{1,0:T(8,128)(2,1)S(1)} collective-permute-done((bf16[128,2048]{1,0:T(8,128)(2,1)S(1)}, bf16[128,2048]{1,0:T(8,128)(2,1)S(1)}, u32[]{:S(2)}, u32[]{:S(2)}) %collective-permute-start.53) | collective-permute-done | bytes 524320 | tf_op jit(solution)/shard_map/ppermute | solution.py:30
  564.1 21.5 %collective-permute-start.60 = (f32[8,256]{1,0:T(8,128)S(1)}, f32[8,256]{1,0:T(8,128)S(1)}, u32[]{:S(2)}, u32[]{:S(2)}) collective-permute-start(f32[8,256]{1,0:T(8,128)S(1)} %get-tuple-element.159), channel_id=1, source_target_pairs={{0,8},{4,12},{8,0},{12,4},{16,24},{20,28},{24,16},{28,20},{1,9},{5... | collective-permute-start | bytes 24584 | tf_op jit(solution)/shard_map/ppermute | solution.py:30
  605.9 9.1 %collective-permute-done.50 = bf16[128,2048]{1,0:T(8,128)(2,1)S(1)} collective-permute-done((bf16[128,2048]{1,0:T(8,128)(2,1)}, bf16[128,2048]{1,0:T(8,128)(2,1)S(1)}, u32[]{:S(2)}, u32[]{:S(2)}) %collective-permute-start.50) | collective-permute-done | bytes 524320 | tf_op jit(solution)/shard_map/ppermute | solution.py:30
  641.9 56.1 %reduce-scatter.9.cloned.1.call-done.share_ref = bf16[256,2816]{1,0:T(8,128)(2,1)} async-done(((bf16[1024,2816]{1,0:T(8,128)(2,1)}), bf16[256,2816]{1,0:T(8,128)(2,1)}) %reduce-scatter.9.cloned.1.call-update) | async-done | bytes 1441808 | tf_op jit(solution)/shard_map/reduce_scatter | solution.py:59
  699.3 10.7 %adam.6 = (f32[256,2,1408]{2,1,0:T(2,128)}, f32[256,2,1408]{2,1,0:T(2,128)}, f32[256,2,1408]{2,1,0:T(2,128)}, f32[256,2,1408]{2,1,0:T(2,128)}) custom-call(bf16[256,2816]{1,0:T(8,128)(2,1)S(1)} %copy-done.15, f32[256,2,1408]{2,1,0:T(2,128)S(1)} %copy-done.3, f32[256,2,1408]{2,1,0:T(2,128)} %first_ref.1, f32[256,2,1408]{2,1,0:T(2,128)} %second_ref.1), custom_call_target="tpu_custom_call" | custom-call | bytes 21626880 | tf_op jit(solution)/shard_map/adam/pallas_call | solution.py:431
  (371 shorter events, 248.8 us)
Async XLA Ops:
  7.2 91.5 %all-gather.4.cloned.1.call-start = ((), (), s32[]{:S(2)}) async-start(), calls=%async_computation.4 | async-start | bytes 9437184 | tf_op jit(solution)/shard_map/all_gather | solution.py:514
  11.0 274.6 %all-gather.6.cloned.1.call-start = ((), (), s32[]{:S(2)}) async-start(), calls=%async_computation.5 | async-start | bytes 12976128 | tf_op jit(solution)/shard_map/all_gather | solution.py:516
  13.4 299.9 %all-gather.8.cloned.1.call-start = ((), (), s32[]{:S(2)}) async-start(), calls=%async_computation.6 | async-start | bytes 6488064 | tf_op jit(solution)/shard_map/all_gather | solution.py:517
  15.8 603.7 %reduce-scatter.7.cloned.1.call-start = ((), (), s32[]{:S(2)}) async-start(), calls=%async_computation.8 | async-start | bytes 1310720 | tf_op jit(solution)/shard_map/reduce_scatter | solution.py:59
  15.8 30.9 %collective-permute-start = (bf16[128,2048]{1,0:T(8,128)(2,1)S(1)}, bf16[128,2048]{1,0:T(8,128)(2,1)}, u32[]{:S(2)}, u32[]{:S(2)}) collective-permute-start(bf16[128,2048]{1,0:T(8,128)(2,1)S(1)} %bitcast.90), channel_id=1, source_target_pairs={{0,1},{1,0},{2,3},{3,2},{4,5},{5,4},{6,7},{7,6},{8,9},{9,8},{10,11... | collective-permute-start | bytes 1572872 | tf_op jit(solution)/shard_map/ppermute | solution.py:30
  18.9 27.9 %collective-permute-start.1 = (bf16[128,2048]{1,0:T(8,128)(2,1)S(1)}, bf16[128,2048]{1,0:T(8,128)(2,1)}, u32[]{:S(2)}, u32[]{:S(2)}) collective-permute-start(bf16[128,2048]{1,0:T(8,128)(2,1)S(1)} %bitcast.91), channel_id=1, source_target_pairs={{0,2},{1,3},{2,0},{3,1},{4,6},{5,7},{6,4},{7,5},{8,10},{9,11},{10,... | collective-permute-start | bytes 1572872 | tf_op jit(solution)/shard_map/ppermute | solution.py:30
  20.4 26.4 %collective-permute-start.2 = (bf16[128,2048]{1,0:T(8,128)(2,1)S(1)}, bf16[128,2048]{1,0:T(8,128)(2,1)}, u32[]{:S(2)}, u32[]{:S(2)}) collective-permute-start(bf16[128,2048]{1,0:T(8,128)(2,1)S(1)} %bitcast.92), channel_id=1, source_target_pairs={{0,3},{1,2},{2,1},{3,0},{4,7},{5,6},{6,5},{7,4},{8,11},{9,10},{10,... | collective-permute-start | bytes 1572872 | tf_op jit(solution)/shard_map/ppermute | solution.py:30
  114.4 32.0 %collective-permute-start.10 = (bf16[128,768]{1,0:T(8,128)(2,1)}, bf16[128,768]{1,0:T(8,128)(2,1)}, u32[]{:S(2)}, u32[]{:S(2)}) collective-permute-start(bf16[128,768]{1,0:T(8,128)(2,1)} %get-tuple-element.130), channel_id=1, source_target_pairs={{0,20},{4,16},{8,28},{12,24},{16,4},{20,0},{24,12},{28,8},{1,21},{... | collective-permute-start | bytes 589832 | tf_op jit(solution)/shard_map/ppermute | solution.py:30
  115.1 31.3 %collective-permute-start.11 = (bf16[128,768]{1,0:T(8,128)(2,1)}, bf16[128,768]{1,0:T(8,128)(2,1)}, u32[]{:S(2)}, u32[]{:S(2)}) collective-permute-start(bf16[128,768]{1,0:T(8,128)(2,1)} %get-tuple-element.129), channel_id=1, source_target_pairs={{0,24},{4,28},{8,16},{12,20},{16,8},{20,12},{24,0},{28,4},{1,25},{... | collective-permute-start | bytes 589832 | tf_op jit(solution)/shard_map/ppermute | solution.py:30
  115.4 45.4 %collective-permute-start.12 = (bf16[128,768]{1,0:T(8,128)(2,1)}, bf16[128,768]{1,0:T(8,128)(2,1)}, u32[]{:S(2)}, u32[]{:S(2)}) collective-permute-start(bf16[128,768]{1,0:T(8,128)(2,1)} %get-tuple-element.128), channel_id=1, source_target_pairs={{0,28},{4,24},{8,20},{12,16},{16,12},{20,8},{24,4},{28,0},{1,29},{... | collective-permute-start | bytes 589832 | tf_op jit(solution)/shard_map/ppermute | solution.py:30
  118.5 42.3 %collective-permute-start.6 = (bf16[128,768]{1,0:T(8,128)(2,1)}, bf16[128,768]{1,0:T(8,128)(2,1)}, u32[]{:S(2)}, u32[]{:S(2)}) collective-permute-start(bf16[128,768]{1,0:T(8,128)(2,1)} %get-tuple-element.134), channel_id=1, source_target_pairs={{0,4},{4,0},{8,12},{12,8},{16,20},{20,16},{24,28},{28,24},{1,5},{5... | collective-permute-start | bytes 589832 | tf_op jit(solution)/shard_map/ppermute | solution.py:30
  119.0 41.8 %collective-permute-start.7 = (bf16[128,768]{1,0:T(8,128)(2,1)}, bf16[128,768]{1,0:T(8,128)(2,1)}, u32[]{:S(2)}, u32[]{:S(2)}) collective-permute-start(bf16[128,768]{1,0:T(8,128)(2,1)} %get-tuple-element.133), channel_id=1, source_target_pairs={{0,8},{4,12},{8,0},{12,4},{16,24},{20,28},{24,16},{28,20},{1,9},{5... | collective-permute-start | bytes 589832 | tf_op jit(solution)/shard_map/ppermute | solution.py:30
  146.4 45.5 %collective-permute-start.9 = (bf16[128,768]{1,0:T(8,128)(2,1)}, bf16[128,768]{1,0:T(8,128)(2,1)}, u32[]{:S(2)}, u32[]{:S(2)}) collective-permute-start(bf16[128,768]{1,0:T(8,128)(2,1)} %get-tuple-element.131), channel_id=1, source_target_pairs={{0,16},{4,20},{8,24},{12,28},{16,0},{20,4},{24,8},{28,12},{1,17},{... | collective-permute-start | bytes 589832 | tf_op jit(solution)/shard_map/ppermute | solution.py:30
  230.8 24.9 %collective-permute-start.21 = (bf16[128,2048]{1,0:T(8,128)(2,1)S(1)}, bf16[128,2048]{1,0:T(8,128)(2,1)S(1)}, u32[]{:S(2)}, u32[]{:S(2)}) collective-permute-start(bf16[128,2048]{1,0:T(8,128)(2,1)S(1)} %get-tuple-element.119), channel_id=1, source_target_pairs={{0,2},{1,3},{2,0},{3,1},{4,6},{5,7},{6,4},{7,5},{8,10},{9,11},{10,... | collective-permute-start | bytes 1572872 | tf_op jit(solution)/shard_map/ppermute | solution.py:30
  258.8 26.0 %collective-permute-start.24 = (bf16[128,2048]{1,0:T(8,128)(2,1)S(1)}, bf16[128,2048]{1,0:T(8,128)(2,1)S(1)}, u32[]{:S(2)}, u32[]{:S(2)}) collective-permute-start(bf16[128,2048]{1,0:T(8,128)(2,1)S(1)} %add_convert_fusion.5), channel_id=1, source_target_pairs={{0,2},{1,3},{2,0},{3,1},{4,6},{5,7},{6,4},{7,5},{8,10},{9,11},{10,... | collective-permute-start | bytes 1572872 | tf_op jit(solution)/shard_map/ppermute | solution.py:30
  259.6 26.0 %collective-permute-start.25 = (bf16[128,2048]{1,0:T(8,128)(2,1)S(1)}, bf16[128,2048]{1,0:T(8,128)(2,1)}, u32[]{:S(2)}, u32[]{:S(2)}) collective-permute-start(bf16[128,2048]{1,0:T(8,128)(2,1)S(1)} %add_convert_fusion.5), channel_id=1, source_target_pairs={{0,3},{1,2},{2,1},{3,0},{4,7},{5,6},{6,5},{7,4},{8,11},{9,10},{10,... | collective-permute-start | bytes 1572872 | tf_op jit(solution)/shard_map/ppermute | solution.py:30
  261.1 36.7 %collective-permute-start.26 = (bf16[128,2048]{1,0:T(8,128)(2,1)}, bf16[128,2048]{1,0:T(8,128)(2,1)}, u32[]{:S(2)}, u32[]{:S(2)}) collective-permute-start(bf16[128,2048]{1,0:T(8,128)(2,1)} %bitcast.16), channel_id=1, source_target_pairs={{0,1},{1,0},{2,3},{3,2},{4,5},{5,4},{6,7},{7,6},{8,9},{9,8},{10,11... | collective-permute-start | bytes 1572872 | tf_op jit(solution)/shard_map/ppermute | solution.py:30
  262.3 43.1 %collective-permute-start.27 = (bf16[128,2048]{1,0:T(8,128)(2,1)}, bf16[128,2048]{1,0:T(8,128)(2,1)}, u32[]{:S(2)}, u32[]{:S(2)}) collective-permute-start(bf16[128,2048]{1,0:T(8,128)(2,1)} %bitcast.16), channel_id=1, source_target_pairs={{0,2},{1,3},{2,0},{3,1},{4,6},{5,7},{6,4},{7,5},{8,10},{9,11},{10,... | collective-permute-start | bytes 1572872 | tf_op jit(solution)/shard_map/ppermute | solution.py:30
  272.4 33.0 %collective-permute-start.28 = (bf16[128,2048]{1,0:T(8,128)(2,1)}, bf16[128,2048]{1,0:T(8,128)(2,1)}, u32[]{:S(2)}, u32[]{:S(2)}) collective-permute-start(bf16[128,2048]{1,0:T(8,128)(2,1)} %bitcast.16), channel_id=1, source_target_pairs={{0,3},{1,2},{2,1},{3,0},{4,7},{5,6},{6,5},{7,4},{8,11},{9,10},{10,... | collective-permute-start | bytes 1572872 | tf_op jit(solution)/shard_map/ppermute | solution.py:30
  330.7 25.1 %collective-permute-start.30 = (bf16[128,2048]{1,0:T(8,128)(2,1)S(1)}, bf16[128,2048]{1,0:T(8,128)(2,1)}, u32[]{:S(2)}, u32[]{:S(2)}) collective-permute-start(bf16[128,2048]{1,0:T(8,128)(2,1)S(1)} %get-tuple-element.116), channel_id=1, source_target_pairs={{0,2},{1,3},{2,0},{3,1},{4,6},{5,7},{6,4},{7,5},{8,10},{9,11},{10,... | collective-permute-start | bytes 1572872 | tf_op jit(solution)/shard_map/ppermute | solution.py:30
  394.3 229.8 %reduce-scatter.11.cloned.1.call-start = ((), (), s32[]{:S(2)}) async-start(), calls=%async_computation.10 | async-start | bytes 3604480 | tf_op jit(solution)/shard_map/reduce_scatter | solution.py:59
  403.7 229.0 %reduce-scatter.5.cloned.1.call-start = ((), (), s32[]{:S(2)}) async-start(), calls=%async_computation.7 | async-start | bytes 3932160 | tf_op jit(solution)/shard_map/reduce_scatter | solution.py:59
  442.8 33.8 %collective-permute-start.44 = (bf16[128,768]{1,0:T(8,128)(2,1)S(1)}, bf16[128,768]{1,0:T(8,128)(2,1)S(1)}, u32[]{:S(2)}, u32[]{:S(2)}) collective-permute-start(bf16[128,768]{1,0:T(8,128)(2,1)S(1)} %get-tuple-element.124), channel_id=1, source_target_pairs={{0,12},{4,8},{8,4},{12,0},{16,28},{20,24},{24,20},{28,16},{1,13},{... | collective-permute-start | bytes 589832 | tf_op jit(solution)/shard_map/ppermute | solution.py:30
  442.8 33.8 %collective-permute-start.45 = (bf16[128,768]{1,0:T(8,128)(2,1)S(1)}, bf16[128,768]{1,0:T(8,128)(2,1)S(1)}, u32[]{:S(2)}, u32[]{:S(2)}) collective-permute-start(bf16[128,768]{1,0:T(8,128)(2,1)S(1)} %get-tuple-element.123), channel_id=1, source_target_pairs={{0,16},{4,20},{8,24},{12,28},{16,0},{20,4},{24,8},{28,12},{1,17},{... | collective-permute-start | bytes 589832 | tf_op jit(solution)/shard_map/ppermute | solution.py:30
  444.6 38.8 %collective-permute-start.46 = (bf16[128,768]{1,0:T(8,128)(2,1)S(1)}, bf16[128,768]{1,0:T(8,128)(2,1)S(1)}, u32[]{:S(2)}, u32[]{:S(2)}) collective-permute-start(bf16[128,768]{1,0:T(8,128)(2,1)S(1)} %get-tuple-element.122), channel_id=1, source_target_pairs={{0,20},{4,16},{8,28},{12,24},{16,4},{20,0},{24,12},{28,8},{1,21},{... | collective-permute-start | bytes 589832 | tf_op jit(solution)/shard_map/ppermute | solution.py:30
  445.2 42.8 %collective-permute-start.47 = (bf16[128,768]{1,0:T(8,128)(2,1)S(1)}, bf16[128,768]{1,0:T(8,128)(2,1)S(1)}, u32[]{:S(2)}, u32[]{:S(2)}) collective-permute-start(bf16[128,768]{1,0:T(8,128)(2,1)S(1)} %get-tuple-element.121), channel_id=1, source_target_pairs={{0,24},{4,28},{8,16},{12,20},{16,8},{20,12},{24,0},{28,4},{1,25},{... | collective-permute-start | bytes 589832 | tf_op jit(solution)/shard_map/ppermute | solution.py:30
  463.0 32.8 %collective-permute-start.48 = (bf16[128,768]{1,0:T(8,128)(2,1)S(1)}, bf16[128,768]{1,0:T(8,128)(2,1)S(1)}, u32[]{:S(2)}, u32[]{:S(2)}) collective-permute-start(bf16[128,768]{1,0:T(8,128)(2,1)S(1)} %get-tuple-element.120), channel_id=1, source_target_pairs={{0,28},{4,24},{8,20},{12,16},{16,12},{20,8},{24,4},{28,0},{1,29},{... | collective-permute-start | bytes 589832 | tf_op jit(solution)/shard_map/ppermute | solution.py:30
  512.8 185.1 %reduce-scatter.9.cloned.1.call-start = ((), (), s32[]{:S(2)}) async-start(), calls=%async_computation.9 | async-start | bytes 7208960 | tf_op jit(solution)/shard_map/reduce_scatter | solution.py:59
  536.9 24.9 %collective-permute-start.53 = (bf16[128,2048]{1,0:T(8,128)(2,1)S(1)}, bf16[128,2048]{1,0:T(8,128)(2,1)S(1)}, u32[]{:S(2)}, u32[]{:S(2)}) collective-permute-start(bf16[128,2048]{1,0:T(8,128)(2,1)S(1)} %get-tuple-element.110), channel_id=1, source_target_pairs={{0,2},{1,3},{2,0},{3,1},{4,6},{5,7},{6,4},{7,5},{8,10},{9,11},{10,... | collective-permute-start | bytes 1572872 | tf_op jit(solution)/shard_map/ppermute | solution.py:30
  564.1 25.4 %collective-permute-start.59 = (f32[8,256]{1,0:T(8,128)S(1)}, f32[8,256]{1,0:T(8,128)S(1)}, u32[]{:S(2)}, u32[]{:S(2)}) collective-permute-start(f32[8,256]{1,0:T(8,128)S(1)} %get-tuple-element.153), channel_id=1, source_target_pairs={{0,4},{4,0},{8,12},{12,8},{16,20},{20,16},{24,28},{28,24},{1,5},{5... | collective-permute-start | bytes 24584 | tf_op jit(solution)/shard_map/ppermute | solution.py:30
  564.1 26.6 %collective-permute-start.60 = (f32[8,256]{1,0:T(8,128)S(1)}, f32[8,256]{1,0:T(8,128)S(1)}, u32[]{:S(2)}, u32[]{:S(2)}) collective-permute-start(f32[8,256]{1,0:T(8,128)S(1)} %get-tuple-element.159), channel_id=1, source_target_pairs={{0,8},{4,12},{8,0},{12,4},{16,24},{20,28},{24,16},{28,20},{1,9},{5... | collective-permute-start | bytes 24584 | tf_op jit(solution)/shard_map/ppermute | solution.py:30
  591.5 25.1 %collective-permute-start.51 = (bf16[128,2048]{1,0:T(8,128)(2,1)}, bf16[128,2048]{1,0:T(8,128)(2,1)S(1)}, u32[]{:S(2)}, u32[]{:S(2)}) collective-permute-start(bf16[128,2048]{1,0:T(8,128)(2,1)} %get-tuple-element.112), channel_id=1, source_target_pairs={{0,3},{1,2},{2,1},{3,0},{4,7},{5,6},{6,5},{7,4},{8,11},{9,10},{10,... | collective-permute-start | bytes 1572872 | tf_op jit(solution)/shard_map/ppermute | solution.py:30
  (122 other events, 1564.4 us)
Sparse Core Ops, SparseCore 0:
  11.1 87.5 all-gather.3
  100.9 151.1 all-gather.5
  254.3 58.9 all-gather.7
  394.4 30.8 reduce-scatter.6
  428.0 81.8 reduce-scatter.10
  512.9 80.4 reduce-scatter.4
  595.7 102.2 reduce-scatter.8
